TPU v7x, 32 devices: a whole 2x2x4 slice. The times are simulated.
32 devices in a mesh: seq: 8 (over z, x), head: 4 (over y, core).
Axes of the slice: x: 2, y: 2, z: 4, core: 2. Of those that a mesh axis runs over, the one named last changes fastest.
Arguments:
- block_input: bfloat16 [2048, 2048], P('seq'), may hold values from -6 to 6
- first_gain: float32 [2048], replicated, may hold values from 0.5 to 1.5
- query_weight: bfloat16 [2048, 1024], P(None, 'head'), may hold values from -0.125 to 0.125
- key_weight: bfloat16 [2048, 1024], P(None, 'head'), may hold values from -0.125 to 0.125
- value_weight: bfloat16 [2048, 2048], P(None, 'head'), may hold values from -0.125 to 0.125
- query_conv: float32 [4, 1024], P(None, 'head'), may hold values from -3 to 3
- key_conv: float32 [4, 1024], P(None, 'head'), may hold values from -3 to 3
- value_conv: float32 [4, 2048], P(None, 'head'), may hold values from -3 to 3
- lowrank_down: bfloat16 [2048, 16], replicated, may hold values from -0.125 to 0.125
- lowrank_up: bfloat16 [16, 1024], P(None, 'head'), may hold values from -1.5 to 1.5
- decay_bias: float32 [1024], P('head'), may hold values from 1 to 8
- outgate_weight: bfloat16 [2048, 2048], P(None, 'head'), may hold values from -0.125 to 0.125
- outnorm_gain: float32 [512], replicated, may hold values from 0.5 to 1.5
- output_weight: bfloat16 [2048, 2048], P(None, 'head'), may hold values from -0.125 to 0.125
- second_gain: float32 [2048], replicated, may hold values from 0.5 to 1.5
- gate_weight: bfloat16 [2048, 5632], P(None, 'head'), may hold values from -0.125 to 0.125
- up_weight: bfloat16 [2048, 5632], P(None, 'head'), may hold values from -0.125 to 0.125
- down_weight: bfloat16 [2048, 5632], P(None, 'head'), may hold values from -0.078125 to 0.078125
- starts: int32 [2048], P('seq'), may hold values 0 or 1
- valid_mask: int32 [2048], P('seq'), may hold values from 0 to 1
- cotangent: bfloat16 [2048, 2048], P('seq'), may hold values from -6 to 6
- teacher: bfloat16 [2048, 2048], P('seq'), may hold values from -6 to 6
Outputs:
- block_output: float32 [2048, 2048], P('seq')
- distill_loss: float32 [], replicated
- grad_input: float32 [2048, 2048], P('seq')
- grad_first_gain: float32 [2048], replicated
- grad_query_weight: float32 [2048, 1024], P('seq', 'head')
- grad_key_weight: float32 [2048, 1024], P('seq', 'head')
- grad_value_weight: float32 [2048, 2048], P('seq', 'head')
- grad_query_conv: float32 [4, 1024], P(None, 'head')
- grad_key_conv: float32 [4, 1024], P(None, 'head')
- grad_value_conv: float32 [4, 2048], P(None, 'head')
- grad_lowrank_down: float32 [2048, 16], P('seq')
- grad_lowrank_up: float32 [16, 1024], P(None, 'head')
- grad_decay_bias: float32 [1024], P('head')
- grad_outgate_weight: float32 [2048, 2048], P('seq', 'head')
- grad_outnorm_gain: float32 [512], replicated
- grad_output_weight: float32 [2048, 2048], P('seq', 'head')
- grad_second_gain: float32 [2048], replicated
- grad_gate_weight: float32 [2048, 5632], P('seq', 'head')
- grad_up_weight: float32 [2048, 5632], P('seq', 'head')
- grad_down_weight: float32 [2048, 5632], P('seq', 'head')
All inputs are finite; a program needn't handle non-finite values. No bound on the sum of `starts` on one device may be relied on, other than what follows from the above.
Results may differ from a plain program's by a relative error of at most 0.029.
The roundings to bfloat16 on the way count: a program that leaves them out, or rounds other values in their place, can miss the bound.
Values may be sent and summed in bfloat16 or wider, within the bound.
No kernel may reach another device: no remote copies, remote signals or barrier semaphores. Data moves between devices by JAX's collectives and lax.ppermute only.
A program may use at most 320 MiB of HBM per device.

v0:
```python
import jax
import jax.numpy as jnp
from jax import lax
from jax.sharding import PartitionSpec as P

D = 2048
DK = 256
DV = 512
RANK = 16
TAPS = 4
BLOCK = 64


EPSILON = 1e-05
FINEST_PRECISION = lax.Precision.HIGHEST


def from_behind(block, axis, distance):
    devices = range(lax.axis_size(axis))
    route = [(i - distance, i) for i in devices if i - distance in devices]
    return lax.ppermute(block, axis, route)


def prefix(part, axis, combine, identity):
    place = lax.axis_index(axis)
    gathered = jax.tree.map(lambda a: lax.all_gather(a, axis), part)
    state = jax.tree.map(lambda a, e: jnp.zeros_like(a) + jnp.asarray(e, a.dtype), part, identity)

    def one(hop, state):
        return combine(
            state, jax.tree.map(lambda a: lax.dynamic_index_in_dim(a, hop, 0, False), gathered)
        )

    return lax.fori_loop(0, place, one, state)


def prefix_2(x, axis, join, neutral):
    count = lax.axis_size(axis)
    place = lax.axis_index(axis)
    ahead = count - 1 - place
    gathered = jax.tree.map(
        lambda a, kind: lax.all_gather(a.astype(kind), axis),
        x,
        jax.tree.map(lambda a: jnp.bfloat16 if a.dtype == jnp.float32 else a.dtype, x),
    )
    state = jax.tree.map(lambda a, e: jnp.zeros_like(a) + jnp.asarray(e, a.dtype), x, neutral)

    def one(hop, state):
        source = count - 1 - hop
        return join(
            state,
            jax.tree.map(
                lambda a, own: lax.dynamic_index_in_dim(a, source, 0, False).astype(own.dtype),
                gathered,
                x,
            ),
        )

    return lax.fori_loop(0, ahead, one, state)


def root_scale(incoming_values):
    return lax.rsqrt(jnp.mean(incoming_values * incoming_values, axis=-1, keepdims=True) + EPSILON)


def norm_backward(incoming_values, scale, gain, upstream):
    scaled_up = upstream * gain
    return scale * scaled_up - incoming_values * scale * scale * scale * jnp.mean(
        scaled_up * incoming_values, axis=-1, keepdims=True
    )


def contract_rows(left, right):
    return lax.dot_general(
        left, right, (((0,), (0,)), ((), ())), preferred_element_type=jnp.float32
    )


def contract_cols(left, right):
    return lax.dot_general(
        left, right, (((1,), (1,)), ((), ())), preferred_element_type=jnp.float32
    )


def convolve(extended, weights, starts_cum):
    length = extended.shape[0] - (TAPS - 1)
    padded_cum = jnp.concatenate([jnp.zeros((TAPS - 1,), jnp.int32), starts_cum])
    running = extended[TAPS - 1 :] * weights[TAPS - 1]
    for offset in range(1, TAPS):
        shifted = extended[TAPS - 1 - offset : TAPS - 1 - offset + length]
        earlier = padded_cum[TAPS - 1 - offset : TAPS - 1 - offset + length]
        same_doc = (starts_cum - earlier == 0).astype(jnp.float32)
        running = running + shifted * weights[TAPS - 1 - offset] * same_doc[:, None]
    return jax.nn.silu(running)


def block_step(state_running, queries, keys_in, incoming_values, decays, resets):
    cumulative = jnp.cumsum(decays, axis=1)
    segment = jnp.cumsum(resets)
    living_mask = (segment == 0.0).astype(jnp.float32)
    row_ids = lax.broadcasted_iota(jnp.int32, (BLOCK, BLOCK), 0)
    col_ids = lax.broadcasted_iota(jnp.int32, (BLOCK, BLOCK), 1)
    allowed = ((col_ids <= row_ids) & (segment[:, None] == segment[None, :])).astype(jnp.float32)
    rising_factor = queries * jnp.exp(cumulative)
    falling = keys_in * jnp.exp(-cumulative)
    scores = (
        jnp.einsum("hqk,hsk->hqs", rising_factor, falling, precision=FINEST_PRECISION) * allowed
    )
    output_rows = jnp.einsum("hqs,hsv->hqv", scores, incoming_values, precision=FINEST_PRECISION)
    output_rows = output_rows + jnp.einsum(
        "luy,lyb->lub",
        rising_factor * living_mask[None, :, None],
        state_running,
        precision=FINEST_PRECISION,
    )
    final_log = cumulative[:, -1, :]
    tail_mask = (segment == segment[-1]).astype(jnp.float32)
    closing_state = keys_in * jnp.exp(final_log[:, None, :] - cumulative) * tail_mask[None, :, None]
    carried_over = state_running * (jnp.exp(final_log) * living_mask[-1])[:, :, None]
    updated_state = carried_over + jnp.einsum(
        "otn,otl->onl", closing_state, incoming_values, precision=FINEST_PRECISION
    )
    return (updated_state, output_rows, cumulative, living_mask)


def local_mixer(queries, keys_in, incoming_values, decays, resets):
    length = queries.shape[0]
    heads_here = queries.shape[1] // DK
    blocks = length // BLOCK

    def to_blocks(array, width):
        return array.reshape(blocks, BLOCK, heads_here, width).transpose(0, 2, 1, 3)

    def advance(carry, pieces):
        state_running, running_log, running_alive = carry
        updated_state, output_rows, cumulative, living_mask = block_step(state_running, *pieces)
        factor = (
            jnp.exp(running_log[:, None, :] + cumulative)
            * (running_alive * living_mask)[None, :, None]
        )
        return (
            (updated_state, running_log + cumulative[:, -1, :], running_alive * living_mask[-1]),
            (output_rows, factor),
        )

    initial = (
        jnp.zeros((heads_here, DK, DV), jnp.float32),
        jnp.zeros((heads_here, DK), jnp.float32),
        jnp.ones((), jnp.float32),
    )
    (end_state, spent_log, spent_alive), (outputs, factors) = lax.scan(
        advance,
        initial,
        (
            to_blocks(queries, DK),
            to_blocks(keys_in, DK),
            to_blocks(incoming_values, DV),
            to_blocks(decays, DK),
            resets.reshape(blocks, BLOCK),
        ),
    )
    mixed_flat = outputs.transpose(0, 2, 1, 3).reshape(length, heads_here * DV)
    return (mixed_flat, end_state, factors.transpose(0, 2, 1, 3).reshape(length, heads_here, DK))


def carry_forward(earlier, later):
    return (earlier[0] * later[0], later[0][..., None] * earlier[1] + later[1])


def carry_backward(earlier, later):
    return (earlier[0] * later[0], later[1] + later[0][..., None] * earlier[1])


def on_device(
    block_input,
    first_gain,
    query_weight,
    key_weight,
    value_weight,
    query_conv,
    key_conv,
    value_conv,
    lowrank_down,
    lowrank_up,
    decay_bias,
    outgate_weight,
    outnorm_gain,
    output_weight,
    second_gain,
    gate_weight,
    up_weight,
    down_weight,
    starts,
    valid_mask,
    cotangent,
    teacher,
):
    length = block_input.shape[0]
    key_local = query_weight.shape[1]
    value_local = value_weight.shape[1]
    heads_here = key_local // DK
    loss_weight = float(length * lax.axis_size("seq") * D // 8)
    input_float = block_input.astype(jnp.float32)
    first_scale = root_scale(input_float)
    normed = (input_float * first_scale * first_gain).astype(jnp.bfloat16)
    pre_conv = jnp.concatenate(
        [
            jnp.dot(normed, query_weight, preferred_element_type=jnp.float32),
            jnp.dot(normed, key_weight, preferred_element_type=jnp.float32),
            jnp.dot(normed, value_weight, preferred_element_type=jnp.float32),
        ],
        axis=1,
    ).astype(jnp.bfloat16)
    starts_cum = jnp.cumsum(starts)
    tail_keep = (starts_cum[-1] - starts_cum[length - (TAPS - 1) :] == 0).astype(jnp.bfloat16)
    edge_rows = from_behind(pre_conv[length - (TAPS - 1) :] * tail_keep[:, None], "seq", 1)
    extended = jnp.concatenate([edge_rows, pre_conv], axis=0).astype(jnp.float32)
    conv_weights = jnp.concatenate([query_conv, key_conv, value_conv], axis=1)
    convolved, conv_pull = jax.vjp(
        lambda ext_rows, taps_in: convolve(ext_rows, taps_in, starts_cum), extended, conv_weights
    )
    queries = convolved[:, :key_local] * DK ** (-0.5)
    keys_in = convolved[:, key_local : 2 * key_local]
    incoming_values = convolved[:, 2 * key_local :]
    low_rank = jnp.dot(normed, lowrank_down, preferred_element_type=jnp.float32).astype(
        jnp.bfloat16
    )
    gate_logit = jnp.dot(low_rank, lowrank_up, preferred_element_type=jnp.float32) + decay_bias
    decays = jax.nn.log_sigmoid(gate_logit) / 16.0
    outgate = jnp.dot(normed, outgate_weight, preferred_element_type=jnp.float32)
    resets = starts.astype(jnp.float32)
    (mixed_local, end_state, factors), mixer_pull = jax.vjp(
        lambda qin, kin, vin, din: local_mixer(qin, kin, vin, din, resets),
        queries,
        keys_in,
        incoming_values,
        decays,
    )
    last_factor = factors[-1]
    zero_state = jnp.zeros_like(end_state)
    spent_factor, incoming_state = prefix(
        (last_factor, end_state), "seq", carry_forward, (jnp.ones_like(last_factor), zero_state)
    )
    queries_heads = queries.reshape(length, heads_here, DK)
    query_scaled = queries_heads * factors
    mixer_out = mixed_local.reshape(length, heads_here, DV) + jnp.einsum(
        "clg,lgf->clf", query_scaled, incoming_state, precision=FINEST_PRECISION
    )
    out_scale = root_scale(mixer_out)
    normed_out = mixer_out * out_scale * outnorm_gain
    outgate_heads = outgate.reshape(length, heads_here, DV)
    swish = jax.nn.silu(outgate_heads)
    gated_out = (normed_out * swish).reshape(length, value_local).astype(jnp.bfloat16)
    branch = lax.psum(contract_cols(gated_out, output_weight).astype(jnp.bfloat16), "head").astype(
        jnp.float32
    )
    hidden = input_float + branch
    second_scale = root_scale(hidden)
    normed_ffn = (hidden * second_scale * second_gain).astype(jnp.bfloat16)
    gate_val = jnp.dot(normed_ffn, gate_weight, preferred_element_type=jnp.float32)
    up_val = jnp.dot(normed_ffn, up_weight, preferred_element_type=jnp.float32)
    sigmoid_gate = jax.nn.sigmoid(gate_val)
    activated = (gate_val * sigmoid_gate * up_val).astype(jnp.bfloat16)
    ffn_out = lax.psum(contract_cols(activated, down_weight).astype(jnp.bfloat16), "head").astype(
        jnp.float32
    )
    block_output = hidden + ffn_out
    valid_float = valid_mask.astype(jnp.float32)
    mismatch = block_output - teacher.astype(jnp.float32)
    squared_sum, valid_count = lax.psum(
        (jnp.sum(valid_float[:, None] * mismatch * mismatch), jnp.sum(valid_float)), "seq"
    )
    distill = squared_sum / (valid_count * D)
    d_out = cotangent.astype(jnp.float32) + valid_float[:, None] * 2.0 * loss_weight * mismatch / (
        valid_count * D
    )
    d_ffn = d_out.astype(jnp.bfloat16)
    d_act = jnp.dot(d_ffn, down_weight, preferred_element_type=jnp.float32)
    d_gate_val = (d_act * up_val * sigmoid_gate * (1.0 + gate_val * (1.0 - sigmoid_gate))).astype(
        jnp.bfloat16
    )
    d_up_val = (d_act * gate_val * sigmoid_gate).astype(jnp.bfloat16)
    d_nffn_part = contract_cols(d_gate_val, gate_weight) + contract_cols(d_up_val, up_weight)
    d_nffn = lax.psum(d_nffn_part.astype(jnp.bfloat16), "head").astype(jnp.float32)
    grad_second_gain = jnp.sum(d_nffn * hidden * second_scale, axis=0)
    d_hidden = d_out + norm_backward(hidden, second_scale, second_gain, d_nffn)
    d_branch = d_hidden.astype(jnp.bfloat16)
    d_gated = jnp.dot(d_branch, output_weight, preferred_element_type=jnp.float32).reshape(
        length, heads_here, DV
    )
    d_normed_out = d_gated * swish
    sigmoid_out = jax.nn.sigmoid(outgate_heads)
    d_outgate = (
        (d_gated * normed_out * sigmoid_out * (1.0 + outgate_heads * (1.0 - sigmoid_out)))
        .reshape(length, value_local)
        .astype(jnp.bfloat16)
    )
    outnorm_part = jnp.sum(d_normed_out * mixer_out * out_scale, axis=(0, 1))
    mixer_gradient = norm_backward(mixer_out, out_scale, outnorm_gain, d_normed_out)
    direct_term = jnp.einsum(
        "bwq,bwo->wqo", query_scaled, mixer_gradient, precision=FINEST_PRECISION
    )
    spent_back, later = prefix_2(
        (last_factor, direct_term), "seq", carry_backward, (jnp.ones_like(last_factor), zero_state)
    )
    scaled_gradient = jnp.einsum(
        "ylg,lwg->ylw", mixer_gradient, incoming_state, precision=FINEST_PRECISION
    )
    d_factors = (
        (scaled_gradient * queries_heads).at[-1].add(jnp.sum(later * incoming_state, axis=-1))
    )
    d_queries, d_keys, d_values, d_decays = mixer_pull(
        (mixer_gradient.reshape(length, value_local), later, d_factors)
    )
    d_queries = d_queries + (scaled_gradient * factors).reshape(length, key_local)
    d_logit_float = (d_decays * jax.nn.sigmoid(-gate_logit) / 16.0).astype(jnp.bfloat16)
    grad_decay_bias = jnp.sum(d_logit_float.astype(jnp.float32), axis=0)
    grad_lowrank_up = contract_rows(low_rank, d_logit_float)
    d_lowrank_part = contract_cols(d_logit_float, lowrank_up)
    d_extended, grad_conv = conv_pull(
        jnp.concatenate([d_queries * DK ** (-0.5), d_keys, d_values], axis=1)
    )
    back_rows = from_behind(d_extended[: TAPS - 1], "seq", -1)
    tail_float = tail_keep.astype(jnp.float32)
    d_pre = d_extended[TAPS - 1 :] + jnp.concatenate(
        [
            jnp.zeros((length - (TAPS - 1), back_rows.shape[1]), jnp.float32),
            back_rows * tail_float[:, None],
        ],
        axis=0,
    )
    d_pre = d_pre.astype(jnp.bfloat16)
    d_first_part = contract_cols(d_pre[:, :key_local], query_weight) + contract_cols(
        d_pre[:, key_local : 2 * key_local], key_weight
    )
    d_first_part = (
        d_first_part
        + contract_cols(d_pre[:, 2 * key_local :], value_weight)
        + contract_cols(d_outgate, outgate_weight)
    )
    d_first, d_lowrank, grad_outnorm_gain = (
        lax.psum(d_first_part.astype(jnp.bfloat16), "head").astype(jnp.float32),
        lax.psum(d_lowrank_part.astype(jnp.bfloat16), "head").astype(jnp.float32),
        lax.psum(outnorm_part.astype(jnp.bfloat16), "head").astype(jnp.float32),
    )
    d_lowrank = d_lowrank.astype(jnp.bfloat16)
    d_first = d_first + contract_cols(d_lowrank, lowrank_down)
    grad_first_gain = jnp.sum(d_first * input_float * first_scale, axis=0)
    grad_input = d_hidden + norm_backward(input_float, first_scale, first_gain, d_first)
    reduced = lax.psum_scatter(
        jnp.concatenate(
            [
                contract_rows(normed, d_pre),
                contract_rows(normed, d_lowrank),
                contract_rows(normed, d_outgate),
                contract_rows(d_branch, gated_out),
                contract_rows(normed_ffn, d_gate_val),
                contract_rows(normed_ffn, d_up_val),
                contract_rows(d_ffn, activated),
            ],
            axis=1,
        ).astype(jnp.bfloat16),
        "seq",
        scatter_dimension=0,
        tiled=True,
    ).astype(jnp.float32)
    widths = [
        key_local,
        key_local,
        value_local,
        RANK,
        value_local,
        value_local,
        gate_weight.shape[1],
        gate_weight.shape[1],
        gate_weight.shape[1],
    ]
    pieces = []
    begin = 0
    for span in widths:
        pieces.append(reduced[:, begin : begin + span])
        begin = begin + span
    (
        conv_sum,
        grad_lowrank_up,
        grad_decay_bias,
        grad_first_gain,
        grad_outnorm_gain,
        grad_second_gain,
    ) = (
        lax.psum(grad_conv.astype(jnp.bfloat16), "seq").astype(jnp.float32),
        lax.psum(grad_lowrank_up.astype(jnp.bfloat16), "seq").astype(jnp.float32),
        lax.psum(grad_decay_bias.astype(jnp.bfloat16), "seq").astype(jnp.float32),
        lax.psum(grad_first_gain.astype(jnp.bfloat16), "seq").astype(jnp.float32),
        lax.psum(grad_outnorm_gain.astype(jnp.bfloat16), "seq").astype(jnp.float32),
        lax.psum(grad_second_gain.astype(jnp.bfloat16), "seq").astype(jnp.float32),
    )
    return (
        block_output,
        distill,
        grad_input,
        grad_first_gain,
        pieces[0],
        pieces[1],
        pieces[2],
        conv_sum[:, :key_local],
        conv_sum[:, key_local : 2 * key_local],
        conv_sum[:, 2 * key_local :],
        pieces[3],
        grad_lowrank_up,
        grad_decay_bias,
        pieces[4],
        grad_outnorm_gain,
        pieces[5],
        grad_second_gain,
        pieces[6],
        pieces[7],
        pieces[8],
    )


def solution(mesh):
    in_specs = (
        P("seq", None),
        P(),
        P(None, "head"),
        P(None, "head"),
        P(None, "head"),
        P(None, "head"),
        P(None, "head"),
        P(None, "head"),
        P(),
        P(None, "head"),
        P("head"),
        P(None, "head"),
        P(),
        P(None, "head"),
        P(),
        P(None, "head"),
        P(None, "head"),
        P(None, "head"),
        P("seq"),
        P("seq"),
        P("seq", None),
        P("seq", None),
    )
    out_specs = (
        P("seq", None),
        P(),
        P("seq", None),
        P(),
        P("seq", "head"),
        P("seq", "head"),
        P("seq", "head"),
        P(None, "head"),
        P(None, "head"),
        P(None, "head"),
        P("seq", None),
        P(None, "head"),
        P("head"),
        P("seq", "head"),
        P(),
        P("seq", "head"),
        P(),
        P("seq", "head"),
        P("seq", "head"),
        P("seq", "head"),
    )
    return jax.shard_map(
        on_device, mesh=mesh, in_specs=in_specs, out_specs=out_specs, check_vma=False
    )
```

profile of v0, /device:TPU:0, one launch (start us, length us, event | category | flops | bytes accessed | tf_op | source)
XLA Modules:
  0.0 1025.0 jit_solution(17676214076428010569)
XLA Ops:
  9.0 2.8 convolution_convert_fusion.9
  16.2 4.8 collective-permute-start
  35.0 74.0 %while.109 = (s32[]{:T(128)}, f32[1,256,512]{2,1,0:T(8,128)S(1)}, f32[1,256]{1,0:T(1,128)S(1)}, f32[]{:T(128)}, f32[4,1,64,512]{3,2,1,0:T(8,128)}, /*index=5*/f3...) while((s32[]{:T(128)}, f32[1,256,512]{2,1,0:T(8,128)S(1)}, ...), condition=%wide.region_6.7_spmd.clone.clone, body=%wide.region_3.6_spmd.clone.clone.sunk | while | flops 241112704 | bytes 4998958 | solution.py:151
  109.9 3.5 fusion.173
  113.4 19.4 %all_gather.19 = f32[8,1,256]{2,1,0:T(1,128)S(1)} all-gather(f32[1,1,256]{2,1,0:T(1,128)S(1)} %slice_bitcast_fusion), channel_id=1, replica_groups=mesh['seq'=8,'head'=4] {'seq'}, dimensions={0}, use_global_device_ids=true | all-gather | bytes 9216 | tf_op jit(solution)/shard_map/all_gather | solution.py:26
  134.5 49.2 %all-gather.5.cloned.1.call-done = f32[8,256,512]{2,1,0:T(8,128)} async-done(((f32[1,256,512]{2,1,0:T(8,128)}), f32[8,256,512]{2,1,0:T(8,128)}) %all-gather.5.cloned.1.call-update) | async-done | bytes 4194320 | tf_op jit(solution)/shard_map/all_gather | solution.py:26
  189.4 42.9 %all-reduce.20.cloned.1.call-done = bf16[256,2048]{1,0:T(8,128)(2,1)} async-done(((bf16[256,2048]{1,0:T(8,128)(2,1)}), bf16[256,2048]{1,0:T(8,128)(2,1)}) %all-reduce.20.cloned.1.call-update) | async-done | bytes 1048592 | tf_op jit(solution)/shard_map/psum | solution.py:254
  236.3 4.9 fusion.188
  241.2 3.0 multiply_convert_fusion.3
  248.6 36.0 %all-reduce.22.cloned.1.call-done = bf16[256,2048]{1,0:T(8,128)(2,1)} async-done(((bf16[256,2048]{1,0:T(8,128)(2,1)}), bf16[256,2048]{1,0:T(8,128)(2,1)}) %all-reduce.22.cloned.1.call-update) | async-done | bytes 1048592 | tf_op jit(solution)/shard_map/psum | solution.py:264
  284.5 4.9 fusion.127
  289.5 22.0 %all-reduce.12 = (f32[]{:T(128)}, f32[]{:T(128)}) all-reduce(f32[]{:T(128)} %get-tuple-element.1646, f32[]{:T(128)} %get-tuple-element.1584), channel_id=1, replica_groups=mesh['seq'=8,'head'=4] {'seq'}, use_global_device_ids=true, to_apply=%region_16.17 | all-reduce | flops 2 | bytes 16 | tf_op jit(solution)/shard_map/psum | solution.py:270
  312.1 2.9 divide_add_fusion
  315.1 7.0 multiply_convert_fusion.1
  327.1 32.7 %all-reduce.24.cloned.1.call-done = bf16[256,2048]{1,0:T(8,128)(2,1)} async-done(((bf16[256,2048]{1,0:T(8,128)(2,1)}), bf16[256,2048]{1,0:T(8,128)(2,1)}) %all-reduce.24.cloned.1.call-update) | async-done | bytes 1048592 | tf_op jit(solution)/shard_map/psum | solution.py:284
  370.0 20.7 %all_gather.24 = bf16[8,1,256]{2,1,0:T(2,128)(2,1)S(1)} all-gather(bf16[1,1,256]{2,1,0:T(2,128)(2,1)S(1)} %convert_bitcast_fusion), channel_id=1, replica_groups=mesh['seq'=8,'head'=4] {'seq'}, dimensions={0}, use_global_device_ids=true | all-gather | bytes 4608 | tf_op jit(solution)/shard_map/all_gather | solution.py:42
  393.0 26.1 %all-gather.7.cloned.1.call-done = bf16[2048,512]{1,0:T(8,128)(2,1)} async-done(((bf16[256,512]{1,0:T(8,128)(2,1)}), bf16[2048,512]{1,0:T(8,128)(2,1)}) %all-gather.7.cloned.1.call-update) | async-done | bytes 2097168 | tf_op jit(solution)/shard_map/all_gather | solution.py:42
  419.1 8.1 while.107
  430.7 81.4 %while.108 = (s32[]{:T(128)}, f32[1,256,512]{1,2,0:T(8,128)S(1)}, f32[1,256]{1,0:T(1,128)S(1)}, f32[4,1,64,256]{3,2,1,0:T(8,128)}, f32[4,1,64,256]{3,2,1,0:T(8,1...) while((s32[]{:T(128)}, f32[1,256,512]{1,2,0:T(8,128)S(1)}, ...), condition=%wide.region_28.29_spmd.clone, body=%wide.region_23.28_spmd.clone.sunk | while | flops 480170752 | bytes 16529876 | solution.py:151
  519.4 6.3 all-reduce.14
  527.2 3.4 convert_dynamic-update-slice_fusion.1
  536.5 4.3 fusion.105
  545.8 5.4 fusion.106
  551.2 4.2 fusion.107
  556.3 25.3 %all-reduce.26.cloned.1.call-done = bf16[256,2048]{1,0:T(8,128)(2,1)} async-done(((bf16[256,2048]{1,0:T(8,128)(2,1)}), bf16[256,2048]{1,0:T(8,128)(2,1)}) %all-reduce.26.cloned.1.call-update) | async-done | bytes 1048592 | tf_op jit(solution)/shard_map/psum | solution.py:342
  581.6 3.4 fusion.131
  584.9 39.0 %all-reduce.13 = (bf16[4,1024]{1,0:T(4,128)(2,1)S(1)}, bf16[2048]{0:T(1024)(128)(2,1)S(1)}, bf16[16,256]{1,0:T(8,128)(2,1)S(1)}, bf16[256]{0:T(256)(128)(2,1)S(1...) all-reduce(bf16[4,1024]{1,0:T(4,128)(2,1)S(1)} %add_convert_fusion,, ...), channel_id=1, replica_groups=mesh['seq'=8,'head'=4] {'seq'}, use_global_device_ids=true, to_apply=%region_39.40 | all-reduce | flops 13056 | bytes 52224 | tf_op jit(solution)/shard_map/psum | solution.py:391
  628.0 4.3 fusion.121
  632.4 365.4 %reduce-scatter.2.cloned.1.call-done = bf16[256,6288]{0,1:T(8,128)(2,1)} async-done(((bf16[2048,6288]{0,1:T(8,128)(2,1)}), bf16[256,6288]{0,1:T(8,128)(2,1)}) %reduce-scatter.2.cloned.1.call-update) | async-done | bytes 3219472 | tf_op jit(solution)/shard_map/reduce_scatter | solution.py:350
  997.8 3.5 fusion.183
  1001.3 2.9 copy.117
  1004.2 2.9 copy.118
  (525 shorter events, 250.6 us)
Async XLA Ops:
  7.2 180.3 %copy-start = (bf16[2048,512]{1,0:T(8,128)(2,1)S(1)}, bf16[2048,512]{1,0:T(8,128)(2,1)}, u32[]{:S(2)}) copy-start(bf16[2048,512]{1,0:T(8,128)(2,1)} %param.45) | copy-start | bytes 6291460
  7.2 176.6 %all-gather.5.cloned.1.call-start = ((), (), s32[]{:S(2)}) async-start(), calls=%async_computation.6 | async-start | bytes 4718592 | tf_op jit(solution)/shard_map/all_gather | solution.py:26
  8.9 12.3 %copy-start.52 = (f32[256]{0:T(256)}, f32[256]{0:T(256)S(1)}, u32[]{:S(2)}) copy-start(f32[256]{0:T(256)S(1)} %add_rsqrt_fusion.2) | copy-start | bytes 3076
  13.6 9.3 copy-start.46
  13.6 9.3 copy-start.61
  16.2 8.6 collective-permute-start
  109.8 122.5 %all-reduce.20.cloned.1.call-start = ((), (), s32[]{:S(2)}) async-start(), calls=%async_computation.1 | async-start | bytes 2097152 | tf_op jit(solution)/shard_map/psum | solution.py:254
  189.2 45.2 %copy-start.43 = (f32[2048]{0:T(1024)S(1)}, f32[2048]{0:T(1024)}, u32[]{:S(2)}) copy-start(f32[2048]{0:T(1024)} %param.46) | copy-start | bytes 24580
  189.2 95.3 %all-reduce.22.cloned.1.call-start = ((), (), s32[]{:S(2)}) async-start(), calls=%async_computation.2 | async-start | bytes 2097152 | tf_op jit(solution)/shard_map/psum | solution.py:264
  247.9 111.9 %all-reduce.24.cloned.1.call-start = ((), (), s32[]{:S(2)}) async-start(), calls=%async_computation.3 | async-start | bytes 2097152 | tf_op jit(solution)/shard_map/psum | solution.py:284
  312.1 10.0 slice-start.2
  312.1 11.8 %slice-start.6 = ((s8[5767168]{0:T(1024)(128)(4,1)}), s8[4194304]{0:T(1024)(128)(4,1)S(1)}, s32[]{:S(2)}) async-start(s8[5767168]{0:T(1024)(128)(4,1)} %bitcast.687), calls=%async_computation.14 | async-start | bytes 8388608
  315.0 8.9 slice-start.7
  326.8 92.3 %all-gather.7.cloned.1.call-start = ((), (), s32[]{:S(2)}) async-start(), calls=%async_computation.7 | async-start | bytes 2359296 | tf_op jit(solution)/shard_map/all_gather | solution.py:42
  367.9 51.2 %copy-start.7 = (f32[256,1,512]{2,0,1:T(8,128)}, f32[256,1,512]{2,0,1:T(8,128)S(1)}, u32[]{:S(2)}) copy-start(f32[256,1,512]{2,0,1:T(8,128)S(1)} %bitcast_subtract_fusion.2) | copy-start | bytes 1572868
  369.2 212.3 %all-reduce.26.cloned.1.call-start = ((), (), s32[]{:S(2)}) async-start(), calls=%async_computation.4 | async-start | bytes 2097152 | tf_op jit(solution)/shard_map/psum | solution.py:342
  430.7 82.6 %copy-start.4 = (f32[259,1024]{1,0:T(8,128)S(1)}, f32[259,1024]{1,0:T(8,128)}, u32[]{:S(2)}) copy-start(f32[259,1024]{1,0:T(8,128)} %copy-done.3) | copy-start | bytes 3182596
  434.1 11.5 %copy-start.8 = (f32[4,1,64,512]{3,2,1,0:T(8,128)S(1)}, f32[4,1,64,512]{3,2,1,0:T(8,128)}, u32[]{:S(2)}) copy-start(f32[4,1,64,512]{3,2,1,0:T(8,128)} %get-tuple-element.2356) | copy-start | bytes 1572868 | tf_op jit(solution)/shard_map/transpose(jvp())/while
  439.8 11.3 %copy-start.17 = (f32[4,1,64,512]{3,2,1,0:T(8,128)S(1)}, f32[4,1,64,512]{3,2,1,0:T(8,128)}, u32[]{:S(2)}) copy-start(f32[4,1,64,512]{3,2,1,0:T(8,128)} %copy-done.16) | copy-start | bytes 1572868 | tf_op jit(solution)/shard_map/transpose(jvp())/while
  454.4 11.5 %copy-start.8 = (f32[4,1,64,512]{3,2,1,0:T(8,128)S(1)}, f32[4,1,64,512]{3,2,1,0:T(8,128)}, u32[]{:S(2)}) copy-start(f32[4,1,64,512]{3,2,1,0:T(8,128)} %get-tuple-element.2356) | copy-start | bytes 1572868 | tf_op jit(solution)/shard_map/transpose(jvp())/while
  460.1 11.3 %copy-start.17 = (f32[4,1,64,512]{3,2,1,0:T(8,128)S(1)}, f32[4,1,64,512]{3,2,1,0:T(8,128)}, u32[]{:S(2)}) copy-start(f32[4,1,64,512]{3,2,1,0:T(8,128)} %copy-done.16) | copy-start | bytes 1572868 | tf_op jit(solution)/shard_map/transpose(jvp())/while
  473.4 8.9 copy-start.21
  474.7 11.5 %copy-start.8 = (f32[4,1,64,512]{3,2,1,0:T(8,128)S(1)}, f32[4,1,64,512]{3,2,1,0:T(8,128)}, u32[]{:S(2)}) copy-start(f32[4,1,64,512]{3,2,1,0:T(8,128)} %get-tuple-element.2356) | copy-start | bytes 1572868 | tf_op jit(solution)/shard_map/transpose(jvp())/while
  480.5 11.3 %copy-start.17 = (f32[4,1,64,512]{3,2,1,0:T(8,128)S(1)}, f32[4,1,64,512]{3,2,1,0:T(8,128)}, u32[]{:S(2)}) copy-start(f32[4,1,64,512]{3,2,1,0:T(8,128)} %copy-done.16) | copy-start | bytes 1572868 | tf_op jit(solution)/shard_map/transpose(jvp())/while
  495.1 11.5 %copy-start.8 = (f32[4,1,64,512]{3,2,1,0:T(8,128)S(1)}, f32[4,1,64,512]{3,2,1,0:T(8,128)}, u32[]{:S(2)}) copy-start(f32[4,1,64,512]{3,2,1,0:T(8,128)} %get-tuple-element.2356) | copy-start | bytes 1572868 | tf_op jit(solution)/shard_map/transpose(jvp())/while
  500.8 11.3 %copy-start.17 = (f32[4,1,64,512]{3,2,1,0:T(8,128)S(1)}, f32[4,1,64,512]{3,2,1,0:T(8,128)}, u32[]{:S(2)}) copy-start(f32[4,1,64,512]{3,2,1,0:T(8,128)} %copy-done.16) | copy-start | bytes 1572868 | tf_op jit(solution)/shard_map/transpose(jvp())/while
  516.2 9.5 collective-permute-start.1
  517.9 9.3 copy-start.6
  517.9 9.3 copy-start.45
  517.9 9.2 copy-start.53
  545.7 452.1 %reduce-scatter.2.cloned.1.call-start = ((), (), s32[]{:S(2)}) async-start(), calls=%async_computation.5 | async-start | bytes 28975104 | tf_op jit(solution)/shard_map/reduce_scatter | solution.py:350
  555.4 26.2 %copy-start.60 = (bf16[2048,16]{0,1:T(8,128)(2,1)S(1)}, bf16[2048,16]{0,1:T(8,128)(2,1)}, u32[]{:S(2)}) copy-start(bf16[2048,16]{0,1:T(8,128)(2,1)} %param.40) | copy-start | bytes 196612
  (72 other events, 267.9 us)
Sparse Core Ops, SparseCore 0:
  109.9 73.7 all-gather.4
  189.3 42.9 all-reduce.19
  248.0 36.4 all-reduce.21
  326.9 32.7 all-reduce.23
  369.4 49.6 all-gather.6
  545.8 35.7 all-reduce.25
  585.5 412.2 reduce-scatter.1
where the time goes:
time: 1040 us; the launch traced here: 1020 us
  waiting for transfers between devices  578 us (56%)
  matrix products  140 us (13%)
  blocking collectives  107 us (10%)
  other arithmetic  93.2 us (9%)
  local copies, waits for them, and re-layouts  78.6 us (8%)
  between operations  17.9 us (2%)
    reduce_scatter x1, waiting for transfers between devices, on_device(): lax.psum_scatter(jnp.concatenate([contract_rows(normed, d_pre), contract_...  365 us
    all_gather x1, waiting for transfers between devices, prefix(): gathered = jax.tree.map(lambda a: lax.all_gather(a, axis), part)  49.2 us
    psum x1, waiting for transfers between devices, on_device(): lax.psum(contract_cols(gated_out, output_weight).astype(jnp.bfloat16), 'h...  42.9 us
    psum x1, blocking collectives, on_device(): lax.psum(grad_conv.astype(jnp.bfloat16), 'seq').astype(jnp.float32)  39 us
    psum x1, waiting for transfers between devices, on_device(): lax.psum(contract_cols(activated, down_weight).astype(jnp.bfloat16), 'head')  36 us
    psum x1, waiting for transfers between devices, on_device(): lax.psum(d_nffn_part.astype(jnp.bfloat16), 'head').astype(jnp.float32)  32.7 us
    all_gather x1, waiting for transfers between devices, prefix_2(): lax.all_gather(a.astype(kind), axis)  26.1 us
    psum x1, waiting for transfers between devices, on_device(): lax.psum(d_first_part.astype(jnp.bfloat16), 'head').astype(jnp.float32)  25.3 us
  transfers between devices with their start and end apart: 9, of which 7 were waited for; matrix products, arithmetic and copies ran while one was open for 3% of the time, Pallas kernels for 0%

commit v1 on v0

v1 whole, which is shorter than its diff:
```python
import functools

import jax
import jax.numpy as jnp
from jax import lax
from jax.experimental import pallas as pl
from jax.experimental.pallas import tpu as pltpu
from jax.sharding import PartitionSpec as P

D = 2048
DK = 256
DV = 512
RANK = 16
TAPS = 4
BLOCK = 64
EPSILON = 1e-05
HIGHEST = lax.Precision.HIGHEST
F32 = jnp.float32
BF16 = jnp.bfloat16
VMEM_LIMIT = 48 * 1024 * 1024


def contract_rows(left, right):
    return lax.dot_general(left, right, (((0,), (0,)), ((), ())), preferred_element_type=F32)


def contract_cols(left, right):
    return lax.dot_general(left, right, (((1,), (1,)), ((), ())), preferred_element_type=F32)


def dot(left, right, precision=None):
    return lax.dot_general(
        left, right, (((1,), (0,)), ((), ())), precision=precision, preferred_element_type=F32
    )


def root_scale(v):
    return lax.rsqrt(jnp.mean(v * v, axis=-1, keepdims=True) + EPSILON)


def norm_backward(v, scale, gain, upstream):
    scaled_up = upstream * gain
    return scale * scaled_up - v * scale * scale * scale * jnp.mean(
        scaled_up * v, axis=-1, keepdims=True
    )


def flip(x, axis, bit):
    n = lax.axis_size(axis)
    return lax.ppermute(x, axis, [(i, i ^ bit) for i in range(n)])


def shift(x, axis, by):
    n = lax.axis_size(axis)
    return lax.ppermute(x, axis, [(i, i + by) for i in range(n) if 0 <= i + by < n])


def turn(x, by):
    n = lax.axis_size("seq")
    return lax.ppermute(x, "seq", [(i, (i + 2 * by) % n) for i in range(n)])


def ring(x):
    out = []
    for _ in range(lax.axis_size("seq") // 2 - 1):
        x = turn(x, 1)
        out.append(x)
    return out


def scatter_sum(part):
    half = part[0].shape[0] // 2
    got = flip(part[1].astype(BF16), "head", 1)
    kept = part[0] + got.astype(F32)
    got = flip(kept[half:].astype(BF16), "head", 2)
    return kept[:half] + got.astype(F32)


def gather_half(own):
    return jnp.concatenate([own, flip(own, "head", 2)], axis=0)


def gather_full(half):
    return jnp.concatenate([half, flip(half, "head", 1)], axis=0)


def total(x, axes):
    for axis in axes:
        bit = 1
        while bit < lax.axis_size(axis):
            x = x + flip(x, axis, bit)
            bit *= 2
    return x


def carry(decay, state, sign):
    found = None
    step = 1
    while step < lax.axis_size("seq"):
        got_decay = shift(decay, "seq", sign * step)
        got = shift(state.astype(BF16), "seq", sign * step).astype(F32)
        if found is None:
            found = (got_decay, got)
        else:
            found = (found[0] * got_decay, found[0][:, None] * got + found[1])
        step *= 2
        if step < lax.axis_size("seq"):
            state = decay[:, None] * got + state
            decay = decay * got_decay
    return found[1]


def grids(n):
    return (
        lax.broadcasted_iota(jnp.int32, (n, n), 0),
        lax.broadcasted_iota(jnp.int32, (n, n), 1),
    )


def column(row, rows, cols, back):
    return jnp.sum(jnp.where(cols == rows - back, row, 0.0), axis=1, keepdims=True)


def tap_masks(start_row, rows, cols):
    here, one, two = (column(start_row, rows, cols, back) for back in range(3))
    first = 1.0 - here
    second = first * (1.0 - one)
    return here, (first, second, second * (1.0 - two))


def segments(start_row, start_col, rows, cols):
    seg_col = jnp.sum(jnp.where(cols <= rows, start_row, 0.0), axis=1, keepdims=True)
    seg_row = jnp.sum(jnp.where(rows <= cols, start_col, 0.0), axis=0, keepdims=True)
    return seg_col, seg_row, jnp.sum(start_row)


def block_middles(x):
    n = x.shape[0] // BLOCK
    mids = []
    for b in range(n):
        last = x[(b + 1) * BLOCK - 1 : (b + 1) * BLOCK]
        before = x[b * BLOCK - 1 : b * BLOCK] if b else jnp.zeros_like(last)
        mids.append(0.5 * (before + last))
    return mids


def spread(mids):
    return jnp.concatenate(
        [jnp.broadcast_to(mid, (BLOCK, mid.shape[1])) for mid in mids], axis=0
    )


def state_kernel(
    pre_q, pre_k, pre_v, edge, taps, start_row, low_rank, lowrank_up, bias,
    u_out, v_out, x_out, logit_out, state_out, last_out, ext,
):
    n = pre_q.shape[0]
    rows, cols = grids(n)
    sr = start_row[...]
    start_col, masks = tap_masks(sr, rows, cols)
    seg_col, _, seg_last = segments(sr, start_col, rows, cols)
    ext[0:8, :] = edge[...].astype(F32)
    ext[8:, 0:DK] = pre_q[...].astype(F32)
    ext[8:, DK : 2 * DK] = pre_k[...].astype(F32)
    ext[8:, 2 * DK :] = pre_v[...].astype(F32)
    for part in range(4):
        lanes = slice(part * DK, (part + 1) * DK)
        u = ext[8 : 8 + n, lanes] * taps[3:4, lanes]
        for back in range(1, TAPS):
            u = u + ext[8 - back : 8 - back + n, lanes] * taps[3 - back : 4 - back, lanes] * masks[
                back - 1
            ]
        u_out[:, lanes] = u
        if part >= 2:
            v_out[:, (part - 2) * DK : (part - 1) * DK] = (u * jax.nn.sigmoid(u)).astype(BF16)
    logit = dot(low_rank[...], lowrank_up[...]) + bias[...]
    logit_out[...] = logit
    decays = (jnp.minimum(logit, 0.0) - jnp.log1p(jnp.exp(-jnp.abs(logit)))) * (1.0 / 16.0)
    x = dot((cols <= rows).astype(F32), decays, HIGHEST)
    x_out[...] = x
    u = u_out[:, DK : 2 * DK]
    keys = u * jax.nn.sigmoid(u)
    tail = (seg_col == seg_last).astype(F32)
    final = x[n - 1 : n]
    closing = (keys * jnp.exp(final - x) * tail).astype(BF16)
    state_out[...] = contract_rows(closing, v_out[...])
    last_out[...] = jnp.exp(final) * (seg_last == 0.0).astype(F32)


def local_scores(q, k, x):
    n = x.shape[0] // BLOCK
    mids = block_middles(x)
    mid = spread(mids)
    grow, shrink = jnp.exp(x - mid), jnp.exp(mid - x)
    rising, falling = q * grow, (k * shrink).astype(BF16)
    lifted, scales = [], []
    for j in range(n):
        pieces = [jnp.exp(mids[i] - mids[j]) for i in range(j, n)]
        scale = spread(pieces)
        scales.append(scale)
        lifted.append((rising[j * BLOCK :] * scale).astype(BF16))
    return grow, shrink, lifted, scales, falling


def output_kernel(
    place, u_qk, v, x_in, start_row, state_in, outgate, gain,
    gated_out, mixed_out, scores_out,
):
    n = x_in.shape[0]
    blocks = n // BLOCK
    rows, cols = grids(n)
    sr = start_row[...]
    start_col = column(sr, rows, cols, 0)
    seg_col, seg_row, _ = segments(sr, start_col, rows, cols)
    allowed = (cols <= rows) & (seg_col == seg_row)
    alive = (seg_col == 0.0).astype(F32)
    x = x_in[...]
    uq = u_qk[:, 0:DK]
    uk = u_qk[:, DK : 2 * DK]
    q = uq * jax.nn.sigmoid(uq) * DK**-0.5
    k = uk * jax.nn.sigmoid(uk)
    _, _, lifted, _, falling = local_scores(q, k, x)
    scores_out[...] = jnp.zeros_like(scores_out)
    for j in range(blocks):
        lo, hi = j * BLOCK, (j + 1) * BLOCK
        s = contract_cols(lifted[j], falling[lo:hi])
        scores_out[lo:, lo:hi] = jnp.where(allowed[lo:, lo:hi], s, 0.0).astype(BF16)
    carried = (q * jnp.exp(x) * alive).astype(BF16)
    out = dot(scores_out[...], v[...]) + dot(carried, state_in[...])
    mixed_out[...] = out
    og = outgate[...]
    gated = (out * root_scale(out) * gain[...] * (og * jax.nn.sigmoid(og))).astype(BF16)
    m = place[0]
    for b in range(blocks):
        at = pl.multiple_of((m ^ b) * BLOCK, BLOCK)
        gated_out[pl.ds(at, BLOCK), :] = gated[b * BLOCK : (b + 1) * BLOCK]


def gate_back_kernel(
    place, d_gated, mixed, outgate, gain, u_q, x_in, start_row,
    d_outgate_out, d_mixed_out, gain_out, direct_out, order,
):
    n = x_in.shape[0]
    blocks = n // BLOCK
    m = place[0]
    for b in range(blocks):
        at = pl.multiple_of((m ^ b) * BLOCK, BLOCK)
        order[b * BLOCK : (b + 1) * BLOCK, :] = d_gated[pl.ds(at, BLOCK), :]
    up = order[...]
    og = outgate[...]
    sig = jax.nn.sigmoid(og)
    out = mixed[...]
    scale = root_scale(out)
    g = gain[...]
    d_outgate = (up * (out * scale * g) * sig * (1.0 + og * (1.0 - sig))).astype(BF16)
    for b in range(blocks):
        at = pl.multiple_of((m ^ b) * BLOCK, BLOCK)
        d_outgate_out[pl.ds(at, BLOCK), :] = d_outgate[b * BLOCK : (b + 1) * BLOCK]
    d_norm = up * (og * sig)
    gain_out[...] = jnp.sum(d_norm * out * scale, axis=0, keepdims=True)
    d_mixed = norm_backward(out, scale, g, d_norm).astype(BF16)
    d_mixed_out[...] = d_mixed
    rows, cols = grids(n)
    seg_col = jnp.sum(jnp.where(cols <= rows, start_row[...], 0.0), axis=1, keepdims=True)
    alive = (seg_col == 0.0).astype(F32)
    uq = u_q[...]
    carried = (uq * jax.nn.sigmoid(uq) * DK**-0.5 * jnp.exp(x_in[...]) * alive).astype(BF16)
    direct_out[...] = contract_rows(carried, d_mixed)


def mixer_back_kernel(
    place, d_mixed, state_in, later, u_in, v, x_in, scores, pre_q, pre_k, pre_v, edge, taps,
    logit, start_row, low_rank, lowrank_up,
    d_pre_out, last_rows_out, back_rows_out, taps_out, d_low_out, d_up_out, d_bias_out,
    ext, du_ext, small, dx_buf,
):
    n = x_in.shape[0]
    blocks = n // BLOCK
    m = place[0]
    rows, cols = grids(n)
    sr = start_row[...]
    start_col, masks = tap_masks(sr, rows, cols)
    seg_col, seg_row, seg_last = segments(sr, start_col, rows, cols)
    allowed = (cols <= rows) & (seg_col == seg_row)
    alive = (seg_col == 0.0).astype(F32)
    tail = (seg_col == seg_last).astype(F32)
    x = x_in[...]
    uq = u_in[:, 0:DK]
    uk = u_in[:, DK : 2 * DK]
    sq, sk = jax.nn.sigmoid(uq), jax.nn.sigmoid(uk)
    q = uq * sq * DK**-0.5
    k = uk * sk
    grow, shrink, lifted, scales, falling = local_scores(q, k, x)
    dm = d_mixed[...]
    later_f = later[...]
    state_f = state_in[...].astype(F32)
    d_scores = jnp.where(allowed, contract_cols(dm, v[...]), 0.0).astype(BF16)
    final = x[n - 1 : n]
    leaving = jnp.exp(final - x) * tail
    closing = (k * leaving).astype(BF16)
    later_b = later_f.astype(BF16)
    d_closing = contract_cols(v[...], later_b)
    entering = jnp.exp(x) * alive
    d_carried = contract_cols(dm, state_in[...])
    dq = d_carried * entering
    dk = d_closing * leaving
    closed = d_closing * closing.astype(F32)
    dx_buf[...] = d_carried * (q * entering) - closed
    through = jnp.sum(later_f * state_f, axis=1, keepdims=True)
    through_row = jnp.sum(jnp.where(rows == cols, through, 0.0), axis=0, keepdims=True)
    at_last = jnp.sum(closed, axis=0, keepdims=True) + through_row * jnp.exp(final) * (
        seg_last == 0.0
    ).astype(F32)
    dx_buf[n - 1 : n, :] = dx_buf[n - 1 : n, :] + at_last
    dq_parts = [dq[b * BLOCK : (b + 1) * BLOCK] for b in range(blocks)]
    dk_parts = []
    for j in range(blocks):
        lo, hi = j * BLOCK, (j + 1) * BLOCK
        ds = d_scores[lo:, lo:hi]
        d_lift = dot(ds, falling[lo:hi])
        d_fall = contract_rows(ds, lifted[j])
        dx_buf[lo:, :] = dx_buf[lo:, :] + d_lift * lifted[j].astype(F32)
        dx_buf[lo:hi, :] = dx_buf[lo:hi, :] - d_fall * falling[lo:hi].astype(F32)
        d_rise = d_lift * scales[j] * grow[lo:]
        for b in range(j, blocks):
            dq_parts[b] = dq_parts[b] + d_rise[(b - j) * BLOCK : (b - j + 1) * BLOCK]
        dk_parts.append(dk[lo:hi] + d_fall * shrink[lo:hi])
    dq = jnp.concatenate(dq_parts, axis=0)
    dk = jnp.concatenate(dk_parts, axis=0)
    d_decays = dot((cols >= rows).astype(F32), dx_buf[...], HIGHEST)
    d_logit = (d_decays * jax.nn.sigmoid(-logit[...]) * (1.0 / 16.0)).astype(BF16)
    d_bias_out[...] = jnp.sum(d_logit.astype(F32), axis=0, keepdims=True)
    d_up_out[...] = contract_rows(low_rank[...], d_logit)
    d_low_out[...] = contract_cols(d_logit, lowrank_up[...])

    ext[0:8, :] = edge[...].astype(F32)
    ext[8:, 0:DK] = pre_q[...].astype(F32)
    ext[8:, DK : 2 * DK] = pre_k[...].astype(F32)
    ext[8:, 2 * DK :] = pre_v[...].astype(F32)
    du_ext[n:, :] = jnp.zeros((8, du_ext.shape[1]), F32)
    du_ext[0:n, 0:DK] = dq * (DK**-0.5) * (sq * (1.0 + uq * (1.0 - sq)))
    du_ext[0:n, DK : 2 * DK] = dk * (sk * (1.0 + uk * (1.0 - sk)))
    dv = contract_rows(scores[...], dm) + dot(closing, later_b)
    for half in range(2):
        uv = u_in[:, (2 + half) * DK : (3 + half) * DK]
        sv = jax.nn.sigmoid(uv)
        du_ext[0:n, (2 + half) * DK : (3 + half) * DK] = dv[:, half * DK : (half + 1) * DK] * (
            sv * (1.0 + uv * (1.0 - sv))
        )
    ahead = []
    for back in range(1, TAPS):
        mask_row = jnp.sum(jnp.where(rows == cols, masks[back - 1], 0.0), axis=0, keepdims=True)
        ahead.append(column(mask_row, rows, cols, -back))
    for part in range(4):
        lanes = slice(part * DK, (part + 1) * DK)
        du = du_ext[0:n, lanes]
        d_pre = du * taps[3:4, lanes]
        back_rows = jnp.zeros((8, DK), F32)
        taps_out[3:4, lanes] = jnp.sum(du * ext[8 : 8 + n, lanes], axis=0, keepdims=True)
        for back in range(1, TAPS):
            weight = taps[3 - back : 4 - back, lanes]
            d_pre = d_pre + du_ext[back : back + n, lanes] * weight * ahead[back - 1]
            masked = du * masks[back - 1]
            taps_out[3 - back : 4 - back, lanes] = jnp.sum(
                masked * ext[8 - back : 8 - back + n, lanes], axis=0, keepdims=True
            )
            small[0:8, :] = jnp.zeros((8, DK), F32)
            small[8:16, :] = masked[0:8]
            back_rows = back_rows + small[back : back + 8, :] * weight
        back_rows_out[:, lanes] = back_rows
        last_rows_out[:, lanes] = d_pre[n - 8 :]
        rounded = d_pre.astype(BF16)
        for b in range(blocks):
            at = pl.multiple_of((m ^ b) * BLOCK, BLOCK)
            d_pre_out[pl.ds(at, BLOCK), lanes] = rounded[b * BLOCK : (b + 1) * BLOCK]


def call(body, outs, scratch, args, flops, placed=True):
    in_specs = [pl.BlockSpec(memory_space=pltpu.VMEM) for _ in args]
    if placed:
        in_specs[0] = pl.BlockSpec(memory_space=pltpu.SMEM)
    moved = sum(a.size * a.dtype.itemsize for a in args)
    return pl.pallas_call(
        body,
        out_shape=[jax.ShapeDtypeStruct(shape, kind) for shape, kind in outs],
        in_specs=in_specs,
        out_specs=[pl.BlockSpec(memory_space=pltpu.VMEM) for _ in outs],
        scratch_shapes=[pltpu.VMEM(shape, kind) for shape, kind in scratch],
        compiler_params=pltpu.CompilerParams(vmem_limit_bytes=VMEM_LIMIT),
        cost_estimate=pl.CostEstimate(flops=flops, bytes_accessed=moved, transcendentals=0),
    )(*args)


def on_device(
    block_input,
    first_gain,
    query_weight,
    key_weight,
    value_weight,
    query_conv,
    key_conv,
    value_conv,
    lowrank_down,
    lowrank_up,
    decay_bias,
    outgate_weight,
    outnorm_gain,
    output_weight,
    second_gain,
    gate_weight,
    up_weight,
    down_weight,
    starts,
    valid_mask,
    cotangent,
    teacher,
):
    length = block_input.shape[0]
    quarter, half = length // 4, length // 2
    places = lax.axis_size("seq")
    turns = places // 2
    share = D // places
    seq, head = lax.axis_index("seq"), lax.axis_index("head")
    mine = (head % 2) * 2 + head // 2
    zone, side = seq // 2, seq % 2
    place = mine.astype(jnp.int32).reshape(1)
    loss_weight = float(length * places * D // 8)

    def own(x):
        return lax.dynamic_slice_in_dim(x, mine * quarter, quarter, 0)

    def own_first(x):
        return jnp.concatenate(
            [lax.dynamic_slice_in_dim(x, (mine ^ p) * quarter, quarter, 0) for p in range(4)], axis=0
        )

    def natural(own_rows):
        near = gather_half(own_rows)
        swapped = jnp.concatenate([near[quarter:], near[:quarter]], axis=0)
        near = jnp.where(head // 2 == 0, near, swapped)
        far = flip(near, "head", 1)
        return jnp.where(
            head % 2 == 0,
            jnp.concatenate([near, far], axis=0),
            jnp.concatenate([far, near], axis=0),
        ).astype(F32)

    def rows_of(x, where):
        return lax.dynamic_slice_in_dim(x, where * share, share, 1)

    valid_float = valid_mask.astype(F32)
    valid_count = total(jnp.full((8, 128), jnp.sum(valid_float), F32), ["seq"])[0, 0]
    input_float = block_input.astype(F32)
    normed = (input_float * root_scale(input_float) * first_gain).astype(BF16)
    pre_k = dot(normed, key_weight).astype(BF16)
    pre_v = dot(normed, value_weight).astype(BF16)
    pre_q = dot(normed, query_weight).astype(BF16)
    start_row = starts.astype(F32).reshape(1, length)
    last_start, before_last = start_row[0, length - 1], start_row[0, length - 2]
    keep_one = 1.0 - last_start
    tail_keep = jnp.concatenate(
        [jnp.zeros((5,), F32), jnp.stack([keep_one * (1.0 - before_last), keep_one, jnp.ones((), F32)])]
    )
    tails = jnp.concatenate([pre_q[length - 8 :], pre_k[length - 8 :], pre_v[length - 8 :]], axis=1)
    edge = shift(tails * tail_keep[:, None].astype(BF16), "seq", 1)
    taps = jnp.concatenate([query_conv, key_conv, value_conv], axis=1)
    low_rank = dot(normed, lowrank_down).astype(BF16)
    bias_row = decay_bias.reshape(1, DK)
    channels = 2 * DK + DV
    u, v, x, logit, end_state, last = call(
        state_kernel,
        [
            ((length, channels), F32),
            ((length, DV), BF16),
            ((length, DK), F32),
            ((length, DK), F32),
            ((DK, DV), F32),
            ((1, DK), F32),
        ],
        [((length + 8, channels), F32)],
        (pre_q, pre_k, pre_v, edge, taps, start_row, low_rank, lowrank_up, bias_row),
        400_000_000,
        placed=False,
    )
    outgate = dot(normed, outgate_weight)
    last = last.reshape(DK)
    state_in = carry(last, end_state, 1).astype(BF16)
    gain_row = outnorm_gain.reshape(1, DV)
    gated, mixed, scores = call(
        output_kernel,
        [((length, DV), BF16), ((length, DV), F32), ((length, length), BF16)],
        [],
        (place, u, v, x, start_row, state_in, outgate, gain_row),
        400_000_000,
    )

    def parts(make):
        far = make(slice(half, length))
        return make(slice(0, half)), far

    branch = scatter_sum(parts(lambda r: contract_cols(gated[r], output_weight)))
    input_own = own(block_input).astype(F32)
    hidden = input_own + branch
    second_scale = root_scale(hidden)
    ffn_half = gather_half((hidden * second_scale * second_gain).astype(BF16))
    ffn_in = gather_full(ffn_half)
    gate_val = dot(ffn_in, gate_weight)
    up_val = dot(ffn_in, up_weight)
    sigmoid_gate = jax.nn.sigmoid(gate_val)
    activated = (gate_val * sigmoid_gate * up_val).astype(BF16)
    ffn_out = scatter_sum(parts(lambda r: contract_cols(activated[r], down_weight)))
    output_own = hidden + ffn_out
    valid_own = own(valid_float)[:, None]
    mismatch = output_own - own(teacher).astype(F32)
    squared = jnp.sum(valid_own * mismatch * mismatch)
    d_out = own(cotangent).astype(F32) + valid_own * 2.0 * loss_weight * mismatch / (valid_count * D)
    d_ffn_half = gather_half(d_out.astype(BF16))
    d_ffn = gather_full(d_ffn_half)
    d_act = dot(d_ffn, down_weight)
    d_gate_val = (d_act * up_val * sigmoid_gate * (1.0 + gate_val * (1.0 - sigmoid_gate))).astype(BF16)
    d_up_val = (d_act * gate_val * sigmoid_gate).astype(BF16)
    d_nffn = scatter_sum(
        parts(
            lambda r: contract_cols(d_gate_val[r], gate_weight) + contract_cols(d_up_val[r], up_weight)
        )
    )
    second_part = jnp.sum(d_nffn * hidden * second_scale, axis=0)
    d_hidden = d_out + norm_backward(hidden, second_scale, second_gain, d_nffn)
    d_branch_half = gather_half(d_hidden.astype(BF16))
    d_branch = gather_full(d_branch_half)

    d_gated = dot(d_branch, output_weight)
    d_outgate, d_mixed, outnorm_part, direct = call(
        gate_back_kernel,
        [((length, DV), BF16), ((length, DV), BF16), ((1, DV), F32), ((DK, DV), F32)],
        [((length, DV), F32)],
        (place, d_gated, mixed, outgate, gain_row, u[:, :DK], x, start_row),
        200_000_000,
    )
    later = carry(last, direct, -1)
    d_pre, last_rows, back_rows, taps_part, d_low, lowup_part, bias_part = call(
        mixer_back_kernel,
        [
            ((length, channels), BF16),
            ((8, channels), F32),
            ((8, channels), F32),
            ((TAPS, channels), F32),
            ((length, RANK), F32),
            ((RANK, DK), F32),
            ((1, DK), F32),
        ],
        [
            ((length + 8, channels), F32),
            ((length + 8, channels), F32),
            ((16, DK), F32),
            ((length, DK), F32),
        ],
        (
            place, d_mixed, state_in, later, u, v, x, scores, pre_q, pre_k, pre_v, edge, taps,
            logit, start_row, low_rank, lowrank_up,
        ),
        1_000_000_000,
    )
    from_next = shift(back_rows, "seq", -1)
    fixed = (last_rows + from_next * tail_keep[:, None]).astype(BF16)
    d_pre = lax.dynamic_update_slice(d_pre, fixed, ((mine ^ 3) * quarter + quarter - 8, 0))
    d_lowrank = total(d_low, ["head"]).astype(BF16)
    d_first = scatter_sum(
        parts(
            lambda r: contract_cols(d_outgate[r], outgate_weight)
            + contract_cols(d_pre[r, :DK], query_weight)
            + contract_cols(d_pre[r, DK : 2 * DK], key_weight)
            + contract_cols(d_pre[r, 2 * DK :], value_weight)
        )
    )
    d_first = d_first + contract_cols(own(d_lowrank), lowrank_down)
    first_scale = root_scale(input_own)
    first_part = jnp.sum(d_first * input_own * first_scale, axis=0)
    grad_own = d_hidden + norm_backward(input_own, first_scale, first_gain, d_first)
    block_output = natural(output_own.astype(BF16))
    grad_input = natural(grad_own.astype(BF16))

    def collect(half_rows):
        got = ring(half_rows)
        return jnp.concatenate(got + [flip(g, "head", 1) for g in got], axis=0)

    ffn_far, d_ffn_far = collect(ffn_half), collect(d_ffn_half)
    gate_far, up_far = dot(ffn_far, gate_weight), dot(ffn_far, up_weight)
    act_far = dot(d_ffn_far, down_weight)
    sig_far = jax.nn.sigmoid(gate_far)
    activated_far = (gate_far * sig_far * up_far).astype(BF16)
    d_gate_far = (act_far * up_far * sig_far * (1.0 + gate_far * (1.0 - sig_far))).astype(BF16)
    d_up_far = (act_far * gate_far * sig_far).astype(BF16)

    def pair_sum(make):
        sent = make(zone * 2 + 1 - side).astype(BF16)
        got = flip(sent, "seq", 1)
        return make(zone * 2 + side) + got.astype(F32)

    def ffn_grad(near_left, far_left, near_right, far_right):
        return pair_sum(
            lambda where: contract_rows(rows_of(near_left, where), near_right)
            + contract_rows(rows_of(far_left, where), far_right)
        )

    grad_gate = ffn_grad(ffn_in, ffn_far, d_gate_val, d_gate_far)
    grad_up = ffn_grad(ffn_in, ffn_far, d_up_val, d_up_far)
    grad_down = ffn_grad(d_ffn, d_ffn_far, activated, activated_far)

    def slices(x, half_rows):
        both = [lax.dynamic_slice_in_dim(x, zone * 2 * share, 2 * share, 1)]
        for by in range(1, turns):
            target = lax.rem(zone + by, turns)
            sent = lax.dynamic_slice_in_dim(half_rows, target * 2 * share, 2 * share, 1)
            got = turn(sent, by)
            both.append(jnp.concatenate([got, flip(got, "head", 1)], axis=0))
        return both

    def mixer_grad(lefts, right):
        rights = [right, *ring(right)]

        def make(where):
            at = (where - zone * 2) * share
            acc = None
            for left, one in zip(lefts, rights):
                term = contract_rows(lax.dynamic_slice_in_dim(left, at, share, 1), one)
                acc = term if acc is None else acc + term
            return acc

        return pair_sum(make)

    normed_first = own_first(normed)
    normed_slices = slices(normed_first, normed_first[:half])
    branch_slices = slices(d_branch, d_branch_half)
    grad_output = mixer_grad(branch_slices, gated)
    grad_outgate = mixer_grad(normed_slices, d_outgate)
    grad_pre = mixer_grad(normed_slices, d_pre)

    shared = jnp.concatenate(
        [second_part.reshape(4, DV), outnorm_part, jnp.full((3, DV), squared, F32)], axis=0
    )
    shared = total(shared, ["seq", "head"])
    grad_second_gain = shared[0:4].reshape(D)
    grad_outnorm = shared[4]
    distill = shared[5, 0] / (valid_count * D)
    first_total = total(first_part.reshape(4, DV), ["seq", "head"]).reshape(D)
    low_part = contract_rows(d_lowrank, normed)
    apart = jnp.concatenate(
        [
            taps_part.reshape(2, D),
            lowup_part.reshape(2, D),
            jnp.concatenate([bias_part, jnp.zeros((1, D - DK), F32)], axis=1),
            jnp.zeros((3, D), F32),
            low_part,
        ],
        axis=0,
    )
    apart = total(apart, ["seq"])
    taps_sum = apart[0:2].reshape(TAPS, channels)
    grad_lowrank_up = apart[2:4].reshape(RANK, DK)
    grad_bias = apart[4, :DK]
    grad_lowrank_down = lax.dynamic_slice_in_dim(apart[8:], seq * share, share, 1).T
    return (
        block_output,
        distill,
        grad_input,
        first_total,
        grad_pre[:, :DK],
        grad_pre[:, DK : 2 * DK],
        grad_pre[:, 2 * DK :],
        taps_sum[:, :DK],
        taps_sum[:, DK : 2 * DK],
        taps_sum[:, 2 * DK :],
        grad_lowrank_down,
        grad_lowrank_up,
        grad_bias,
        grad_outgate,
        grad_outnorm,
        grad_output,
        grad_second_gain,
        grad_gate,
        grad_up,
        grad_down,
    )


def solution(mesh):
    rows, cols, whole = P("seq", None), P(None, "head"), P()
    in_specs = (
        rows, whole, cols, cols, cols, cols, cols, cols, whole, cols, P("head"), cols, whole, cols,
        whole, cols, cols, cols, P("seq"), P("seq"), rows, rows,
    )
    tiles = P("seq", "head")
    out_specs = (
        rows, whole, rows, whole, tiles, tiles, tiles, cols, cols, cols, rows, cols, P("head"), tiles,
        whole, tiles, whole, tiles, tiles, tiles,
    )
    return jax.shard_map(
        on_device, mesh=mesh, in_specs=in_specs, out_specs=out_specs, check_vma=False
    )
```

time: 1040 us -> 508 us (0.49)
  waiting for transfers between devices: 578 us -> 201 us
  blocking collectives: 107 us -> 0 us
  starting transfers between devices: 6.93 us -> 92.4 us
  other arithmetic: 93.2 us -> 37.1 us
  local copies, waits for them, and re-layouts: 78.6 us -> 35.4 us
  matrix products: 140 us -> 119 us
  between operations: 17.9 us -> 7.15 us
    reduce_scatter x1 -> x0, waiting for transfers between devices: 365 us -> none  [on_device(): lax.psum_scatter(jnp.concatenate([contract_rows(normed, d_pre), contract_...]
    ppermute x2 -> x87, waiting for transfers between devices: 0.01 us -> 201 us  [the longest x54 98.1 us: flip(): return lax.ppermute(x, axis, [(i, i ^ bit) for i in range(n)])]
    psum x4 -> x0, waiting for transfers between devices: 137 us -> none  [the longest x1 42.9 us: on_device(): lax.psum(contract_cols(gated_out, output_weight).astype(jnp.bfloat16), 'h...]
    ppermute x2 -> x87, starting transfers between devices: 6.26 us -> 92.4 us  [the longest x54 40.8 us: flip(): return lax.ppermute(x, axis, [(i, i ^ bit) for i in range(n)])]
    all_gather x2 -> x0, waiting for transfers between devices: 75.3 us -> none  [the longest x1 49.2 us: prefix(): gathered = jax.tree.map(lambda a: lax.all_gather(a, axis), part)]
    psum x3 -> x0, blocking collectives: 67.2 us -> none  [the longest x1 39 us: on_device(): lax.psum(grad_conv.astype(jnp.bfloat16), 'seq').astype(jnp.float32)]
    dot_general x61 -> x12, matrix products: 101 us -> 41.4 us  [dot(): lax.dot_general(left, right, (((1,), (0,)), ((), ())), precision=precisio...]
    all_gather x2 -> x0, blocking collectives: 40.1 us -> none  [the longest x1 20.7 us: prefix_2(): lax.all_gather(a.astype(kind), axis)]
  transfers between devices with their start and end apart: 9 -> 87, of which waited for: 7 -> 38; matrix products, arithmetic and copies ran while one was open for 3% -> 34% of each run, Pallas kernels for 0% -> 1%
where the time goes in v1:
time: 508 us; the launch traced here: 499 us
  waiting for transfers between devices  201 us (40%)
  matrix products  119 us (23%)
  starting transfers between devices  92.4 us (18%)
  other arithmetic  37.1 us (7%)
  local copies, waits for them, and re-layouts  35.4 us (7%)
  between operations  7.15 us (1%)
  Pallas kernels  6.89 us (1%)
    ppermute x54, waiting for transfers between devices, flip(): return lax.ppermute(x, axis, [(i, i ^ bit) for i in range(n)])  98.1 us
    ppermute x21, waiting for transfers between devices, turn(): return lax.ppermute(x, 'seq', [(i, (i + 2 * by) % n) for i in range(n)])  80.9 us
    dot_general x37, matrix products, contract_rows(): lax.dot_general(left, right, (((0,), (0,)), ((), ())), preferred_element_...  53.2 us
    dot_general x12, matrix products, dot(): lax.dot_general(left, right, (((1,), (0,)), ((), ())), precision=precisio...  41.4 us
    ppermute x54, starting transfers between devices, flip(): return lax.ppermute(x, axis, [(i, i ^ bit) for i in range(n)])  40.8 us
    ppermute x12, starting transfers between devices, shift(): lax.ppermute(x, axis, [(i, i + by) for i in range(n) if 0 <= i + by < n])  32.1 us
    dot_general x17, matrix products, contract_cols(): lax.dot_general(left, right, (((1,), (1,)), ((), ())), preferred_element_...  24.3 us
    ppermute x12, waiting for transfers between devices, shift(): lax.ppermute(x, axis, [(i, i + by) for i in range(n) if 0 <= i + by < n])  22 us
  transfers between devices with their start and end apart: 87, of which 38 were waited for; matrix products, arithmetic and copies ran while one was open for 34% of the time, Pallas kernels for 1%

profile of v1, /device:TPU:0, one launch (start us, length us, event | category | flops | bytes accessed | tf_op | source)
XLA Modules:
  0.0 498.8 jit_solution(12822497331876540606)
XLA Ops:
  9.9 4.8 collective-permute-start
  18.9 4.2 collective-permute-start.3
  23.2 4.4 collective-permute-done.3
  28.4 7.0 %collective-permute-start.4 = (bf16[256,512]{1,0:T(8,128)(2,1)}, bf16[256,512]{1,0:T(8,128)(2,1)}, u32[]{:S(2)}, u32[]{:S(2)}) collective-permute-start(bf16[256,512]{1,0:T(8,128)(2,1)} %fusion.62), channel_id=1, source_target_pairs={{0,8},{4,12},{8,16},{12,20},{16,24},{20,28},{1,9},{5,13},{9,17},{1... | collective-permute-start | bytes 786440 | tf_op jit(solution)/shard_map/ppermute | solution.py:55
  38.3 4.8 collective-permute-done.28
  45.6 5.0 collective-permute-start.5
  102.1 4.8 fusion.173
  115.1 12.2 %collective-permute-done.67 = bf16[256,512]{1,0:T(8,128)(2,1)} collective-permute-done((bf16[256,512]{1,0:T(8,128)(2,1)S(1)}, bf16[256,512]{1,0:T(8,128)(2,1)}, u32[]{:S(2)}, u32[]{:S(2)}) %collective-permute-start.67) | collective-permute-done | bytes 262176 | tf_op jit(solution)/shard_map/ppermute | solution.py:60
  132.8 15.6 %collective-permute-done.73 = bf16[128,2048]{1,0:T(8,128)(2,1)S(1)} collective-permute-done((bf16[128,2048]{1,0:T(8,128)(2,1)S(1)}, bf16[128,2048]{1,0:T(8,128)(2,1)S(1)}, u32[]{:S(2)}, u32[]{:S(2)}) %collective-permute-start.73) | collective-permute-done | bytes 524320 | tf_op jit(solution)/shard_map/ppermute | solution.py:60
  152.9 3.6 collective-permute-done.17
  156.8 8.3 %collective-permute-done.74 = bf16[128,2048]{1,0:T(8,128)(2,1)S(1)} collective-permute-done((bf16[128,2048]{1,0:T(8,128)(2,1)S(1)}, bf16[128,2048]{1,0:T(8,128)(2,1)S(1)}, u32[]{:S(2)}, u32[]{:S(2)}) %collective-permute-start.74) | collective-permute-done | bytes 524320 | tf_op jit(solution)/shard_map/ppermute | solution.py:60
  175.3 6.6 %fusion.185 = f32[768,1408]{1,0:T(8,128)} fusion(bf16[768,2048]{1,0:T(8,128)(2,1)S(1)} %constant_dynamic-update-slice_fusion.15, bf16[2048,1408]{1,0:T(8,128)(2,1)S(1)} %bitcast.110), kind=kOutput, calls=%fused_computation.326 | convolution fusion | flops 4429185024 | bytes 13238272 | tf_op jit(solution)/shard_map/dot_general | solution.py:32
  195.9 9.5 %collective-permute-done.79 = bf16[128,2048]{1,0:T(8,128)(2,1)} collective-permute-done((bf16[128,2048]{1,0:T(8,128)(2,1)}, bf16[128,2048]{1,0:T(8,128)(2,1)}, u32[]{:S(2)}, u32[]{:S(2)}) %collective-permute-start.79) | collective-permute-done | bytes 524320 | tf_op jit(solution)/shard_map/ppermute | solution.py:60
  211.6 9.3 %collective-permute-done.80 = bf16[128,2048]{1,0:T(8,128)(2,1)} collective-permute-done((bf16[128,2048]{1,0:T(8,128)(2,1)}, bf16[128,2048]{1,0:T(8,128)(2,1)}, u32[]{:S(2)}, u32[]{:S(2)}) %collective-permute-start.80) | collective-permute-done | bytes 524320 | tf_op jit(solution)/shard_map/ppermute | solution.py:60
  230.8 6.2 %collective-permute-done.68 = bf16[128,512]{1,0:T(8,128)(2,1)S(1)} collective-permute-done((bf16[128,512]{1,0:T(8,128)(2,1)S(1)}, bf16[128,512]{1,0:T(8,128)(2,1)S(1)}, u32[]{:S(2)}, u32[]{:S(2)}) %collective-permute-start.68) | collective-permute-done | bytes 131104 | tf_op jit(solution)/shard_map/ppermute | solution.py:60
  237.1 7.3 %collective-permute-done.65 = bf16[128,512]{1,0:T(8,128)(2,1)S(1)} collective-permute-done((bf16[128,512]{1,0:T(8,128)(2,1)S(1)}, bf16[128,512]{1,0:T(8,128)(2,1)S(1)}, u32[]{:S(2)}, u32[]{:S(2)}) %collective-permute-start.65) | collective-permute-done | bytes 131104 | tf_op jit(solution)/shard_map/ppermute | solution.py:60
  246.6 10.7 %fusion.184 = f32[768,1408]{1,0:T(8,128)} fusion(bf16[768,2048]{1,0:T(8,128)(2,1)S(1)} %constant_dynamic-update-slice_fusion.21, bf16[2048,1408]{1,0:T(8,128)(2,1)} %param.39), kind=kOutput, calls=%fused_computation.325 | convolution fusion | flops 4429185024 | bytes 13238272 | tf_op jit(solution)/shard_map/dot_general | solution.py:32
  257.3 8.7 %multiply_convert_fusion = (bf16[768,1408]{1,0:T(8,128)(2,1)S(1)}, bf16[768,1408]{1,0:T(8,128)(2,1)S(1)}, bf16[768,1408]{1,0:T(8,128)(2,1)S(1)}) fusion(f32[768,1408]{1,0:T(8,128)} %fusion.185, f32[768,1408]{1,0:T(8,128)} %fusion.184, bf16[768,2048]{1,0:T(8,128)(2,1)S(1)} %copy-done.78, bf16[2048,1408]{1,0:T(8,128)(2,1)S(1)} %bitcast.116), kind=kOutput, calls=%fused_computation | convolution fusion | flops 4446486528 | bytes 24051712 | tf_op jit(solution)/shard_map/dot_general | solution.py:32
  285.4 32.6 %collective-permute-done.23 = f32[8,512]{1,0:T(8,128)S(1)} collective-permute-done((f32[8,512]{1,0:T(8,128)S(1)}, f32[8,512]{1,0:T(8,128)S(1)}, u32[]{:S(2)}, u32[]{:S(2)}) %collective-permute-start.23) | collective-permute-done | bytes 16416 | tf_op jit(solution)/shard_map/ppermute | solution.py:50
  318.4 3.4 collective-permute-done.24
  323.0 3.4 collective-permute-done.25
  334.3 3.8 collective-permute-start.58
  340.5 7.8 %collective-permute-start.71 = (bf16[256,512]{1,0:T(8,128)(2,1)}, bf16[256,512]{1,0:T(8,128)(2,1)S(1)}, u32[]{:S(2)}, u32[]{:S(2)}) collective-permute-start(bf16[256,512]{1,0:T(8,128)(2,1)} %fusion.17), channel_id=1, source_target_pairs={{0,4},{4,0},{8,12},{12,8},{16,20},{20,16},{24,28},{28,24},{1,5},{5... | collective-permute-start | bytes 786440 | tf_op jit(solution)/shard_map/ppermute | solution.py:50
  365.2 3.3 fusion
  368.7 3.3 fusion.1
  372.0 8.0 %collective-permute-done.32 = bf16[256,512]{1,0:T(8,128)(2,1)S(1)} collective-permute-done((bf16[256,512]{1,0:T(8,128)(2,1)S(1)}, bf16[256,512]{1,0:T(8,128)(2,1)S(1)}, u32[]{:S(2)}, u32[]{:S(2)}) %collective-permute-start.32) | collective-permute-done | bytes 262176 | tf_op jit(solution)/shard_map/ppermute | solution.py:55
  380.4 3.6 shard_map.368
  407.8 9.8 %collective-permute-done.56 = f32[24,2048]{1,0:T(8,128)S(1)} collective-permute-done((f32[24,2048]{1,0:T(8,128)S(1)}, f32[24,2048]{1,0:T(8,128)S(1)}, u32[]{:S(2)}, u32[]{:S(2)}) %collective-permute-start.56) | collective-permute-done | bytes 196640 | tf_op jit(solution)/shard_map/ppermute | solution.py:50
  428.3 11.5 %collective-permute-done.57 = f32[24,2048]{1,0:T(8,128)S(1)} collective-permute-done((f32[24,2048]{1,0:T(8,128)S(1)}, f32[24,2048]{1,0:T(8,128)S(1)}, u32[]{:S(2)}, u32[]{:S(2)}) %collective-permute-start.57) | collective-permute-done | bytes 196640 | tf_op jit(solution)/shard_map/ppermute | solution.py:50
  449.6 4.5 collective-permute-done.42
  469.8 12.6 %collective-permute-done.53 = bf16[256,1024]{1,0:T(8,128)(2,1)S(1)} collective-permute-done((bf16[256,1024]{1,0:T(8,128)(2,1)}, bf16[256,1024]{1,0:T(8,128)(2,1)S(1)}, u32[]{:S(2)}, u32[]{:S(2)}) %collective-permute-start.53) | collective-permute-done | bytes 524320 | tf_op jit(solution)/shard_map/ppermute | solution.py:60
  486.7 8.7 %collective-permute-done.54 = bf16[256,1024]{1,0:T(8,128)(2,1)S(1)} collective-permute-done((bf16[256,1024]{1,0:T(8,128)(2,1)S(1)}, bf16[256,1024]{1,0:T(8,128)(2,1)S(1)}, u32[]{:S(2)}, u32[]{:S(2)}) %collective-permute-start.54) | collective-permute-done | bytes 524320 | tf_op jit(solution)/shard_map/ppermute | solution.py:50
  (594 shorter events, 242.3 us)
Async XLA Ops:
  28.4 15.3 %collective-permute-start.4 = (bf16[256,512]{1,0:T(8,128)(2,1)}, bf16[256,512]{1,0:T(8,128)(2,1)}, u32[]{:S(2)}, u32[]{:S(2)}) collective-permute-start(bf16[256,512]{1,0:T(8,128)(2,1)} %fusion.62), channel_id=1, source_target_pairs={{0,8},{4,12},{8,16},{12,20},{16,24},{20,28},{1,9},{5,13},{9,17},{1... | collective-permute-start | bytes 786440 | tf_op jit(solution)/shard_map/ppermute | solution.py:55
  78.4 20.2 %collective-permute-start.45 = (bf16[128,512]{1,0:T(8,128)(2,1)}, bf16[128,512]{1,0:T(8,128)(2,1)}, u32[]{:S(2)}, u32[]{:S(2)}) collective-permute-start(bf16[128,512]{1,0:T(8,128)(2,1)} %get-tuple-element.90), channel_id=1, source_target_pairs={{0,8},{4,12},{8,16},{12,20},{16,24},{20,28},{24,0},{28,4},{1,9},{5... | collective-permute-start | bytes 393224 | tf_op jit(solution)/shard_map/ppermute | solution.py:60
  80.8 31.2 %collective-permute-start.48 = (bf16[128,512]{1,0:T(8,128)(2,1)}, bf16[128,512]{1,0:T(8,128)(2,1)}, u32[]{:S(2)}, u32[]{:S(2)}) collective-permute-start(bf16[128,512]{1,0:T(8,128)(2,1)} %get-tuple-element.91), channel_id=1, source_target_pairs={{0,16},{4,20},{8,24},{12,28},{16,0},{20,4},{24,8},{28,12},{1,17},{... | collective-permute-start | bytes 393224 | tf_op jit(solution)/shard_map/ppermute | solution.py:60
  92.3 20.7 %collective-permute-start.51 = (bf16[128,512]{1,0:T(8,128)(2,1)}, bf16[128,512]{1,0:T(8,128)(2,1)S(1)}, u32[]{:S(2)}, u32[]{:S(2)}) collective-permute-start(bf16[128,512]{1,0:T(8,128)(2,1)} %get-tuple-element.89), channel_id=1, source_target_pairs={{0,24},{4,28},{8,0},{12,4},{16,8},{20,12},{24,16},{28,20},{1,25},{... | collective-permute-start | bytes 393224 | tf_op jit(solution)/shard_map/ppermute | solution.py:60
  100.0 27.2 %collective-permute-start.72 = (bf16[128,2048]{1,0:T(8,128)(2,1)}, bf16[128,2048]{1,0:T(8,128)(2,1)S(1)}, u32[]{:S(2)}, u32[]{:S(2)}) collective-permute-start(bf16[128,2048]{1,0:T(8,128)(2,1)} %pad_maximum_fusion.5), channel_id=1, source_target_pairs={{0,8},{4,12},{8,16},{12,20},{16,24},{20,28},{24,0},{28,4},{1,9},{5... | collective-permute-start | bytes 1572872 | tf_op jit(solution)/shard_map/ppermute | solution.py:60
  127.2 203.3 %collective-permute-start.70 = (bf16[256,512]{1,0:T(8,128)(2,1)}, bf16[256,512]{1,0:T(8,128)(2,1)}, u32[]{:S(2)}, u32[]{:S(2)}) collective-permute-start(bf16[256,512]{1,0:T(8,128)(2,1)} %collective-permute-done.67), channel_id=1, source_target_pairs={{0,8},{4,12},{8,16},{12,20},{16,24},{20,28},{24,0},{28,4},{1,9},{5... | collective-permute-start | bytes 786440 | tf_op jit(solution)/shard_map/ppermute | solution.py:60
  127.2 21.2 %collective-permute-start.73 = (bf16[128,2048]{1,0:T(8,128)(2,1)S(1)}, bf16[128,2048]{1,0:T(8,128)(2,1)S(1)}, u32[]{:S(2)}, u32[]{:S(2)}) collective-permute-start(bf16[128,2048]{1,0:T(8,128)(2,1)S(1)} %collective-permute-done.72), channel_id=1, source_target_pairs={{0,8},{4,12},{8,16},{12,20},{16,24},{20,28},{24,0},{28,4},{1,9},{5... | collective-permute-start | bytes 1572872 | tf_op jit(solution)/shard_map/ppermute | solution.py:60
  129.3 19.1 %collective-permute-start.11 = (bf16[64,2048]{1,0:T(8,128)(2,1)S(1)}, bf16[64,2048]{1,0:T(8,128)(2,1)S(1)}, u32[]{:S(2)}, u32[]{:S(2)}) collective-permute-start(bf16[64,2048]{1,0:T(8,128)(2,1)S(1)} %slice.281), channel_id=1, source_target_pairs={{0,2},{1,3},{2,0},{3,1},{4,6},{5,7},{6,4},{7,5},{8,10},{9,11},{10,... | collective-permute-start | bytes 786440 | tf_op jit(solution)/shard_map/ppermute | solution.py:50
  148.4 16.7 %collective-permute-start.74 = (bf16[128,2048]{1,0:T(8,128)(2,1)S(1)}, bf16[128,2048]{1,0:T(8,128)(2,1)S(1)}, u32[]{:S(2)}, u32[]{:S(2)}) collective-permute-start(bf16[128,2048]{1,0:T(8,128)(2,1)S(1)} %collective-permute-done.73), channel_id=1, source_target_pairs={{0,8},{4,12},{8,16},{12,20},{16,24},{20,28},{24,0},{28,4},{1,9},{5... | collective-permute-start | bytes 1572872 | tf_op jit(solution)/shard_map/ppermute | solution.py:60
  156.6 32.5 %collective-permute-start.78 = (bf16[128,2048]{1,0:T(8,128)(2,1)S(1)}, bf16[128,2048]{1,0:T(8,128)(2,1)}, u32[]{:S(2)}, u32[]{:S(2)}) collective-permute-start(bf16[128,2048]{1,0:T(8,128)(2,1)S(1)} %pad_maximum_fusion.6), channel_id=1, source_target_pairs={{0,8},{4,12},{8,16},{12,20},{16,24},{20,28},{24,0},{28,4},{1,9},{5... | collective-permute-start | bytes 1572872 | tf_op jit(solution)/shard_map/ppermute | solution.py:60
  189.1 16.3 %collective-permute-start.79 = (bf16[128,2048]{1,0:T(8,128)(2,1)}, bf16[128,2048]{1,0:T(8,128)(2,1)}, u32[]{:S(2)}, u32[]{:S(2)}) collective-permute-start(bf16[128,2048]{1,0:T(8,128)(2,1)} %collective-permute-done.78), channel_id=1, source_target_pairs={{0,8},{4,12},{8,16},{12,20},{16,24},{20,28},{24,0},{28,4},{1,9},{5... | collective-permute-start | bytes 1572872 | tf_op jit(solution)/shard_map/ppermute | solution.py:60
  195.8 28.6 %collective-permute-start.81 = (bf16[128,2048]{1,0:T(8,128)(2,1)}, bf16[128,2048]{1,0:T(8,128)(2,1)}, u32[]{:S(2)}, u32[]{:S(2)}) collective-permute-start(bf16[128,2048]{1,0:T(8,128)(2,1)} %collective-permute-done.78), channel_id=1, source_target_pairs={{0,1},{1,0},{2,3},{3,2},{4,5},{5,4},{6,7},{7,6},{8,9},{9,8},{10,11... | collective-permute-start | bytes 1572872 | tf_op jit(solution)/shard_map/ppermute | solution.py:50
  205.4 15.5 %collective-permute-start.80 = (bf16[128,2048]{1,0:T(8,128)(2,1)}, bf16[128,2048]{1,0:T(8,128)(2,1)}, u32[]{:S(2)}, u32[]{:S(2)}) collective-permute-start(bf16[128,2048]{1,0:T(8,128)(2,1)} %collective-permute-done.79), channel_id=1, source_target_pairs={{0,8},{4,12},{8,16},{12,20},{16,24},{20,28},{24,0},{28,4},{1,9},{5... | collective-permute-start | bytes 1572872 | tf_op jit(solution)/shard_map/ppermute | solution.py:60
  205.4 20.9 %collective-permute-start.82 = (bf16[128,2048]{1,0:T(8,128)(2,1)}, bf16[128,2048]{1,0:T(8,128)(2,1)}, u32[]{:S(2)}, u32[]{:S(2)}) collective-permute-start(bf16[128,2048]{1,0:T(8,128)(2,1)} %collective-permute-done.79), channel_id=1, source_target_pairs={{0,1},{1,0},{2,3},{3,2},{4,5},{5,4},{6,7},{7,6},{8,9},{9,8},{10,11... | collective-permute-start | bytes 1572872 | tf_op jit(solution)/shard_map/ppermute | solution.py:50
  208.8 19.4 %collective-permute-start.21 = (bf16[64,2048]{1,0:T(8,128)(2,1)S(1)}, bf16[64,2048]{1,0:T(8,128)(2,1)S(1)}, u32[]{:S(2)}, u32[]{:S(2)}) collective-permute-start(bf16[64,2048]{1,0:T(8,128)(2,1)S(1)} %get-tuple-element.66), channel_id=1, source_target_pairs={{0,2},{1,3},{2,0},{3,1},{4,6},{5,7},{6,4},{7,5},{8,10},{9,11},{10,... | collective-permute-start | bytes 786440 | tf_op jit(solution)/shard_map/ppermute | solution.py:50
  224.4 22.1 %collective-permute-start.83 = (bf16[128,2048]{1,0:T(8,128)(2,1)}, bf16[128,2048]{1,0:T(8,128)(2,1)S(1)}, u32[]{:S(2)}, u32[]{:S(2)}) collective-permute-start(bf16[128,2048]{1,0:T(8,128)(2,1)} %collective-permute-done.80), channel_id=1, source_target_pairs={{0,1},{1,0},{2,3},{3,2},{4,5},{5,4},{6,7},{7,6},{8,9},{9,8},{10,11... | collective-permute-start | bytes 1572872 | tf_op jit(solution)/shard_map/ppermute | solution.py:50
  230.6 43.4 %collective-permute-start.22 = (bf16[128,2048]{1,0:T(8,128)(2,1)S(1)}, bf16[128,2048]{1,0:T(8,128)(2,1)S(1)}, u32[]{:S(2)}, u32[]{:S(2)}) collective-permute-start(bf16[128,2048]{1,0:T(8,128)(2,1)S(1)} %pad_maximum_fusion.4), channel_id=1, source_target_pairs={{0,1},{1,0},{2,3},{3,2},{4,5},{5,4},{6,7},{7,6},{8,9},{9,8},{10,11... | collective-permute-start | bytes 1572872 | tf_op jit(solution)/shard_map/ppermute | solution.py:50
  245.7 35.8 %collective-permute-start.13 = (bf16[128,2048]{1,0:T(8,128)(2,1)S(1)}, bf16[128,2048]{1,0:T(8,128)(2,1)}, u32[]{:S(2)}, u32[]{:S(2)}) collective-permute-start(bf16[128,2048]{1,0:T(8,128)(2,1)S(1)} %maximum_select_fusion.2), channel_id=1, source_target_pairs={{0,1},{1,0},{2,3},{3,2},{4,5},{5,4},{6,7},{7,6},{8,9},{9,8},{10,11... | collective-permute-start | bytes 1572872 | tf_op jit(solution)/shard_map/ppermute | solution.py:50
  267.8 97.3 %collective-permute-start.86 = (bf16[256,1408]{1,0:T(8,128)(2,1)}, bf16[256,1408]{1,0:T(8,128)(2,1)}, u32[]{:S(2)}, u32[]{:S(2)}) collective-permute-start(bf16[256,1408]{1,0:T(8,128)(2,1)} %fusion.5), channel_id=1, source_target_pairs={{0,4},{4,0},{8,12},{12,8},{16,20},{20,16},{24,28},{28,24},{1,5},{5... | collective-permute-start | bytes 2162696 | tf_op jit(solution)/shard_map/ppermute | solution.py:50
  271.6 97.1 %collective-permute-start.85 = (bf16[256,1408]{1,0:T(8,128)(2,1)}, bf16[256,1408]{1,0:T(8,128)(2,1)}, u32[]{:S(2)}, u32[]{:S(2)}) collective-permute-start(bf16[256,1408]{1,0:T(8,128)(2,1)} %fusion.4), channel_id=1, source_target_pairs={{0,4},{4,0},{8,12},{12,8},{16,20},{20,16},{24,28},{28,24},{1,5},{5... | collective-permute-start | bytes 2162696 | tf_op jit(solution)/shard_map/ppermute | solution.py:50
  274.0 110.1 %collective-permute-start.84 = (bf16[256,1408]{1,0:T(8,128)(2,1)}, bf16[256,1408]{1,0:T(8,128)(2,1)}, u32[]{:S(2)}, u32[]{:S(2)}) collective-permute-start(bf16[256,1408]{1,0:T(8,128)(2,1)} %fusion.3), channel_id=1, source_target_pairs={{0,4},{4,0},{8,12},{12,8},{16,20},{20,16},{24,28},{28,24},{1,5},{5... | collective-permute-start | bytes 2162696 | tf_op jit(solution)/shard_map/ppermute | solution.py:50
  281.5 36.4 %collective-permute-start.23 = (f32[8,512]{1,0:T(8,128)S(1)}, f32[8,512]{1,0:T(8,128)S(1)}, u32[]{:S(2)}, u32[]{:S(2)}) collective-permute-start(f32[8,512]{1,0:T(8,128)S(1)} %maximum_maximum_fusion), channel_id=1, source_target_pairs={{0,4},{4,0},{8,12},{12,8},{16,20},{20,16},{24,28},{28,24},{1,5},{5... | collective-permute-start | bytes 49160 | tf_op jit(solution)/shard_map/ppermute | solution.py:50
  363.2 16.8 %collective-permute-start.32 = (bf16[256,512]{1,0:T(8,128)(2,1)S(1)}, bf16[256,512]{1,0:T(8,128)(2,1)S(1)}, u32[]{:S(2)}, u32[]{:S(2)}) collective-permute-start(bf16[256,512]{1,0:T(8,128)(2,1)S(1)} %fusion.28), channel_id=1, source_target_pairs={{16,0},{20,4},{24,8},{28,12},{17,1},{21,5},{25,9},{29,13},{18,2},{... | collective-permute-start | bytes 786440 | tf_op jit(solution)/shard_map/ppermute | solution.py:55
  364.5 23.4 %collective-permute-start.60 = (bf16[256,512]{1,0:T(8,128)(2,1)S(1)}, bf16[256,512]{1,0:T(8,128)(2,1)S(1)}, u32[]{:S(2)}, u32[]{:S(2)}) collective-permute-start(bf16[256,512]{1,0:T(8,128)(2,1)S(1)} %collective-permute-done.59), channel_id=1, source_target_pairs={{0,8},{4,12},{8,16},{12,20},{16,24},{20,28},{24,0},{28,4},{1,9},{5... | collective-permute-start | bytes 786440 | tf_op jit(solution)/shard_map/ppermute | solution.py:60
  388.9 16.9 %collective-permute-start.61 = (bf16[256,512]{1,0:T(8,128)(2,1)}, bf16[256,512]{1,0:T(8,128)(2,1)}, u32[]{:S(2)}, u32[]{:S(2)}) collective-permute-start(bf16[256,512]{1,0:T(8,128)(2,1)} %fusion.16), channel_id=1, source_target_pairs={{0,4},{4,0},{8,12},{12,8},{16,20},{20,16},{24,28},{28,24},{1,5},{5... | collective-permute-start | bytes 786440 | tf_op jit(solution)/shard_map/ppermute | solution.py:50
  398.3 20.0 %collective-permute-start.47 = (bf16[256,1024]{1,0:T(8,128)(2,1)S(1)}, bf16[256,1024]{1,0:T(8,128)(2,1)}, u32[]{:S(2)}, u32[]{:S(2)}) collective-permute-start(bf16[256,1024]{1,0:T(8,128)(2,1)S(1)} %fusion.126), channel_id=1, source_target_pairs={{0,8},{4,12},{8,16},{12,20},{16,24},{20,28},{24,0},{28,4},{1,9},{5... | collective-permute-start | bytes 1572872 | tf_op jit(solution)/shard_map/ppermute | solution.py:60
  402.7 19.2 %collective-permute-start.34 = (bf16[128,2048]{1,0:T(8,128)(2,1)S(1)}, bf16[128,2048]{1,0:T(8,128)(2,1)S(1)}, u32[]{:S(2)}, u32[]{:S(2)}) collective-permute-start(bf16[128,2048]{1,0:T(8,128)(2,1)S(1)} %fusion.8), channel_id=1, source_target_pairs={{0,1},{1,0},{2,3},{3,2},{4,5},{5,4},{6,7},{7,6},{8,9},{9,8},{10,11... | collective-permute-start | bytes 1572872 | tf_op jit(solution)/shard_map/ppermute | solution.py:50
  417.6 22.2 %collective-permute-start.57 = (f32[24,2048]{1,0:T(8,128)S(1)}, f32[24,2048]{1,0:T(8,128)S(1)}, u32[]{:S(2)}, u32[]{:S(2)}) collective-permute-start(f32[24,2048]{1,0:T(8,128)S(1)} %add.495), channel_id=1, source_target_pairs={{0,16},{4,20},{8,24},{12,28},{16,0},{20,4},{24,8},{28,12},{1,17},{... | collective-permute-start | bytes 589832 | tf_op jit(solution)/shard_map/ppermute | solution.py:50
  422.8 17.1 %collective-permute-start.35 = (bf16[64,2048]{1,0:T(8,128)(2,1)S(1)}, bf16[64,2048]{1,0:T(8,128)(2,1)S(1)}, u32[]{:S(2)}, u32[]{:S(2)}) collective-permute-start(bf16[64,2048]{1,0:T(8,128)(2,1)S(1)} %slice.279), channel_id=1, source_target_pairs={{0,2},{1,3},{2,0},{3,1},{4,6},{5,7},{6,4},{7,5},{8,10},{9,11},{10,... | collective-permute-start | bytes 786440 | tf_op jit(solution)/shard_map/ppermute | solution.py:50
  424.4 42.5 %collective-permute-start.50 = (bf16[256,1024]{1,0:T(8,128)(2,1)}, bf16[256,1024]{1,0:T(8,128)(2,1)}, u32[]{:S(2)}, u32[]{:S(2)}) collective-permute-start(bf16[256,1024]{1,0:T(8,128)(2,1)} %collective-permute-done.47), channel_id=1, source_target_pairs={{0,8},{4,12},{8,16},{12,20},{16,24},{20,28},{24,0},{28,4},{1,9},{5... | collective-permute-start | bytes 1572872 | tf_op jit(solution)/shard_map/ppermute | solution.py:60
  466.8 15.5 %collective-permute-start.53 = (bf16[256,1024]{1,0:T(8,128)(2,1)}, bf16[256,1024]{1,0:T(8,128)(2,1)S(1)}, u32[]{:S(2)}, u32[]{:S(2)}) collective-permute-start(bf16[256,1024]{1,0:T(8,128)(2,1)} %collective-permute-done.50), channel_id=1, source_target_pairs={{0,8},{4,12},{8,16},{12,20},{16,24},{20,28},{24,0},{28,4},{1,9},{5... | collective-permute-start | bytes 1572872 | tf_op jit(solution)/shard_map/ppermute | solution.py:60
  468.2 16.9 %collective-permute-start.39 = (bf16[128,2048]{1,0:T(8,128)(2,1)S(1)}, bf16[128,2048]{1,0:T(8,128)(2,1)S(1)}, u32[]{:S(2)}, u32[]{:S(2)}) collective-permute-start(bf16[128,2048]{1,0:T(8,128)(2,1)S(1)} %maximum_select_fusion.3), channel_id=1, source_target_pairs={{0,1},{1,0},{2,3},{3,2},{4,5},{5,4},{6,7},{7,6},{8,9},{9,8},{10,11... | collective-permute-start | bytes 1572872 | tf_op jit(solution)/shard_map/ppermute | solution.py:50
  (180 other events, 1852.8 us)

commit v2 on v1

v2 whole, which is shorter than its diff:
```python
import functools

import functools

import jax
import jax.numpy as jnp
from jax import lax
from jax.experimental import pallas as pl
from jax.experimental.pallas import tpu as pltpu
from jax.sharding import PartitionSpec as P

D = 2048
DK = 256
DV = 512
RANK = 16
TAPS = 4
BLOCK = 64
EPSILON = 1e-05
HIGHEST = lax.Precision.HIGHEST
F32 = jnp.float32
BF16 = jnp.bfloat16
MIB = 1024 * 1024


def contract_rows(left, right):
    return lax.dot_general(left, right, (((0,), (0,)), ((), ())), preferred_element_type=F32)


def contract_cols(left, right):
    return lax.dot_general(left, right, (((1,), (1,)), ((), ())), preferred_element_type=F32)


def dot(left, right, precision=None):
    return lax.dot_general(
        left, right, (((1,), (0,)), ((), ())), precision=precision, preferred_element_type=F32
    )


def root_scale(v):
    return lax.rsqrt(jnp.mean(v * v, axis=-1, keepdims=True) + EPSILON)


def norm_backward(v, scale, gain, upstream):
    scaled_up = upstream * gain
    return scale * scaled_up - v * scale * scale * scale * jnp.mean(
        scaled_up * v, axis=-1, keepdims=True
    )


def flip(x, axis, bit):
    n = lax.axis_size(axis)
    return lax.ppermute(x, axis, [(i, i ^ bit) for i in range(n)])


def shift(x, axis, by):
    n = lax.axis_size(axis)
    return lax.ppermute(x, axis, [(i, i + by) for i in range(n) if 0 <= i + by < n])


def turn(x, by):
    n = lax.axis_size("seq")
    return lax.ppermute(x, "seq", [(i, (i + 2 * by) % n) for i in range(n)])


def after(x, *others):
    return lax.optimization_barrier((x, *others))[0]


def join(*xs):
    return lax.optimization_barrier(xs)


def total(x, steps, kind=F32):
    for axis, bit in steps:
        if kind != F32:
            x = lax.reduce_precision(x, 8, 7)
        x = x + flip(x.astype(kind), axis, bit).astype(F32)
    return x


def grids(n):
    return (
        lax.broadcasted_iota(jnp.int32, (n, n), 0),
        lax.broadcasted_iota(jnp.int32, (n, n), 1),
    )


def column(row, rows, cols, back):
    return jnp.sum(jnp.where(cols == rows - back, row, 0.0), axis=1, keepdims=True)


def tap_masks(start_row, rows, cols):
    here, one, two = (column(start_row, rows, cols, back) for back in range(3))
    first = 1.0 - here
    second = first * (1.0 - one)
    return here, (first, second, second * (1.0 - two))


def segments(start_row, start_col, rows, cols):
    seg_col = jnp.sum(jnp.where(cols <= rows, start_row, 0.0), axis=1, keepdims=True)
    seg_row = jnp.sum(jnp.where(rows <= cols, start_col, 0.0), axis=0, keepdims=True)
    return seg_col, seg_row, jnp.sum(start_row)


def block_middles(x):
    n = x.shape[0] // BLOCK
    mids = []
    for b in range(n):
        last = x[(b + 1) * BLOCK - 1 : (b + 1) * BLOCK]
        before = x[b * BLOCK - 1 : b * BLOCK] if b else jnp.zeros_like(last)
        mids.append(0.5 * (before + last))
    return mids


def spread(mids):
    return jnp.concatenate(
        [jnp.broadcast_to(mid, (BLOCK, mid.shape[1])) for mid in mids], axis=0
    )


def state_kernel(
    place, pre_q, pre_k, pre_v, edge, taps, start_row, low_rank, lowrank_up, bias,
    u_out, v_out, x_out, logit_out, state_out, ext,
):
    n = pre_q.shape[0]
    rows, cols = grids(n)
    sr = start_row[...]
    start_col, masks = tap_masks(sr, rows, cols)
    seg_col, _, seg_last = segments(sr, start_col, rows, cols)
    ext[0:8, :] = edge[...].astype(F32)
    ext[8:, 0:DK] = pre_q[...].astype(F32)
    ext[8:, DK : 2 * DK] = pre_k[...].astype(F32)
    ext[8:, 2 * DK :] = pre_v[...].astype(F32)
    for part in range(4):
        lanes = slice(part * DK, (part + 1) * DK)
        u = ext[8 : 8 + n, lanes] * taps[3:4, lanes]
        for back in range(1, TAPS):
            u = u + ext[8 - back : 8 - back + n, lanes] * taps[3 - back : 4 - back, lanes] * masks[
                back - 1
            ]
        u_out[:, lanes] = u
        if part >= 2:
            v_out[:, (part - 2) * DK : (part - 1) * DK] = (u * jax.nn.sigmoid(u)).astype(BF16)
    logit = dot(low_rank[...], lowrank_up[...]) + bias[...]
    logit_out[...] = logit
    decays = (jnp.minimum(logit, 0.0) - jnp.log1p(jnp.exp(-jnp.abs(logit)))) * (1.0 / 16.0)
    x = dot((cols <= rows).astype(F32), decays, HIGHEST)
    x_out[...] = x
    u = u_out[:, DK : 2 * DK]
    keys = u * jax.nn.sigmoid(u)
    tail = (seg_col == seg_last).astype(F32)
    final = x[n - 1 : n]
    closing = (keys * jnp.exp(final - x) * tail).astype(BF16)
    put_decay(
        state_out,
        contract_rows(closing, v_out[...]).astype(BF16),
        jnp.exp(final) * (seg_last == 0.0).astype(F32),
    )


def local_scores(q, k, x):
    n = x.shape[0] // BLOCK
    mids = block_middles(x)
    mid = spread(mids)
    grow, shrink = jnp.exp(x - mid), jnp.exp(mid - x)
    rising, falling = q * grow, (k * shrink).astype(BF16)
    lifted, scales = [], []
    for j in range(n):
        pieces = [jnp.exp(mids[i] - mids[j]) for i in range(j, n)]
        scale = spread(pieces)
        scales.append(scale)
        lifted.append((rising[j * BLOCK :] * scale).astype(BF16))
    return grow, shrink, lifted, scales, falling


def output_kernel(
    place, u_qk, v, x_in, start_row, state_in, outgate, gain, weight,
    gated_out, mixed_out, scores_out, sent_out, kept_out,
):
    n = x_in.shape[0]
    blocks = n // BLOCK
    rows, cols = grids(n)
    sr = start_row[...]
    start_col = column(sr, rows, cols, 0)
    seg_col, seg_row, _ = segments(sr, start_col, rows, cols)
    allowed = (cols <= rows) & (seg_col == seg_row)
    alive = (seg_col == 0.0).astype(F32)
    x = x_in[...]
    uq = u_qk[:, 0:DK]
    uk = u_qk[:, DK : 2 * DK]
    q = uq * jax.nn.sigmoid(uq) * DK**-0.5
    k = uk * jax.nn.sigmoid(uk)
    _, _, lifted, _, falling = local_scores(q, k, x)
    scores_out[...] = jnp.zeros_like(scores_out)
    for j in range(blocks):
        lo, hi = j * BLOCK, (j + 1) * BLOCK
        s = contract_cols(lifted[j], falling[lo:hi])
        scores_out[lo:, lo:hi] = jnp.where(allowed[lo:, lo:hi], s, 0.0).astype(BF16)
    carried = (q * jnp.exp(x) * alive).astype(BF16)
    out = dot(scores_out[...], v[...]) + dot(carried, state_in[...])
    mixed_out[...] = out
    og = outgate[...]
    gated = (out * root_scale(out) * gain[...] * (og * jax.nn.sigmoid(og))).astype(BF16)
    m = place[0]
    for b in range(blocks):
        at = pl.multiple_of((m ^ b) * BLOCK, BLOCK)
        gated_out[pl.ds(at, BLOCK), :] = gated[b * BLOCK : (b + 1) * BLOCK]
    half = n // 2
    for part in range(4):
        lanes = slice(part * DV, (part + 1) * DV)
        branch = contract_cols(gated_out[...], weight[lanes, :])
        kept_out[:, lanes] = branch[0:half]
        sent_out[:, lanes] = branch[half:].astype(BF16)


def gate_back_kernel(
    place, branch_0, branch_1, branch_2, branch_3, weight, mixed, outgate, gain, u_in, x_in,
    start_row, d_outgate_out, d_mixed_out, gain_out, direct_out, cut_out, order,
):
    n = x_in.shape[0]
    blocks = n // BLOCK
    m = place[0]
    for p, piece in enumerate((branch_0, branch_1, branch_2, branch_3)):
        at = pl.multiple_of((m ^ p) * BLOCK, BLOCK)
        order[pl.ds(at, BLOCK), :] = piece[...]
        cut_out[p * BLOCK : (p + 1) * BLOCK, :] = piece[:, pair_lanes(place, cut_out)]
    up = dot(order[...], weight[...])
    og = outgate[...]
    sig = jax.nn.sigmoid(og)
    out = mixed[...]
    scale = root_scale(out)
    g = gain[...]
    d_outgate = (up * (out * scale * g) * sig * (1.0 + og * (1.0 - sig))).astype(BF16)
    for b in range(blocks):
        at = pl.multiple_of((m ^ b) * BLOCK, BLOCK)
        d_outgate_out[pl.ds(at, BLOCK), :] = d_outgate[b * BLOCK : (b + 1) * BLOCK]
    d_norm = up * (og * sig)
    gain_out[...] = jnp.sum(d_norm * out * scale, axis=0, keepdims=True)
    d_mixed = norm_backward(out, scale, g, d_norm).astype(BF16)
    d_mixed_out[...] = d_mixed
    rows, cols = grids(n)
    sr = start_row[...]
    seg_col = jnp.sum(jnp.where(cols <= rows, sr, 0.0), axis=1, keepdims=True)
    alive = (seg_col == 0.0).astype(F32)
    uq = u_in[:, 0:DK]
    x = x_in[...]
    carried = (uq * jax.nn.sigmoid(uq) * DK**-0.5 * jnp.exp(x) * alive).astype(BF16)
    put_decay(
        direct_out,
        contract_rows(carried, d_mixed).astype(BF16),
        jnp.exp(x[n - 1 : n]) * (jnp.sum(sr) == 0.0).astype(F32),
    )


def mixer_back_kernel(
    place, d_mixed, state_in, later, u_in, v, x_in, scores, pre_q, pre_k, pre_v, edge, taps,
    logit, start_row, low_rank, lowrank_up,
    d_pre_out, last_rows_out, pack_out, d_low_out, back_rows_out,
    ext, du_ext, small, dx_buf,
):
    n = x_in.shape[0]
    blocks = n // BLOCK
    m = place[0]
    rows, cols = grids(n)
    sr = start_row[...]
    start_col, masks = tap_masks(sr, rows, cols)
    seg_col, seg_row, seg_last = segments(sr, start_col, rows, cols)
    allowed = (cols <= rows) & (seg_col == seg_row)
    alive = (seg_col == 0.0).astype(F32)
    tail = (seg_col == seg_last).astype(F32)
    x = x_in[...]
    uq = u_in[:, 0:DK]
    uk = u_in[:, DK : 2 * DK]
    sq, sk = jax.nn.sigmoid(uq), jax.nn.sigmoid(uk)
    q = uq * sq * DK**-0.5
    k = uk * sk
    grow, shrink, lifted, scales, falling = local_scores(q, k, x)
    dm = d_mixed[...]
    later_b = later[...]
    later_f = later_b.astype(F32)
    state_f = state_in[...].astype(F32)
    d_scores = jnp.where(allowed, contract_cols(dm, v[...]), 0.0).astype(BF16)
    final = x[n - 1 : n]
    leaving = jnp.exp(final - x) * tail
    closing = (k * leaving).astype(BF16)
    d_closing = contract_cols(v[...], later_b)
    entering = jnp.exp(x) * alive
    d_carried = contract_cols(dm, state_in[...])
    dq = d_carried * entering
    dk = d_closing * leaving
    closed = d_closing * closing.astype(F32)
    dx_buf[...] = d_carried * (q * entering) - closed
    through = jnp.sum(later_f * state_f, axis=1, keepdims=True)
    through_row = jnp.sum(jnp.where(rows == cols, through, 0.0), axis=0, keepdims=True)
    at_last = jnp.sum(closed, axis=0, keepdims=True) + through_row * jnp.exp(final) * (
        seg_last == 0.0
    ).astype(F32)
    dx_buf[n - 1 : n, :] = dx_buf[n - 1 : n, :] + at_last
    dq_parts = [dq[b * BLOCK : (b + 1) * BLOCK] for b in range(blocks)]
    dk_parts = []
    for j in range(blocks):
        lo, hi = j * BLOCK, (j + 1) * BLOCK
        ds = d_scores[lo:, lo:hi]
        d_lift = dot(ds, falling[lo:hi])
        d_fall = contract_rows(ds, lifted[j])
        dx_buf[lo:, :] = dx_buf[lo:, :] + d_lift * lifted[j].astype(F32)
        dx_buf[lo:hi, :] = dx_buf[lo:hi, :] - d_fall * falling[lo:hi].astype(F32)
        d_rise = d_lift * scales[j] * grow[lo:]
        for b in range(j, blocks):
            dq_parts[b] = dq_parts[b] + d_rise[(b - j) * BLOCK : (b - j + 1) * BLOCK]
        dk_parts.append(dk[lo:hi] + d_fall * shrink[lo:hi])
    dq = jnp.concatenate(dq_parts, axis=0)
    dk = jnp.concatenate(dk_parts, axis=0)
    d_decays = dot((cols >= rows).astype(F32), dx_buf[...], HIGHEST)
    d_logit = (d_decays * jax.nn.sigmoid(-logit[...]) * (1.0 / 16.0)).astype(BF16)
    pack_out[...] = jnp.zeros_like(pack_out)
    pack_out[4:5, 0:DK] = jnp.sum(d_logit.astype(F32), axis=0, keepdims=True)
    d_up = contract_rows(low_rank[...], d_logit)
    per = pack_out.shape[1] // DK
    for row in range(RANK):
        at = (row % per) * DK
        pack_out[2 + row // per : 3 + row // per, at : at + DK] = d_up[row : row + 1]
    d_low_out[...] = contract_cols(lowrank_up[...], d_logit)

    ext[0:8, :] = edge[...].astype(F32)
    ext[8:, 0:DK] = pre_q[...].astype(F32)
    ext[8:, DK : 2 * DK] = pre_k[...].astype(F32)
    ext[8:, 2 * DK :] = pre_v[...].astype(F32)
    du_ext[n:, :] = jnp.zeros((8, du_ext.shape[1]), F32)
    du_ext[0:n, 0:DK] = dq * (DK**-0.5) * (sq * (1.0 + uq * (1.0 - sq)))
    du_ext[0:n, DK : 2 * DK] = dk * (sk * (1.0 + uk * (1.0 - sk)))
    dv = contract_rows(scores[...], dm) + dot(closing, later_b)
    for half in range(2):
        uv = u_in[:, (2 + half) * DK : (3 + half) * DK]
        sv = jax.nn.sigmoid(uv)
        du_ext[0:n, (2 + half) * DK : (3 + half) * DK] = dv[:, half * DK : (half + 1) * DK] * (
            sv * (1.0 + uv * (1.0 - sv))
        )
    ahead = []
    for back in range(1, TAPS):
        mask_row = jnp.sum(jnp.where(rows == cols, masks[back - 1], 0.0), axis=0, keepdims=True)
        ahead.append(column(mask_row, rows, cols, -back))
    for part in range(4):
        lanes = slice(part * DK, (part + 1) * DK)
        du = du_ext[0:n, lanes]
        d_pre = du * taps[3:4, lanes]
        back_rows = jnp.zeros((8, DK), F32)
        wide = du_ext.shape[1]
        pack_out[1:2, wide + part * DK : wide + (part + 1) * DK] = jnp.sum(
            du * ext[8 : 8 + n, lanes], axis=0, keepdims=True
        )
        for back in range(1, TAPS):
            weight = taps[3 - back : 4 - back, lanes]
            d_pre = d_pre + du_ext[back : back + n, lanes] * weight * ahead[back - 1]
            masked = du * masks[back - 1]
            row, at = (3 - back) // 2, (3 - back) % 2 * wide + part * DK
            pack_out[row : row + 1, at : at + DK] = jnp.sum(
                masked * ext[8 - back : 8 - back + n, lanes], axis=0, keepdims=True
            )
            small[0:8, :] = jnp.zeros((8, DK), F32)
            small[8:16, :] = masked[0:8]
            back_rows = back_rows + small[back : back + 8, :] * weight
        back_rows_out[:, lanes] = back_rows
        last_rows_out[:, lanes] = d_pre[n - 8 :]
        rounded = d_pre.astype(BF16)
        for b in range(blocks):
            at = pl.multiple_of((m ^ b) * BLOCK, BLOCK)
            d_pre_out[pl.ds(at, BLOCK), lanes] = rounded[b * BLOCK : (b + 1) * BLOCK]


def whole_spec():
    return pl.BlockSpec(memory_space=pltpu.VMEM)


def call(body, place, args, outs, scratch=(), vmem=6, micros=1.0):
    return pl.pallas_call(
        body,
        out_shape=[jax.ShapeDtypeStruct(shape, kind) for shape, kind in outs],
        in_specs=[pl.BlockSpec(memory_space=pltpu.SMEM)] + [whole_spec() for _ in args],
        out_specs=[whole_spec() for _ in outs],
        scratch_shapes=[pltpu.VMEM(shape, kind) for shape, kind in scratch],
        compiler_params=pltpu.CompilerParams(vmem_limit_bytes=vmem * MIB),
        cost_estimate=pl.CostEstimate(
            flops=int(micros * 1e9), bytes_accessed=int(micros * 3e6), transcendentals=0
        ),
    )(place, *args)


def spans(width, tile):
    return [slice(at, min(at + tile, width)) for at in range(0, width, tile)]


def fold_kernel(place, kept, got, near_out, far_out):
    quarter = near_out.shape[0]
    near_out[...] = kept[0:quarter] + got[0:quarter].astype(F32)
    far_out[...] = (kept[quarter:] + got[quarter:].astype(F32)).astype(BF16)


def hidden_kernel(place, kept, got, own_input, gain, hidden_out, ffn_out):
    hidden = own_input[...].astype(F32) + (kept[...] + got[...].astype(F32))
    hidden_out[...] = hidden
    ffn_out[...] = (hidden * root_scale(hidden) * gain[...]).astype(BF16)


def loss_kernel(
    weight, place, kept, got, hidden, teacher, cotangent, valid, count,
    output_out, d_out_out, d_ffn_out, squared_out,
):
    output = hidden[...] + (kept[...] + got[...].astype(F32))
    output_out[...] = output.astype(BF16)
    mismatch = output - teacher[...].astype(F32)
    keep = valid[...]
    squares = jnp.sum(keep * mismatch * mismatch, axis=0, keepdims=True)
    squared_out[...] = jnp.sum(squares, axis=1, keepdims=True)
    d_out = cotangent[...].astype(F32) + keep * (2.0 * weight) * mismatch / (count[...] * D)
    d_out_out[...] = d_out
    d_ffn_out[...] = d_out.astype(BF16)


def hidden_back_kernel(
    place, kept, got, hidden, d_out, gain, d_hidden_out, d_branch_out, gain_out
):
    d_norm = kept[...] + got[...].astype(F32)
    h = hidden[...]
    scale = root_scale(h)
    gain_out[...] = jnp.sum(d_norm * h * scale, axis=0, keepdims=True)
    d_hidden = d_out[...] + norm_backward(h, scale, gain[...], d_norm)
    d_hidden_out[...] = d_hidden
    d_branch_out[...] = d_hidden.astype(BF16)


def input_back_kernel(
    place, kept, got, own_input, d_hidden, gain, d_low, down_turned, grad_out, gain_out
):
    d_norm = (kept[...] + got[...].astype(F32)) + contract_rows(d_low[...], down_turned[...])
    v = own_input[...].astype(F32)
    scale = root_scale(v)
    gain_out[...] = jnp.sum(d_norm * v * scale, axis=0, keepdims=True)
    grad_out[...] = (d_hidden[...] + norm_backward(v, scale, gain[...], d_norm)).astype(BF16)


def carry_kernel(first, last, place, got, *refs):
    refs = list(refs)
    window = None if last else refs.pop(0)
    found = None if first else refs.pop(0)
    n = DK
    rows, cols = grids(n)

    def as_column(row):
        return jnp.sum(jnp.where(rows == cols, row, 0.0), axis=1, keepdims=True)

    def decay_of(ref):
        both = ref[n : n + 1, :].astype(F32)
        return both[:, 0:n] + both[:, n : 2 * n]

    arrived = got[0:n, :].astype(F32)
    if first:
        merged = arrived
        found_decay = decay_of(got)
    else:
        own = decay_of(found)
        merged = as_column(own) * arrived + found[0:n, :].astype(F32)
        found_decay = own * decay_of(got)
    if last:
        refs.pop(0)[...] = merged.astype(BF16)
        return
    window_decay = decay_of(window)
    state = as_column(window_decay) * arrived + window[0:n, :].astype(F32)
    put_decay(refs.pop(0), state.astype(BF16), window_decay * decay_of(got))
    put_decay(refs.pop(0), merged.astype(BF16), found_decay)


def put_decay(ref, state, decay):
    n = DK
    ref[0:n, :] = state
    high = decay.astype(BF16)
    low = (decay - high.astype(F32)).astype(BF16)
    row = jnp.concatenate([high, low], axis=1)
    ref[n:, :] = jnp.broadcast_to(row, (ref.shape[0] - n, 2 * n))


def rows_kernel(count, widths, place, *refs):
    lefts, rights = refs[:count], refs[count : count + len(widths)]
    sent, kept = refs[count + len(widths) :]
    half = sent.shape[0]
    for lanes in spans(kept.shape[1], 1024):
        acc = None
        for (left, at, width), right in zip(widths, rights):
            term = contract_cols(lefts[left][:, at : at + width], right[lanes, :])
            acc = term if acc is None else acc + term
        kept[:, lanes] = acc[0:half]
        sent[:, lanes] = acc[half:].astype(BF16)


def rows_times(lefts, pairs):
    half = lefts[0].shape[0] // 2
    widths = [pair[:3] for pair in pairs]
    return (
        functools.partial(rows_kernel, len(lefts), widths),
        [*lefts, *(pair[3] for pair in pairs)],
        [((half, D), BF16), ((half, D), F32)],
    )


def stack(pieces, buf):
    at = 0
    for piece in pieces:
        buf[at : at + piece.shape[0], :] = piece[...]
        at += piece.shape[0]


def pair_lanes(place, cut_out):
    pair = cut_out.shape[1]
    return pl.ds(pl.multiple_of(place[1] * pair, pair), pair)


def gate_kernel(count, place, *refs):
    pieces, (gate_w, up_w, act_out, gate_out, up_out, cut_out, buf) = refs[:count], refs[count:]
    stack(pieces, buf)
    cut_out[...] = buf[:, pair_lanes(place, cut_out)]
    for lanes in spans(act_out.shape[1], 256):
        gate, up = dot(buf[...], gate_w[:, lanes]), dot(buf[...], up_w[:, lanes])
        sig = jax.nn.sigmoid(gate)
        swish = gate * sig
        act_out[:, lanes] = (swish * up).astype(BF16)
        gate_out[:, lanes] = (up * sig * (1.0 + gate * (1.0 - sig))).astype(gate_out.dtype)
        up_out[:, lanes] = swish.astype(up_out.dtype)


def gate_up(pair, pieces, gate_weight, up_weight, kind):
    length = sum(p.shape[0] for p in pieces)
    width = gate_weight.shape[1]
    return (
        functools.partial(gate_kernel, len(pieces)),
        [*pieces, gate_weight, up_weight],
        [
            ((length, width), BF16),
            ((length, width), kind),
            ((length, width), kind),
            ((length, pair), BF16),
        ],
        [((length, D), BF16)],
    )


def gate_back_kernel_rows(count, place, *refs):
    pieces, (down_w, gate_in, up_in, d_gate_out, d_up_out, cut_out, buf) = refs[:count], refs[count:]
    stack(pieces, buf)
    cut_out[...] = buf[:, pair_lanes(place, cut_out)]
    for lanes in spans(d_gate_out.shape[1], 256):
        d_act = dot(buf[...], down_w[:, lanes])
        d_gate_out[:, lanes] = (d_act * gate_in[:, lanes].astype(F32)).astype(BF16)
        d_up_out[:, lanes] = (d_act * up_in[:, lanes].astype(F32)).astype(BF16)


def gate_back_rows(pair, pieces, down_weight, gate_in, up_in):
    length, width = gate_in.shape
    return (
        functools.partial(gate_back_kernel_rows, len(pieces)),
        [*pieces, down_weight, gate_in, up_in],
        [((length, width), BF16), ((length, width), BF16), ((length, pair), BF16)],
        [((length, D), BF16)],
    )


def weight_kernel(kind, blocks, place, *refs):
    sent, kept, left_buf, res = refs[-4:]
    rights, lefts = refs[-4 - blocks : -4], refs[: -4 - blocks]
    m, side = place[0], place[2]
    share = kept.shape[0]
    length = rights[0].shape[0]
    quarter = length // 4
    if kind == "cuts":
        stack(lefts, left_buf)
    else:
        if kind == "natural":
            lanes = pair_lanes(place, left_buf)
            for p in range(4):
                rows = pl.ds(pl.multiple_of((m ^ p) * quarter, quarter), quarter)
                left_buf[p * quarter : (p + 1) * quarter, :] = lefts[0][rows, lanes]
        else:
            left_buf[0:length, :] = lefts[0][...]
        for block in range(1, blocks):
            for p in range(4):
                at = block * length + p * quarter
                piece = lefts[1 + p][(block - 1) * quarter : block * quarter, :]
                left_buf[at : at + quarter, :] = piece
    for cols in spans(kept.shape[1], 256):
        acc = None
        for block, right in enumerate(rights):
            term = contract_rows(
                left_buf[block * length : (block + 1) * length, :], right[:, cols]
            )
            acc = term if acc is None else acc + term
        width = cols.stop - cols.start
        res[:, 0:width] = acc
        sent[:, cols] = res[
            pl.ds(pl.multiple_of((1 - side) * share, share), share), 0:width
        ].astype(BF16)
        kept[:, cols] = res[pl.ds(pl.multiple_of(side * share, share), share), 0:width]


def weight_args(kind, share, lefts, rights):
    tokens, width = rights[0].shape[0] * len(rights), rights[0].shape[1]
    return (
        functools.partial(weight_kernel, kind, len(rights)),
        [*lefts, *rights],
        [((share, width), BF16), ((share, width), F32)],
        [((tokens, 2 * share), BF16), ((2 * share, 256), F32)],
    )


def natural_kernel(place, piece_0, piece_1, piece_2, piece_3, out):
    quarter = piece_0.shape[0]
    for p, piece in enumerate((piece_0, piece_1, piece_2, piece_3)):
        at = pl.multiple_of((place[0] ^ p) * quarter, quarter)
        out[pl.ds(at, quarter), :] = piece[...].astype(F32)


def settle_kernel(place, kept, got, out_0, out_1, out_2):
    at = 0
    for out in (out_0, out_1, out_2):
        width = out.shape[1]
        out[...] = kept[:, at : at + width] + got[:, at : at + width].astype(F32)
        at += width


def low_kernel(place, d_low, normed, pack, out):
    out[0:RANK, :] = dot(d_low[...], normed[...])
    out[RANK:, :] = pack[...]


def unpack_kernel(share, place, summed, query_out, key_out, value_out, up_out, bias_out, down_out):
    for row in range(TAPS):
        at = (row % 2) * (2 * DK + DV)
        line = summed[RANK + row // 2 : RANK + 1 + row // 2, :]
        query_out[row : row + 1, :] = line[:, at : at + DK]
        key_out[row : row + 1, :] = line[:, at + DK : at + 2 * DK]
        value_out[row : row + 1, :] = line[:, at + 2 * DK : at + 2 * DK + DV]
    per = D // DK
    for row in range(RANK):
        at = (row % per) * DK
        up_out[row : row + 1, :] = summed[RANK + 2 + row // per : RANK + 3 + row // per, at : at + DK]
    bias_out[...] = summed[RANK + 4 : RANK + 5, 0:DK]
    pair = 2 * share
    both = summed[0:RANK, pl.ds(pl.multiple_of(place[1] * pair, pair), pair)]
    down_out[...] = jnp.where(place[2] == 0, both[:, 0:share], both[:, share:])


COST = {
    "state_kernel": 2.3,
    "output_kernel": 2.0,
    "gate_back_kernel": 2.0,
    "mixer_back_kernel": 4.5,
    "rows_kernel": 2.8,
    "gate_kernel": 4.0,
    "gate_back_kernel_rows": 2.4,
    "weight_kernel": 2.4,
    "natural_kernel": 2.0,
}


def on_device(
    block_input,
    first_gain,
    query_weight,
    key_weight,
    value_weight,
    query_conv,
    key_conv,
    value_conv,
    lowrank_down,
    lowrank_up,
    decay_bias,
    outgate_weight,
    outnorm_gain,
    output_weight,
    second_gain,
    gate_weight,
    up_weight,
    down_weight,
    starts,
    valid_mask,
    cotangent,
    teacher,
):
    length = block_input.shape[0]
    quarter, half = length // 4, length // 2
    places = lax.axis_size("seq")
    turns = places // 2
    share = D // places
    pair = 2 * share
    hidden_units = gate_weight.shape[1]
    channels = 2 * DK + DV
    seq, head = lax.axis_index("seq"), lax.axis_index("head")
    mine = (head % 2) * 2 + head // 2
    zone, side = seq // 2, seq % 2
    place = jnp.stack([mine, zone, side]).astype(jnp.int32)
    loss_weight = float(length * places * D // 8)
    row_shape = (quarter, D)
    window_shape = (DK + 16, 2 * DK)


    waiting = []

    def run(body, args, outs, scratch=(), vmem=6):
        micros = COST.get(getattr(body, "func", body).__name__, 1.0)
        gate = after(place, *waiting) if waiting else place
        made = call(body, gate, args, outs, scratch, vmem, micros)
        waiting[:] = [made[-1]]
        return made

    def hold(*xs):
        waiting.extend(xs)
        return xs[0] if len(xs) == 1 else xs

    def ready(x):
        return after(x, *waiting)

    def own(x):
        return lax.dynamic_slice_in_dim(x, mine * quarter, quarter, 0)

    def fold(sent, kept):
        got = flip(sent, "head", 1)
        return run(fold_kernel, [kept, got], [(row_shape, F32), (row_shape, BF16)])

    def cut(own_rows, by):
        target = lax.rem(zone + by, turns)
        return lax.dynamic_slice_in_dim(own_rows, target * pair, pair, 1)

    def quarters(own_rows, side_rows):
        return [own_rows, side_rows, flip(own_rows, "head", 1), flip(side_rows, "head", 1)]

    start_row = starts.astype(F32).reshape(1, length)
    input_float = block_input.astype(F32)
    normed = (input_float * root_scale(input_float) * first_gain).astype(BF16)
    pre_k = dot(normed, key_weight).astype(BF16)
    pre_v = dot(normed, value_weight).astype(BF16)
    pre_q = dot(normed, query_weight).astype(BF16)
    last_start, before_last = start_row[0, length - 1], start_row[0, length - 2]
    keep_one = 1.0 - last_start
    tail_keep = jnp.concatenate(
        [jnp.zeros((5,), F32), jnp.stack([keep_one * (1.0 - before_last), keep_one, jnp.ones((), F32)])]
    )
    tails = jnp.concatenate([pre_q[length - 8 :], pre_k[length - 8 :], pre_v[length - 8 :]], axis=1)
    edge = shift(tails * tail_keep[:, None].astype(BF16), "seq", 1)
    taps = jnp.concatenate([query_conv, key_conv, value_conv], axis=1)
    low_rank = dot(normed, lowrank_down).astype(BF16)
    u, v, x, logit, window = run(
        state_kernel,
        [pre_q, pre_k, pre_v, edge, taps, start_row, low_rank, lowrank_up, decay_bias.reshape(1, DK)],
        [
            ((length, channels), F32),
            ((length, DV), BF16),
            ((length, DK), F32),
            ((length, DK), F32),
            (window_shape, BF16),
        ],
        [((length + 8, channels), F32)],
    )

    def carry(window, sign, beside):
        found = None
        step, at = 1, 0
        while step < places:
            last = 2 * step >= places
            got = shift(window, "seq", sign * step)
            got, *_ = beside(at, step, got, window)
            args = [got] + ([] if last else [window]) + ([] if found is None else [found])
            outs = [((DK, DV), BF16)] if last else [(window_shape, BF16), (window_shape, BF16)]
            made = run(functools.partial(carry_kernel, found is None, last), args, outs)
            if not last:
                window, found = made
            step, at = 2 * step, at + 1
        return made[0]

    def finish(blocks):
        while len(blocks) < turns - 1:
            blocks.append(turn(blocks[-1], 1))
        return blocks

    valid_float = valid_mask.astype(F32)
    normed_own = own(normed)
    counts, normed_got, outgates = [jnp.full((8, 128), jnp.sum(valid_float), F32)], [], []

    def with_forward(at, step, got, window):
        count = after(counts[-1], window)
        beside = [count + flip(count, "seq", step)]
        if at + 1 < turns:
            beside.append(turn(after(cut(normed_own, at + 1), window), at + 1))
        if at == 0:
            beside.append(dot(after(normed, window), outgate_weight))
        got, *beside = join(got, *beside)
        counts.append(beside[0])
        normed_got.extend(beside[1:2])
        outgates.extend(beside[2:])
        return (got,)

    state_in = carry(window, 1, with_forward)
    outgate, valid_count = outgates[0], counts[-1][0:1, 0:1]
    for by in range(len(normed_got) + 1, turns):
        normed_got.append(turn(cut(normed_own, by), by))
    gain_row = outnorm_gain.reshape(1, DV)
    second_row = second_gain.reshape(1, D)
    input_own = own(block_input)
    valid_own = own(valid_float)[:, None]
    teacher_own, cotangent_own = own(teacher), own(cotangent)
    gated, mixed, scores, sent, kept = run(
        output_kernel,
        [u, v, x, start_row, state_in, outgate, gain_row, output_weight],
        [
            ((length, DV), BF16),
            ((length, DV), F32),
            ((length, length), BF16),
            ((half, D), BF16),
            ((half, D), F32),
        ],
    )

    near, far = fold(sent, kept)
    far, turned = join(far, gated)
    far, gated_1 = join(flip(far, "head", 2), turn(turned, 1))
    hidden, ffn_own = run(
        hidden_kernel, [near, far, input_own, second_row], [(row_shape, F32), (row_shape, BF16)]
    )
    ffn_side, ffn_1 = join(flip(ffn_own, "head", 2), turn(ffn_own, 1))
    ffn_in = quarters(ffn_own, ffn_side)
    activated, gate_in, up_in, ffn_cut = run(*gate_up(pair, ffn_in, gate_weight, up_weight, BF16))
    sent, kept = run(*rows_times([activated], [(0, 0, hidden_units, down_weight)]))
    near, far = fold(sent, kept)
    far, turned = join(far, ffn_1)
    far, ffn_2 = join(flip(far, "head", 2), turn(turned, 1))
    output_own, d_out, d_ffn_own, squared = run(
        functools.partial(loss_kernel, loss_weight),
        [near, far, hidden, teacher_own, cotangent_own, valid_own, valid_count],
        [(row_shape, BF16), (row_shape, F32), (row_shape, BF16), ((1, 1), F32)],
    )
    d_ffn_own, turned, turned_too = join(d_ffn_own, ffn_2, gated_1)
    d_ffn_side, ffn_3, gated_2 = join(
        flip(d_ffn_own, "head", 2), turn(turned, 1), turn(turned_too, 1)
    )
    d_ffn = quarters(d_ffn_own, d_ffn_side)
    d_gate, d_up, d_ffn_cut = run(*gate_back_rows(pair, d_ffn, down_weight, gate_in, up_in))
    sent, kept = run(
        *rows_times(
            [d_gate, d_up],
            [(0, 0, hidden_units, gate_weight), (1, 0, hidden_units, up_weight)],
        )
    )
    near, far = fold(sent, kept)
    far, turned = join(far, d_ffn_own)
    far, d_1 = join(flip(far, "head", 2), turn(turned, 1))
    d_hidden, d_branch_own, second_part = run(
        hidden_back_kernel,
        [near, far, hidden, d_out, second_row],
        [(row_shape, F32), (row_shape, BF16), ((1, D), F32)],
    )
    d_branch_own, turned, turned_too = join(d_branch_own, d_1, gated_2)
    d_branch_side, d_2, gated_3 = join(
        flip(d_branch_own, "head", 2), turn(turned, 1), turn(turned_too, 1)
    )
    d_branch = quarters(d_branch_own, d_branch_side)

    d_outgate, d_mixed, outnorm_part, direct, branch_cut = run(
        gate_back_kernel,
        [*d_branch, output_weight, mixed, outgate, gain_row, u, x, start_row],
        [
            ((length, DV), BF16),
            ((length, DV), BF16),
            ((1, DV), F32),
            (window_shape, BF16),
            ((length, pair), BF16),
        ],
        [((length, D), BF16)],
    )

    made, grads = [], []

    def far_forward(own_rows, side_rows):
        made.append(run(*gate_up(pair, quarters(own_rows, side_rows), gate_weight, up_weight, BF16)))

    def far_back(own_rows, side_rows):
        part = made[len(grads)]
        pieces = quarters(own_rows, side_rows)
        grads.append(run(*gate_back_rows(pair, pieces, down_weight, part[1], part[2])))

    ffn_turns, d_turns = finish([ffn_1, ffn_2, ffn_3]), [d_1, d_2]
    gated_turns = finish([gated_1, gated_2, gated_3])
    ffn_sides, d_sides, outgate_turns, branch_got, sums = [], [], [], [], {}

    def weigh(name, lefts, rights):
        sums[name] = run(*weight_args("cuts", share, lefts, rights), vmem=8)

    def with_back(at, step, got, window):
        if at == 0:
            ffn_sides.extend(flip(after(r, window), "head", 2) for r in (ffn_1, ffn_2))
            d_turns.append(turn(after(d_2, window), 1))
            hold(*ffn_sides, d_turns[2])
        elif at == 1:
            ffn_sides.append(flip(after(ffn_3, window), "head", 2))
            d_sides.append(flip(after(d_1, window), "head", 2))
            outgate_turns.append(turn(after(d_outgate, window), 1))
            far_forward(ffn_1, ffn_sides[0])
            far_forward(ffn_2, ffn_sides[1])
            hold(ffn_sides[2], *d_sides, *outgate_turns)
        elif at == 2:
            d_sides.extend(flip(after(r, window), "head", 2) for r in (d_2, d_turns[2]))
            outgate_turns.append(turn(after(outgate_turns[-1], window), 1))
            branch_got.extend(
                turn(after(cut(d_branch_own, by), window), by) for by in range(1, turns)
            )
            far_forward(ffn_3, ffn_sides[2])
            far_back(d_1, d_sides[0])
            hold(*d_sides[1:], outgate_turns[-1], *branch_got)
        return (got,)

    later = carry(direct, -1, with_back)
    d_pre, last_rows, pack, d_low, back_rows = run(
        mixer_back_kernel,
        [
            d_mixed, state_in, later, u, v, x, scores, pre_q, pre_k, pre_v, edge, taps,
            logit, start_row, low_rank, lowrank_up,
        ],
        [
            ((length, channels), BF16),
            ((8, channels), F32),
            ((8, D), F32),
            ((RANK, length), F32),
            ((8, channels), F32),
        ],
        [
            ((length + 8, channels), F32),
            ((length + 8, channels), F32),
            ((16, DK), F32),
            ((length, DK), F32),
        ],
        vmem=7,
    )

    from_next = shift(back_rows, "seq", -1)
    outgate_turns.append(turn(after(outgate_turns[-1], back_rows), 1))
    far_back(d_2, d_sides[1])
    far_back(d_turns[2], d_sides[2])
    finish(d_turns)
    for extra in range(3, turns - 1):
        far_forward(ffn_turns[extra], flip(ffn_turns[extra], "head", 2))
        far_back(d_turns[extra], flip(d_turns[extra], "head", 2))
    hold(outgate_turns[-1])
    fixed = (last_rows + from_next * tail_keep[:, None]).astype(BF16)
    d_pre = lax.dynamic_update_slice(d_pre, fixed, ((mine ^ 3) * quarter + quarter - 8, 0))

    pre_1 = turn(d_pre, 1)

    def across(sums, *gates):
        return sums[0], flip(after(sums[0], *gates), "seq", 1), sums[1]

    sent, kept = run(
        *rows_times(
            [d_outgate, d_pre],
            [
                (0, 0, DV, outgate_weight),
                (1, 0, DK, query_weight),
                (1, DK, DK, key_weight),
                (1, 2 * DK, DV, value_weight),
            ],
        )
    )
    d_low = after(d_low, *waiting)
    near, far = fold(sent, kept)
    far = flip(far, "head", 2)
    d_lowrank = total(d_low, [("head", 1), ("head", 2)]).astype(BF16)
    low_own = lax.dynamic_slice_in_dim(d_lowrank, mine * quarter, quarter, 1)
    cuts = [ffn_cut, *(f[3] for f in made)]
    weigh("gate", cuts, [d_gate, *(g[0] for g in grads)])
    moved_gate = across(sums["gate"])
    weigh("up", cuts, [d_up, *(g[1] for g in grads)])
    moved_up = across(sums["up"])
    hold(pre_1)
    grad_own, first_part = run(
        input_back_kernel,
        [near, far, input_own, d_hidden, first_gain.reshape(1, D), low_own, lowrank_down.T],
        [(row_shape, BF16), ((1, D), F32)],
    )
    pre_2 = turn(ready(pre_1), 1)
    weigh("down", [d_ffn_cut, *(g[2] for g in grads)], [activated, *(f[0] for f in made)])
    moved_down = across(sums["down"])
    branch_near = after(jnp.concatenate(branch_got, axis=0), grad_own)
    branch_far = quarters(branch_near, flip(branch_near, "head", 2))
    normed_near = after(jnp.concatenate(normed_got, axis=0), grad_own)
    normed_far = quarters(normed_near, flip(normed_near, "head", 2))
    grad_side = flip(after(grad_own, branch_near), "head", 2)
    sum_output = run(*weight_args("stacked", share, [branch_cut, *branch_far], [gated, *gated_turns]))
    sum_outgate = run(
        *weight_args("natural", share, [normed, *normed_far], [d_outgate, *finish(outgate_turns)])
    )
    (apart,) = run(low_kernel, [d_lowrank, normed, pack], [((RANK + 8, D), F32)])
    odd = jnp.concatenate(
        [outnorm_part, jnp.broadcast_to(squared, (1, DV)), jnp.zeros((1, D - 2 * DV), F32)], axis=1
    )
    shared = jnp.concatenate([first_part, second_part, odd], axis=0)
    upper = [("seq", bit) for bit in (1 << p for p in range(1, 16)) if bit < places]
    hold(pre_2, grad_side, moved_gate[1])
    (grad_input,) = run(natural_kernel, quarters(grad_own, grad_side), [((length, D), F32)])
    pre_3 = turn(ready(pre_2), 1)
    moved_output, moved_outgate = across(sum_output, pre_2), across(sum_outgate, pre_2)
    output_later = after(output_own, pre_2)
    output_side = flip(output_later, "head", 2)
    shared = total(after(shared, pre_2), [("head", 1), ("head", 2)])
    apart = total(after(apart, pre_2), upper, BF16)
    hold(moved_up[1])
    (block_output,) = run(natural_kernel, quarters(output_later, output_side), [((length, D), F32)])
    sum_pre = run(
        *weight_args(
            "natural", share, [normed, *normed_far], [d_pre, *finish([pre_1, pre_2, pre_3])]
        )
    )
    moved_pre = flip(sum_pre[0], "seq", 1)
    shared = total(after(shared, sum_pre[0]), [*upper, ("seq", 1)])
    apart = total(after(apart, sum_pre[0]), [("seq", 1)], BF16)
    grad_gate, grad_up, grad_down, grad_output, grad_outgate = (
        kept + after(got, sum_pre[0]).astype(F32)
        for _, got, kept in (moved_gate, moved_up, moved_down, moved_output, moved_outgate)
    )
    grad_query, grad_key, grad_value = run(
        settle_kernel, [sum_pre[1], moved_pre],
        [((share, DK), F32), ((share, DK), F32), ((share, DV), F32)],
    )
    taps_query, taps_key, taps_value, grad_lowrank_up, bias_row, down_row = run(
        functools.partial(unpack_kernel, share),
        [apart],
        [
            ((TAPS, DK), F32),
            ((TAPS, DK), F32),
            ((TAPS, DV), F32),
            ((RANK, DK), F32),
            ((1, DK), F32),
            ((RANK, share), F32),
        ],
    )
    distill = shared[2, DV] / (valid_count[0, 0] * D)
    return (
        block_output,
        distill,
        grad_input,
        shared[0],
        grad_query,
        grad_key,
        grad_value,
        taps_query,
        taps_key,
        taps_value,
        down_row.T,
        grad_lowrank_up,
        bias_row.reshape(DK),
        grad_outgate,
        shared[2, :DV],
        grad_output,
        shared[1],
        grad_gate,
        grad_up,
        grad_down,
    )


def solution(mesh):
    rows, cols, whole = P("seq", None), P(None, "head"), P()
    in_specs = (
        rows, whole, cols, cols, cols, cols, cols, cols, whole, cols, P("head"), cols, whole, cols,
        whole, cols, cols, cols, P("seq"), P("seq"), rows, rows,
    )
    tiles = P("seq", "head")
    out_specs = (
        rows, whole, rows, whole, tiles, tiles, tiles, cols, cols, cols, rows, cols, P("head"), tiles,
        whole, tiles, whole, tiles, tiles, tiles,
    )
    return jax.shard_map(
        on_device, mesh=mesh, in_specs=in_specs, out_specs=out_specs, check_vma=False
    )
```

time: 508 us -> 398 us (0.78)
  matrix products: 119 us -> 3.3 us
  Pallas kernels: 6.89 us -> 81.1 us
  waiting for transfers between devices: 201 us -> 159 us
  other arithmetic: 37.1 us -> 13.8 us
    dot_general x54 -> x0, matrix products: 77.5 us -> none  [the longest x37 53.2 us: contract_rows(): lax.dot_general(left, right, (((0,), (0,)), ((), ())), preferred_element_...]
    pallas_call x4 -> x40, Pallas kernels: 6.89 us -> 81.1 us  [call(): pl.pallas_call(body, out_shape=[jax.ShapeDtypeStruct(shape, kind) for sha...]
    dot_general x12 -> x5, matrix products: 41.4 us -> 3.3 us  [dot(): lax.dot_general(left, right, (((1,), (0,)), ((), ())), precision=precisio...]
    ppermute x54 -> x66, waiting for transfers between devices: 98.1 us -> 74.3 us  [flip(): return lax.ppermute(x, axis, [(i, i ^ bit) for i in range(n)])]
    ppermute x12 -> x8, waiting for transfers between devices: 22 us -> 5.06 us  [shift(): lax.ppermute(x, axis, [(i, i + by) for i in range(n) if 0 <= i + by < n])]
    convert_element_type x14 -> x4, other arithmetic: 15.5 us -> 0.06 us  [the longest x3 0.06 us: total(): x = x + flip(x.astype(kind), axis, bit).astype(F32)]
    ppermute x21, starting transfers between devices: 19.5 us -> 29.9 us  [turn(): return lax.ppermute(x, 'seq', [(i, (i + 2 * by) % n) for i in range(n)])]
    unnamed x271 -> x320, local copies, waits for them, and re-layouts: 18.5 us -> 28.4 us
  transfers between devices with their start and end apart: 87 -> 95, of which waited for: 38 -> 45; matrix products, arithmetic and copies ran while one was open for 34% -> 5% of each run, Pallas kernels for 1% -> 12%
where the time goes in v2:
time: 398 us; the launch traced here: 391 us
  waiting for transfers between devices  159 us (40%)
  starting transfers between devices  88.6 us (22%)
  Pallas kernels  81.1 us (20%)
  local copies, waits for them, and re-layouts  37.5 us (9%)
  other arithmetic  13.8 us (3%)
  between operations  7.16 us (2%)
    pallas_call x40, Pallas kernels, call(): pl.pallas_call(body, out_shape=[jax.ShapeDtypeStruct(shape, kind) for sha...  81.1 us
    ppermute x21, waiting for transfers between devices, turn(): return lax.ppermute(x, 'seq', [(i, (i + 2 * by) % n) for i in range(n)])  80.1 us
    ppermute x66, waiting for transfers between devices, flip(): return lax.ppermute(x, axis, [(i, i ^ bit) for i in range(n)])  74.3 us
    ppermute x66, starting transfers between devices, flip(): return lax.ppermute(x, axis, [(i, i ^ bit) for i in range(n)])  36.2 us
    ppermute x21, starting transfers between devices, turn(): return lax.ppermute(x, 'seq', [(i, (i + 2 * by) % n) for i in range(n)])  29.9 us
    unnamed x320, local copies, waits for them, and re-layouts  28.4 us
    ppermute x8, starting transfers between devices, shift(): lax.ppermute(x, axis, [(i, i + by) for i in range(n) if 0 <= i + by < n])  22.5 us
  transfers between devices with their start and end apart: 95, of which 45 were waited for; matrix products, arithmetic and copies ran while one was open for 5% of the time, Pallas kernels for 12%

profile of v2, /device:TPU:0, one launch (start us, length us, event | category | flops | bytes accessed | tf_op | source)
XLA Modules:
  0.0 390.9 jit_solution(1974319547754122415)
XLA Ops:
  9.6 4.8 %collective-permute-start = (bf16[8,1024]{1,0:T(8,128)(2,1)S(1)}, bf16[8,1024]{1,0:T(8,128)(2,1)S(1)}, u32[]{:S(2)}, u32[]{:S(2)}) collective-permute-start(bf16[8,1024]{1,0:T(8,128)(2,1)S(1)} %maximum_multiply_fusion), channel_id=1, source_target_pairs={{0,4},{4,8},{8,12},{12,16},{16,20},{20,24},{24,28},{1,5},{5,9},{9,... | collective-permute-start | bytes 49160 | tf_op jit(solution)/shard_map/ppermute | solution.py:57
  22.7 3.5 collective-permute-start.1
  35.1 3.4 collective-permute-start.4
  41.1 3.6 collective-permute-done.5
  45.6 5.4 %collective-permute-start.7 = (bf16[272,512]{1,0:T(8,128)(2,1)S(1)}, bf16[272,512]{1,0:T(8,128)(2,1)S(1)}, u32[]{:S(2)}, u32[]{:S(2)}) collective-permute-start(bf16[272,512]{1,0:T(8,128)(2,1)S(1)} %get-tuple-element.250), channel_id=1, source_target_pairs={{0,16},{4,20},{8,24},{12,28},{1,17},{5,21},{9,25},{13,29},{2,18},{... | collective-permute-start | bytes 835592 | tf_op jit(solution)/shard_map/ppermute | solution.py:57
  64.6 5.0 %collective-permute-start.12 = (bf16[256,512]{1,0:T(8,128)(2,1)S(1)}, bf16[256,512]{1,0:T(8,128)(2,1)S(1)}, u32[]{:S(2)}, u32[]{:S(2)}) collective-permute-start(bf16[256,512]{1,0:T(8,128)(2,1)S(1)} %get-tuple-element.268.refs_5_), channel_id=1, source_target_pairs={{0,8},{4,12},{8,16},{12,20},{16,24},{20,28},{24,0},{28,4},{1,9},{5... | collective-permute-start | bytes 786440 | tf_op jit(solution)/shard_map/ppermute | solution.py:62
  71.4 7.3 %collective-permute-done.12.refs_6_ = bf16[256,512]{1,0:T(8,128)(2,1)S(1)} collective-permute-done((bf16[256,512]{1,0:T(8,128)(2,1)S(1)}, bf16[256,512]{1,0:T(8,128)(2,1)S(1)}, u32[]{:S(2)}, u32[]{:S(2)}) %collective-permute-start.12) | collective-permute-done | bytes 262176 | tf_op jit(solution)/shard_map/ppermute | solution.py:62
  81.1 6.8 %collective-permute-done.13.refs_1_ = bf16[64,2048]{1,0:T(8,128)(2,1)S(1)} collective-permute-done((bf16[64,2048]{1,0:T(8,128)(2,1)S(1)}, bf16[64,2048]{1,0:T(8,128)(2,1)S(1)}, u32[]{:S(2)}, u32[]{:S(2)}) %collective-permute-start.13) | collective-permute-done | bytes 262176 | tf_op jit(solution)/shard_map/ppermute | solution.py:52
  91.7 4.1 %shard_map.372 = (bf16[256,1408]{1,0:T(8,128)(2,1)S(1)}, bf16[256,1408]{1,0:T(8,128)(2,1)S(1)}, bf16[256,1408]{1,0:T(8,128)(2,1)S(1)}, bf16[256,512]{1,0:T(8,128)(2,1)S(1)}) custom-call(s32[3]{0:T(128)S(1)} %pad_add_fusion.place, bf16[64,2048]{1,0:T(8,128)(2,1)S(1)} %get-tuple-element.270.refs_0_, bf16[64,2048]{1,0:T(8,128)(2,1)S(1)} %collective-permute-done.13.refs_1_, ...), custom_call_target="tpu_custom_call" | custom-call | flops 4000000000 | bytes 12000000 | tf_op jit(solution)/shard_map/pallas_call | solution.py:376
  121.2 6.6 %collective-permute-done.20.refs_1_ = bf16[64,2048]{1,0:T(8,128)(2,1)S(1)} collective-permute-done((bf16[64,2048]{1,0:T(8,128)(2,1)S(1)}, bf16[64,2048]{1,0:T(8,128)(2,1)S(1)}, u32[]{:S(2)}, u32[]{:S(2)}) %collective-permute-start.20) | collective-permute-done | bytes 262176 | tf_op jit(solution)/shard_map/ppermute | solution.py:52
  127.8 4.6 %collective-permute-done.21.refs_0_ = bf16[64,2048]{1,0:T(8,128)(2,1)S(1)} collective-permute-done((bf16[64,2048]{1,0:T(8,128)(2,1)}, bf16[64,2048]{1,0:T(8,128)(2,1)S(1)}, u32[]{:S(2)}, u32[]{:S(2)}) %collective-permute-start.21) | collective-permute-done | bytes 262176 | tf_op jit(solution)/shard_map/ppermute | solution.py:62
  146.7 4.0 %shard_map.377 = (bf16[128,2048]{1,0:T(8,128)(2,1)S(1)}, f32[128,2048]{1,0:T(8,128)S(1)}) custom-call(s32[3]{0:T(128)S(1)} %pad_add_fusion.place, bf16[256,1408]{1,0:T(8,128)(2,1)S(1)} %get-tuple-element.301.refs_0_.refs_4_, bf16[256,1408]{1,0:T(8,128)(2,1)S(1)} %get-tuple-element.302.refs_1_.refs_4_, bf16[2048,1408]{1,0:T(8,128)(2,1)S(1)} %bitcast.33, ...), custom_call_target="tpu_custom_call" | custom-call | flops 2800000000 | bytes 8400000 | tf_op jit(solution)/shard_map/pallas_call | solution.py:376
  155.0 6.8 %collective-permute-done.26.got = bf16[64,2048]{1,0:T(8,128)(2,1)S(1)} collective-permute-done((bf16[64,2048]{1,0:T(8,128)(2,1)S(1)}, bf16[64,2048]{1,0:T(8,128)(2,1)S(1)}, u32[]{:S(2)}, u32[]{:S(2)}) %collective-permute-start.26) | collective-permute-done | bytes 262176 | tf_op jit(solution)/shard_map/ppermute | solution.py:52
  167.3 6.4 %collective-permute-done.28.branch_1 = bf16[64,2048]{1,0:T(8,128)(2,1)S(1)} collective-permute-done((bf16[64,2048]{1,0:T(8,128)(2,1)S(1)}, bf16[64,2048]{1,0:T(8,128)(2,1)S(1)}, u32[]{:S(2)}, u32[]{:S(2)}) %collective-permute-start.28) | collective-permute-done | bytes 262176 | tf_op jit(solution)/shard_map/ppermute | solution.py:52
  173.7 4.5 %collective-permute-done.29.refs_0_ = bf16[64,2048]{1,0:T(8,128)(2,1)} collective-permute-done((bf16[64,2048]{1,0:T(8,128)(2,1)S(1)}, bf16[64,2048]{1,0:T(8,128)(2,1)}, u32[]{:S(2)}, u32[]{:S(2)}) %collective-permute-start.29) | collective-permute-done | bytes 262176 | tf_op jit(solution)/shard_map/ppermute | solution.py:62
  189.0 4.8 %collective-permute-start.35 = (bf16[64,2048]{1,0:T(8,128)(2,1)}, bf16[64,2048]{1,0:T(8,128)(2,1)S(1)}, u32[]{:S(2)}, u32[]{:S(2)}) collective-permute-start(bf16[64,2048]{1,0:T(8,128)(2,1)} %collective-permute-done.29.refs_0_), channel_id=1, source_target_pairs={{0,8},{4,12},{8,16},{12,20},{16,24},{20,28},{24,0},{28,4},{1,9},{5... | collective-permute-start | bytes 786440 | tf_op jit(solution)/shard_map/ppermute | solution.py:62
  195.0 4.8 %collective-permute-done.34.refs_1_ = bf16[64,2048]{1,0:T(8,128)(2,1)S(1)} collective-permute-done((bf16[64,2048]{1,0:T(8,128)(2,1)}, bf16[64,2048]{1,0:T(8,128)(2,1)S(1)}, u32[]{:S(2)}, u32[]{:S(2)}) %collective-permute-start.34) | collective-permute-done | bytes 262176 | tf_op jit(solution)/shard_map/ppermute | solution.py:52
  204.8 4.6 %shard_map.382 = (bf16[256,1408]{1,0:T(8,128)(2,1)S(1)}, bf16[256,1408]{1,0:T(8,128)(2,1)S(1)}, bf16[256,1408]{1,0:T(8,128)(2,1)S(1)}, bf16[256,512]{1,0:T(8,128)(2,1)S(1)}) custom-call(s32[3]{0:T(128)S(1)} %pad_add_fusion.place, bf16[64,2048]{1,0:T(8,128)(2,1)} %collective-permute-done.14.refs_0_, bf16[64,2048]{1,0:T(8,128)(2,1)S(1)} %collective-permute-done.33.refs_1_, ...), custom_call_target="tpu_custom_call" | custom-call | flops 4000000000 | bytes 12000000 | tf_op jit(solution)/shard_map/pallas_call | solution.py:376
  212.3 3.5 collective-permute-start.43
  216.6 4.6 %shard_map.383 = (bf16[256,1408]{1,0:T(8,128)(2,1)S(1)}, bf16[256,1408]{1,0:T(8,128)(2,1)S(1)}, bf16[256,1408]{1,0:T(8,128)(2,1)S(1)}, bf16[256,512]{1,0:T(8,128)(2,1)S(1)}) custom-call(s32[3]{0:T(128)S(1)} %pad_add_fusion.place, bf16[64,2048]{1,0:T(8,128)(2,1)} %collective-permute-done.19.refs_0_, bf16[64,2048]{1,0:T(8,128)(2,1)S(1)} %collective-permute-done.34.refs_1_, ...), custom_call_target="tpu_custom_call" | custom-call | flops 4000000000 | bytes 12000000 | tf_op jit(solution)/shard_map/pallas_call | solution.py:376
  221.3 6.5 %collective-permute-done.43.refs_6_ = bf16[256,512]{1,0:T(8,128)(2,1)S(1)} collective-permute-done((bf16[256,512]{1,0:T(8,128)(2,1)S(1)}, bf16[256,512]{1,0:T(8,128)(2,1)S(1)}, u32[]{:S(2)}, u32[]{:S(2)}) %collective-permute-start.43) | collective-permute-done | bytes 262176 | tf_op jit(solution)/shard_map/ppermute | solution.py:62
  239.1 4.1 %shard_map.385 = (bf16[256,1408]{1,0:T(8,128)(2,1)S(1)}, bf16[256,1408]{1,0:T(8,128)(2,1)S(1)}, bf16[256,1408]{1,0:T(8,128)(2,1)S(1)}, bf16[256,512]{1,0:T(8,128)(2,1)S(1)}) custom-call(s32[3]{0:T(128)S(1)} %pad_add_fusion.place, bf16[64,2048]{1,0:T(8,128)(2,1)S(1)} %collective-permute-done.21.refs_0_, bf16[64,2048]{1,0:T(8,128)(2,1)S(1)} %collective-permute-done.41.refs_1_, ...), custom_call_target="tpu_custom_call" | custom-call | flops 4000000000 | bytes 12000000 | tf_op jit(solution)/shard_map/pallas_call | solution.py:376
  243.3 3.9 collective-permute-start.54
  249.8 6.9 %collective-permute-done.54 = bf16[64,512]{1,0:T(8,128)(2,1)S(1)} collective-permute-done((bf16[64,512]{1,0:T(8,128)(2,1)S(1)}, bf16[64,512]{1,0:T(8,128)(2,1)S(1)}, u32[]{:S(2)}, u32[]{:S(2)}) %collective-permute-start.54) | collective-permute-done | bytes 65568 | tf_op jit(solution)/shard_map/ppermute | solution.py:62
  258.8 4.7 %shard_map.388 = (bf16[256,1024]{1,0:T(8,128)(2,1)S(1)}, f32[8,1024]{1,0:T(8,128)S(1)}, f32[8,2048]{1,0:T(8,128)S(1)}, f32[16,256]{1,0:T(8,128)S(1)}, f32[8,1024]{1,0:T(8,128)}) custom-call(s32[3]{0:T(128)S(1)} %copy-done.17, bf16[256,512]{1,0:T(8,128)(2,1)S(1)} %get-tuple-element.358.d_mixed, bf16[256,512]{1,0:T(8,128)(2,1)S(1)} %copy-done.124, ...), custom_call_target="tpu_custom_call" | custom-call | flops 4499999744 | bytes 13500000 | tf_op jit(solution)/shard_map/pallas_call | solution.py:376
  267.5 4.3 %collective-permute-done.61 = f32[8,1024]{1,0:T(8,128)S(1)} collective-permute-done((f32[8,1024]{1,0:T(8,128)}, f32[8,1024]{1,0:T(8,128)S(1)}, u32[]{:S(2)}, u32[]{:S(2)}) %collective-permute-start.61) | collective-permute-done | bytes 32800 | tf_op jit(solution)/shard_map/ppermute | solution.py:57
  300.9 6.5 %collective-permute-done.63.refs_6_ = bf16[256,1024]{1,0:T(8,128)(2,1)S(1)} collective-permute-done((bf16[256,1024]{1,0:T(8,128)(2,1)S(1)}, bf16[256,1024]{1,0:T(8,128)(2,1)S(1)}, u32[]{:S(2)}, u32[]{:S(2)}) %collective-permute-start.63) | collective-permute-done | bytes 524320 | tf_op jit(solution)/shard_map/ppermute | solution.py:62
  325.1 11.6 %collective-permute-done.73.refs_7_ = bf16[256,1024]{1,0:T(8,128)(2,1)S(1)} collective-permute-done((bf16[256,1024]{1,0:T(8,128)(2,1)S(1)}, bf16[256,1024]{1,0:T(8,128)(2,1)S(1)}, u32[]{:S(2)}, u32[]{:S(2)}) %collective-permute-start.73) | collective-permute-done | bytes 524320 | tf_op jit(solution)/shard_map/ppermute | solution.py:62
  345.5 4.7 %collective-permute-done.83 = f32[3,2048]{1,0:T(4,128)S(1)} collective-permute-done((f32[3,2048]{1,0:T(4,128)S(1)}, f32[3,2048]{1,0:T(4,128)S(1)}, u32[]{:S(2)}, u32[]{:S(2)}) %collective-permute-start.83) | collective-permute-done | bytes 24608 | tf_op jit(solution)/shard_map/ppermute | solution.py:52
  356.5 8.5 %collective-permute-done.84.refs_8_ = bf16[256,1024]{1,0:T(8,128)(2,1)S(1)} collective-permute-done((bf16[256,1024]{1,0:T(8,128)(2,1)S(1)}, bf16[256,1024]{1,0:T(8,128)(2,1)S(1)}, u32[]{:S(2)}, u32[]{:S(2)}) %collective-permute-start.84) | collective-permute-done | bytes 524320 | tf_op jit(solution)/shard_map/ppermute | solution.py:62
  374.6 3.9 %collective-permute-done.86 = f32[3,2048]{1,0:T(4,128)S(1)} collective-permute-done((f32[3,2048]{1,0:T(4,128)S(1)}, f32[3,2048]{1,0:T(4,128)S(1)}, u32[]{:S(2)}, u32[]{:S(2)}) %collective-permute-start.86) | collective-permute-done | bytes 24608 | tf_op jit(solution)/shard_map/ppermute | solution.py:52
  379.5 4.8 %collective-permute-done.87 = f32[3,2048]{1,0:T(4,128)S(1)} collective-permute-done((f32[3,2048]{1,0:T(4,128)S(1)}, f32[3,2048]{1,0:T(4,128)S(1)}, u32[]{:S(2)}, u32[]{:S(2)}) %collective-permute-start.87) | collective-permute-done | bytes 24608 | tf_op jit(solution)/shard_map/ppermute | solution.py:52
  (582 shorter events, 214.4 us)
Async XLA Ops:
  64.6 14.2 %collective-permute-start.12 = (bf16[256,512]{1,0:T(8,128)(2,1)S(1)}, bf16[256,512]{1,0:T(8,128)(2,1)S(1)}, u32[]{:S(2)}, u32[]{:S(2)}) collective-permute-start(bf16[256,512]{1,0:T(8,128)(2,1)S(1)} %get-tuple-element.268.refs_5_), channel_id=1, source_target_pairs={{0,8},{4,12},{8,16},{12,20},{16,24},{20,28},{24,0},{28,4},{1,9},{5... | collective-permute-start | bytes 786440 | tf_op jit(solution)/shard_map/ppermute | solution.py:62
  121.1 14.5 %collective-permute-start.22 = (bf16[256,512]{1,0:T(8,128)(2,1)S(1)}, bf16[256,512]{1,0:T(8,128)(2,1)S(1)}, u32[]{:S(2)}, u32[]{:S(2)}) collective-permute-start(bf16[256,512]{1,0:T(8,128)(2,1)S(1)} %copy-done.42), channel_id=1, source_target_pairs={{0,8},{4,12},{8,16},{12,20},{16,24},{20,28},{24,0},{28,4},{1,9},{5... | collective-permute-start | bytes 786440 | tf_op jit(solution)/shard_map/ppermute | solution.py:62
  121.1 14.5 %collective-permute-start.23 = (bf16[64,2048]{1,0:T(8,128)(2,1)S(1)}, bf16[64,2048]{1,0:T(8,128)(2,1)S(1)}, u32[]{:S(2)}, u32[]{:S(2)}) collective-permute-start(bf16[64,2048]{1,0:T(8,128)(2,1)S(1)} %get-tuple-element.310.refs_0_), channel_id=1, source_target_pairs={{0,1},{1,0},{2,3},{3,2},{4,5},{5,4},{6,7},{7,6},{8,9},{9,8},{10,11... | collective-permute-start | bytes 786440 | tf_op jit(solution)/shard_map/ppermute | solution.py:52
  167.0 14.3 %collective-permute-start.30 = (bf16[256,512]{1,0:T(8,128)(2,1)S(1)}, bf16[256,512]{1,0:T(8,128)(2,1)S(1)}, u32[]{:S(2)}, u32[]{:S(2)}) collective-permute-start(bf16[256,512]{1,0:T(8,128)(2,1)S(1)} %collective-permute-done.22.refs_7_), channel_id=1, source_target_pairs={{0,8},{4,12},{8,16},{12,20},{16,24},{20,28},{24,0},{28,4},{1,9},{5... | collective-permute-start | bytes 786440 | tf_op jit(solution)/shard_map/ppermute | solution.py:62
  167.2 14.1 %collective-permute-start.31 = (bf16[64,2048]{1,0:T(8,128)(2,1)S(1)}, bf16[64,2048]{1,0:T(8,128)(2,1)S(1)}, u32[]{:S(2)}, u32[]{:S(2)}) collective-permute-start(bf16[64,2048]{1,0:T(8,128)(2,1)S(1)} %get-tuple-element.318.branch_0), channel_id=1, source_target_pairs={{0,1},{1,0},{2,3},{3,2},{4,5},{5,4},{6,7},{7,6},{8,9},{9,8},{10,11... | collective-permute-start | bytes 786440 | tf_op jit(solution)/shard_map/ppermute | solution.py:52
  187.2 14.3 %collective-permute-start.36 = (bf16[272,512]{1,0:T(8,128)(2,1)S(1)}, bf16[272,512]{1,0:T(8,128)(2,1)S(1)}, u32[]{:S(2)}, u32[]{:S(2)}) collective-permute-start(bf16[272,512]{1,0:T(8,128)(2,1)S(1)} %get-tuple-element.324.refs_0_), channel_id=1, source_target_pairs={{4,0},{8,4},{12,8},{16,12},{20,16},{24,20},{28,24},{5,1},{9,5},{13... | collective-permute-start | bytes 835592 | tf_op jit(solution)/shard_map/ppermute | solution.py:57
  201.4 29.7 %collective-permute-start.45 = (bf16[64,2048]{1,0:T(8,128)(2,1)S(1)}, bf16[64,2048]{1,0:T(8,128)(2,1)S(1)}, u32[]{:S(2)}, u32[]{:S(2)}) collective-permute-start(bf16[64,2048]{1,0:T(8,128)(2,1)S(1)} %collective-permute-done.21.refs_0_), channel_id=1, source_target_pairs={{0,1},{1,0},{2,3},{3,2},{4,5},{5,4},{6,7},{7,6},{8,9},{9,8},{10,11... | collective-permute-start | bytes 786440 | tf_op jit(solution)/shard_map/ppermute | solution.py:52
  210.9 20.3 %collective-permute-start.47 = (bf16[64,2048]{1,0:T(8,128)(2,1)S(1)}, bf16[64,2048]{1,0:T(8,128)(2,1)S(1)}, u32[]{:S(2)}, u32[]{:S(2)}) collective-permute-start(bf16[64,2048]{1,0:T(8,128)(2,1)S(1)} %collective-permute-done.27.refs_0_), channel_id=1, source_target_pairs={{0,1},{1,0},{2,3},{3,2},{4,5},{5,4},{6,7},{7,6},{8,9},{9,8},{10,11... | collective-permute-start | bytes 786440 | tf_op jit(solution)/shard_map/ppermute | solution.py:52
  210.9 17.6 %collective-permute-start.44 = (bf16[272,512]{1,0:T(8,128)(2,1)S(1)}, bf16[272,512]{1,0:T(8,128)(2,1)S(1)}, u32[]{:S(2)}, u32[]{:S(2)}) collective-permute-start(bf16[272,512]{1,0:T(8,128)(2,1)S(1)} %get-tuple-element.336.refs_0_), channel_id=1, source_target_pairs={{8,0},{12,4},{16,8},{20,12},{24,16},{28,20},{9,1},{13,5},{17,9},{2... | collective-permute-start | bytes 835592 | tf_op jit(solution)/shard_map/ppermute | solution.py:57
  212.3 15.5 %collective-permute-start.43 = (bf16[256,512]{1,0:T(8,128)(2,1)S(1)}, bf16[256,512]{1,0:T(8,128)(2,1)S(1)}, u32[]{:S(2)}, u32[]{:S(2)}) collective-permute-start(bf16[256,512]{1,0:T(8,128)(2,1)S(1)} %get-tuple-element.340.refs_0_.refs_5_), channel_id=1, source_target_pairs={{0,8},{4,12},{8,16},{12,20},{16,24},{20,28},{24,0},{28,4},{1,9},{5... | collective-permute-start | bytes 786440 | tf_op jit(solution)/shard_map/ppermute | solution.py:62
  216.6 22.0 %collective-permute-start.46 = (bf16[64,2048]{1,0:T(8,128)(2,1)S(1)}, bf16[64,2048]{1,0:T(8,128)(2,1)S(1)}, u32[]{:S(2)}, u32[]{:S(2)}) collective-permute-start(bf16[64,2048]{1,0:T(8,128)(2,1)S(1)} %collective-permute-done.41.refs_1_), channel_id=1, source_target_pairs={{0,1},{1,0},{2,3},{3,2},{4,5},{5,4},{6,7},{7,6},{8,9},{9,8},{10,11... | collective-permute-start | bytes 786440 | tf_op jit(solution)/shard_map/ppermute | solution.py:52
  231.2 26.1 %collective-permute-start.55 = (bf16[272,512]{1,0:T(8,128)(2,1)S(1)}, bf16[272,512]{1,0:T(8,128)(2,1)S(1)}, u32[]{:S(2)}, u32[]{:S(2)}) collective-permute-start(bf16[272,512]{1,0:T(8,128)(2,1)S(1)} %get-tuple-element.349), channel_id=1, source_target_pairs={{16,0},{20,4},{24,8},{28,12},{17,1},{21,5},{25,9},{29,13},{18,2},{... | collective-permute-start | bytes 835592 | tf_op jit(solution)/shard_map/ppermute | solution.py:57
  235.9 20.8 %collective-permute-start.49 = (bf16[64,2048]{1,0:T(8,128)(2,1)}, bf16[64,2048]{1,0:T(8,128)(2,1)}, u32[]{:S(2)}, u32[]{:S(2)}) collective-permute-start(bf16[64,2048]{1,0:T(8,128)(2,1)} %collective-permute-done.29.refs_0_), channel_id=1, source_target_pairs={{0,2},{1,3},{2,0},{3,1},{4,6},{5,7},{6,4},{7,5},{8,10},{9,11},{10,... | collective-permute-start | bytes 786440 | tf_op jit(solution)/shard_map/ppermute | solution.py:52
  238.1 18.6 %collective-permute-start.50 = (bf16[64,2048]{1,0:T(8,128)(2,1)S(1)}, bf16[64,2048]{1,0:T(8,128)(2,1)S(1)}, u32[]{:S(2)}, u32[]{:S(2)}) collective-permute-start(bf16[64,2048]{1,0:T(8,128)(2,1)S(1)} %collective-permute-done.35.refs_0_), channel_id=1, source_target_pairs={{0,2},{1,3},{2,0},{3,1},{4,6},{5,7},{6,4},{7,5},{8,10},{9,11},{10,... | collective-permute-start | bytes 786440 | tf_op jit(solution)/shard_map/ppermute | solution.py:52
  238.6 18.1 %collective-permute-start.51 = (bf16[256,512]{1,0:T(8,128)(2,1)S(1)}, bf16[256,512]{1,0:T(8,128)(2,1)S(1)}, u32[]{:S(2)}, u32[]{:S(2)}) collective-permute-start(bf16[256,512]{1,0:T(8,128)(2,1)S(1)} %collective-permute-done.43.refs_6_), channel_id=1, source_target_pairs={{0,8},{4,12},{8,16},{12,20},{16,24},{20,28},{24,0},{28,4},{1,9},{5... | collective-permute-start | bytes 786440 | tf_op jit(solution)/shard_map/ppermute | solution.py:62
  243.3 13.4 %collective-permute-start.54 = (bf16[64,512]{1,0:T(8,128)(2,1)S(1)}, bf16[64,512]{1,0:T(8,128)(2,1)S(1)}, u32[]{:S(2)}, u32[]{:S(2)}) collective-permute-start(bf16[64,512]{1,0:T(8,128)(2,1)S(1)} %get-tuple-element.355), channel_id=1, source_target_pairs={{0,24},{4,28},{8,0},{12,4},{16,8},{20,12},{24,16},{28,20},{1,25},{... | collective-permute-start | bytes 196616 | tf_op jit(solution)/shard_map/ppermute | solution.py:62
  256.7 17.9 %collective-permute-start.56 = (bf16[64,2048]{1,0:T(8,128)(2,1)}, bf16[64,2048]{1,0:T(8,128)(2,1)}, u32[]{:S(2)}, u32[]{:S(2)}) collective-permute-start(bf16[64,2048]{1,0:T(8,128)(2,1)} %collective-permute-done.29.refs_0_), channel_id=1, source_target_pairs={{0,1},{1,0},{2,3},{3,2},{4,5},{5,4},{6,7},{7,6},{8,9},{9,8},{10,11... | collective-permute-start | bytes 786440 | tf_op jit(solution)/shard_map/ppermute | solution.py:52
  256.8 17.9 %collective-permute-start.57 = (bf16[64,2048]{1,0:T(8,128)(2,1)}, bf16[64,2048]{1,0:T(8,128)(2,1)}, u32[]{:S(2)}, u32[]{:S(2)}) collective-permute-start(bf16[64,2048]{1,0:T(8,128)(2,1)} %collective-permute-done.49.refs_1_), channel_id=1, source_target_pairs={{0,1},{1,0},{2,3},{3,2},{4,5},{5,4},{6,7},{7,6},{8,9},{9,8},{10,11... | collective-permute-start | bytes 786440 | tf_op jit(solution)/shard_map/ppermute | solution.py:52
  266.9 16.6 %collective-permute-start.58 = (bf16[64,2048]{1,0:T(8,128)(2,1)}, bf16[64,2048]{1,0:T(8,128)(2,1)S(1)}, u32[]{:S(2)}, u32[]{:S(2)}) collective-permute-start(bf16[64,2048]{1,0:T(8,128)(2,1)} %copy-done.54), channel_id=1, source_target_pairs={{0,1},{1,0},{2,3},{3,2},{4,5},{5,4},{6,7},{7,6},{8,9},{9,8},{10,11... | collective-permute-start | bytes 786440 | tf_op jit(solution)/shard_map/ppermute | solution.py:52
  267.0 16.5 %collective-permute-start.59 = (bf16[64,2048]{1,0:T(8,128)(2,1)}, bf16[64,2048]{1,0:T(8,128)(2,1)S(1)}, u32[]{:S(2)}, u32[]{:S(2)}) collective-permute-start(bf16[64,2048]{1,0:T(8,128)(2,1)} %copy-done.56), channel_id=1, source_target_pairs={{0,1},{1,0},{2,3},{3,2},{4,5},{5,4},{6,7},{7,6},{8,9},{9,8},{10,11... | collective-permute-start | bytes 786440 | tf_op jit(solution)/shard_map/ppermute | solution.py:52
  271.8 14.3 %collective-permute-start.60 = (bf16[256,512]{1,0:T(8,128)(2,1)}, bf16[256,512]{1,0:T(8,128)(2,1)S(1)}, u32[]{:S(2)}, u32[]{:S(2)}) collective-permute-start(bf16[256,512]{1,0:T(8,128)(2,1)} %copy-done.52), channel_id=1, source_target_pairs={{0,8},{4,12},{8,16},{12,20},{16,24},{20,28},{24,0},{28,4},{1,9},{5... | collective-permute-start | bytes 786440 | tf_op jit(solution)/shard_map/ppermute | solution.py:62
  291.9 15.5 %collective-permute-start.63 = (bf16[256,1024]{1,0:T(8,128)(2,1)S(1)}, bf16[256,1024]{1,0:T(8,128)(2,1)S(1)}, u32[]{:S(2)}, u32[]{:S(2)}) collective-permute-start(bf16[256,1024]{1,0:T(8,128)(2,1)S(1)} %copy-done.36), channel_id=1, source_target_pairs={{0,8},{4,12},{8,16},{12,20},{16,24},{20,28},{24,0},{28,4},{1,9},{5... | collective-permute-start | bytes 1572872 | tf_op jit(solution)/shard_map/ppermute | solution.py:62
  310.1 28.7 %collective-permute-start.75 = (bf16[256,1408]{1,0:T(8,128)(2,1)S(1)}, bf16[256,1408]{1,0:T(8,128)(2,1)S(1)}, u32[]{:S(2)}, u32[]{:S(2)}) collective-permute-start(bf16[256,1408]{1,0:T(8,128)(2,1)S(1)} %get-tuple-element.414), channel_id=1, source_target_pairs={{0,4},{4,0},{8,12},{12,8},{16,20},{20,16},{24,28},{28,24},{1,5},{5... | collective-permute-start | bytes 2162696 | tf_op jit(solution)/shard_map/ppermute | solution.py:52
  313.1 32.4 %collective-permute-start.78 = (bf16[256,1408]{1,0:T(8,128)(2,1)S(1)}, bf16[256,1408]{1,0:T(8,128)(2,1)S(1)}, u32[]{:S(2)}, u32[]{:S(2)}) collective-permute-start(bf16[256,1408]{1,0:T(8,128)(2,1)S(1)} %get-tuple-element.416), channel_id=1, source_target_pairs={{0,4},{4,0},{8,12},{12,8},{16,20},{20,16},{24,28},{28,24},{1,5},{5... | collective-permute-start | bytes 2162696 | tf_op jit(solution)/shard_map/ppermute | solution.py:52
  320.5 16.2 %collective-permute-start.73 = (bf16[256,1024]{1,0:T(8,128)(2,1)S(1)}, bf16[256,1024]{1,0:T(8,128)(2,1)S(1)}, u32[]{:S(2)}, u32[]{:S(2)}) collective-permute-start(bf16[256,1024]{1,0:T(8,128)(2,1)S(1)} %collective-permute-done.63.refs_6_), channel_id=1, source_target_pairs={{0,8},{4,12},{8,16},{12,20},{16,24},{20,28},{24,0},{28,4},{1,9},{5... | collective-permute-start | bytes 1572872 | tf_op jit(solution)/shard_map/ppermute | solution.py:62
  322.3 16.0 %collective-permute-start.74 = (bf16[64,2048]{1,0:T(8,128)(2,1)S(1)}, bf16[64,2048]{1,0:T(8,128)(2,1)S(1)}, u32[]{:S(2)}, u32[]{:S(2)}) collective-permute-start(bf16[64,2048]{1,0:T(8,128)(2,1)S(1)} %get-tuple-element.413.piece_0), channel_id=1, source_target_pairs={{0,2},{1,3},{2,0},{3,1},{4,6},{5,7},{6,4},{7,5},{8,10},{9,11},{10,... | collective-permute-start | bytes 786440 | tf_op jit(solution)/shard_map/ppermute | solution.py:52
  338.8 31.7 %collective-permute-start.94 = (bf16[256,1408]{1,0:T(8,128)(2,1)S(1)}, bf16[256,1408]{1,0:T(8,128)(2,1)S(1)}, u32[]{:S(2)}, u32[]{:S(2)}) collective-permute-start(bf16[256,1408]{1,0:T(8,128)(2,1)S(1)} %get-tuple-element.448), channel_id=1, source_target_pairs={{0,4},{4,0},{8,12},{12,8},{16,20},{20,16},{24,28},{28,24},{1,5},{5... | collective-permute-start | bytes 2162696 | tf_op jit(solution)/shard_map/ppermute | solution.py:52
  350.3 14.7 %collective-permute-start.84 = (bf16[256,1024]{1,0:T(8,128)(2,1)S(1)}, bf16[256,1024]{1,0:T(8,128)(2,1)S(1)}, u32[]{:S(2)}, u32[]{:S(2)}) collective-permute-start(bf16[256,1024]{1,0:T(8,128)(2,1)S(1)} %collective-permute-done.73.refs_7_), channel_id=1, source_target_pairs={{0,8},{4,12},{8,16},{12,20},{16,24},{20,28},{24,0},{28,4},{1,9},{5... | collective-permute-start | bytes 1572872 | tf_op jit(solution)/shard_map/ppermute | solution.py:62
  352.3 21.3 %collective-permute-start.92 = (bf16[256,512]{1,0:T(8,128)(2,1)S(1)}, bf16[256,512]{1,0:T(8,128)(2,1)S(1)}, u32[]{:S(2)}, u32[]{:S(2)}) collective-permute-start(bf16[256,512]{1,0:T(8,128)(2,1)S(1)} %get-tuple-element.441), channel_id=1, source_target_pairs={{0,4},{4,0},{8,12},{12,8},{16,20},{20,16},{24,28},{28,24},{1,5},{5... | collective-permute-start | bytes 786440 | tf_op jit(solution)/shard_map/ppermute | solution.py:52
  352.5 22.1 %collective-permute-start.93 = (bf16[256,512]{1,0:T(8,128)(2,1)S(1)}, bf16[256,512]{1,0:T(8,128)(2,1)S(1)}, u32[]{:S(2)}, u32[]{:S(2)}) collective-permute-start(bf16[256,512]{1,0:T(8,128)(2,1)S(1)} %get-tuple-element.444), channel_id=1, source_target_pairs={{0,4},{4,0},{8,12},{12,8},{16,20},{20,16},{24,28},{28,24},{1,5},{5... | collective-permute-start | bytes 786440 | tf_op jit(solution)/shard_map/ppermute | solution.py:52
  367.0 19.7 %collective-permute-start.88 = (bf16[256,1024]{1,0:T(8,128)(2,1)S(1)}, bf16[256,1024]{1,0:T(8,128)(2,1)S(1)}, u32[]{:S(2)}, u32[]{:S(2)}) collective-permute-start(bf16[256,1024]{1,0:T(8,128)(2,1)S(1)} %get-tuple-element.424), channel_id=1, source_target_pairs={{0,4},{4,0},{8,12},{12,8},{16,20},{20,16},{24,28},{28,24},{1,5},{5... | collective-permute-start | bytes 1572872 | tf_op jit(solution)/shard_map/ppermute | solution.py:52
  370.4 16.2 %collective-permute-start.91 = (bf16[24,2048]{1,0:T(8,128)(2,1)S(1)}, bf16[24,2048]{1,0:T(8,128)(2,1)S(1)}, u32[]{:S(2)}, u32[]{:S(2)}) collective-permute-start(bf16[24,2048]{1,0:T(8,128)(2,1)S(1)} %reduce-precision_convert_fusion), channel_id=1, source_target_pairs={{0,4},{4,0},{8,12},{12,8},{16,20},{20,16},{24,28},{28,24},{1,5},{5... | collective-permute-start | bytes 294920 | tf_op jit(solution)/shard_map/ppermute | solution.py:52
  (222 other events, 2477.5 us)

commit v3 on v2

--- a/solution.py
+++ b/solution.py
@@ -215,7 +215,7 @@
 
 def gate_back_kernel(
     place, branch_0, branch_1, branch_2, branch_3, weight, mixed, outgate, gain, u_in, x_in,
-    start_row, d_outgate_out, d_mixed_out, gain_out, direct_out, cut_out, order,
+    start_row, d_outgate_out, d_mixed_out, gain_out, direct_out, order,
 ):
     n = x_in.shape[0]
     blocks = n // BLOCK
@@ -223,7 +223,6 @@
     for p, piece in enumerate((branch_0, branch_1, branch_2, branch_3)):
         at = pl.multiple_of((m ^ p) * BLOCK, BLOCK)
         order[pl.ds(at, BLOCK), :] = piece[...]
-        cut_out[p * BLOCK : (p + 1) * BLOCK, :] = piece[:, pair_lanes(place, cut_out)]
     up = dot(order[...], weight[...])
     og = outgate[...]
     sig = jax.nn.sigmoid(og)
@@ -396,8 +395,12 @@
     far_out[...] = (kept[quarter:] + got[quarter:].astype(F32)).astype(BF16)
 
 
-def hidden_kernel(place, kept, got, own_input, gain, hidden_out, ffn_out):
-    hidden = own_input[...].astype(F32) + (kept[...] + got[...].astype(F32))
+def own_rows(place, ref, quarter):
+    return ref[pl.ds(pl.multiple_of(place[0] * quarter, quarter), quarter), :]
+
+
+def hidden_kernel(place, kept, got, rows, gain, hidden_out, ffn_out):
+    hidden = own_rows(place, rows, kept.shape[0]).astype(F32) + (kept[...] + got[...].astype(F32))
     hidden_out[...] = hidden
     ffn_out[...] = (hidden * root_scale(hidden) * gain[...]).astype(BF16)
 
@@ -406,19 +409,24 @@
     weight, place, kept, got, hidden, teacher, cotangent, valid, count,
     output_out, d_out_out, d_ffn_out, squared_out,
 ):
+    quarter = kept.shape[0]
     output = hidden[...] + (kept[...] + got[...].astype(F32))
     output_out[...] = output.astype(BF16)
-    mismatch = output - teacher[...].astype(F32)
-    keep = valid[...]
+    mismatch = output - own_rows(place, teacher, quarter).astype(F32)
+    length = valid.shape[1]
+    rows = lax.broadcasted_iota(jnp.int32, (quarter, length), 0) + place[0] * quarter
+    cols = lax.broadcasted_iota(jnp.int32, (quarter, length), 1)
+    keep = jnp.sum(jnp.where(rows == cols, valid[...], 0.0), axis=1, keepdims=True)
     squares = jnp.sum(keep * mismatch * mismatch, axis=0, keepdims=True)
     squared_out[...] = jnp.sum(squares, axis=1, keepdims=True)
-    d_out = cotangent[...].astype(F32) + keep * (2.0 * weight) * mismatch / (count[...] * D)
+    scaled = keep * (2.0 * weight) * mismatch / (count[0:1, 0:1] * D)
+    d_out = own_rows(place, cotangent, quarter).astype(F32) + scaled
     d_out_out[...] = d_out
     d_ffn_out[...] = d_out.astype(BF16)
 
 
 def hidden_back_kernel(
-    place, kept, got, hidden, d_out, gain, d_hidden_out, d_branch_out, gain_out
+    turns, place, kept, got, hidden, d_out, gain, normed, d_hidden_out, d_branch_out, gain_out, *cuts
 ):
     d_norm = kept[...] + got[...].astype(F32)
     h = hidden[...]
@@ -427,13 +435,29 @@
     d_hidden = d_out[...] + norm_backward(h, scale, gain[...], d_norm)
     d_hidden_out[...] = d_hidden
     d_branch_out[...] = d_hidden.astype(BF16)
+    quarter = kept.shape[0]
+    rows = pl.ds(pl.multiple_of(place[0] * quarter, quarter), quarter)
+    for by, cut in enumerate(cuts, 1):
+        pair = cut.shape[1] // 2
+        target = place[1] + by
+        target = jnp.where(target >= turns, target - turns, target)
+        lanes = pl.ds(pl.multiple_of(target * pair, pair), pair)
+        cut[:, 0:pair] = normed[rows, lanes]
+        cut[:, pair:] = d_branch_out[:, lanes]
 
 
 def input_back_kernel(
-    place, kept, got, own_input, d_hidden, gain, d_low, down_turned, grad_out, gain_out
+    place, kept, got, rows, d_hidden, gain, d_low, d_low_got, down_turned,
+    grad_out, gain_out, d_low_out,
 ):
-    d_norm = (kept[...] + got[...].astype(F32)) + contract_rows(d_low[...], down_turned[...])
-    v = own_input[...].astype(F32)
+    quarter, length = kept.shape[0], d_low.shape[1]
+    d_lowrank = (d_low[...] + d_low_got[...]).astype(BF16)
+    d_low_out[...] = d_lowrank
+    here = lax.broadcasted_iota(jnp.int32, (quarter, length), 0) + place[0] * quarter
+    tokens = lax.broadcasted_iota(jnp.int32, (quarter, length), 1)
+    own_low = contract_cols((here == tokens).astype(BF16), d_lowrank).astype(BF16)
+    d_norm = (kept[...] + got[...].astype(F32)) + dot(own_low, down_turned[...])
+    v = own_rows(place, rows, quarter).astype(F32)
     scale = root_scale(v)
     gain_out[...] = jnp.sum(d_norm * v * scale, axis=0, keepdims=True)
     grad_out[...] = (d_hidden[...] + norm_backward(v, scale, gain[...], d_norm)).astype(BF16)
@@ -514,107 +538,225 @@
     return pl.ds(pl.multiple_of(place[1] * pair, pair), pair)
 
 
+def stacked(pieces, rest):
+    if len(pieces) == 1:
+        return pieces[0], rest
+    stack(pieces, rest[-1])
+    return rest[-1], rest[:-1]
+
+
+def gate_parts(buf, gate_w, up_w, act_out, gate_out, up_out):
+    for rows in spans(buf.shape[0], 512):
+        for lanes in spans(gate_w.shape[1], 256):
+            gate, up = dot(buf[rows, :], gate_w[:, lanes]), dot(buf[rows, :], up_w[:, lanes])
+            sig = jax.nn.sigmoid(gate)
+            swish = gate * sig
+            act_out[rows, lanes] = (swish * up).astype(BF16)
+            gate_out[rows, lanes] = (up * sig * (1.0 + gate * (1.0 - sig))).astype(BF16)
+            up_out[rows, lanes] = swish.astype(BF16)
+
+
+def gate_back_parts(buf, down_w, gate_in, up_in, d_gate_out, d_up_out):
+    for rows in spans(buf.shape[0], 512):
+        for lanes in spans(down_w.shape[1], 256):
+            d_act = dot(buf[rows, :], down_w[:, lanes])
+            d_gate_out[rows, lanes] = (d_act * gate_in[rows, lanes].astype(F32)).astype(BF16)
+            d_up_out[rows, lanes] = (d_act * up_in[rows, lanes].astype(F32)).astype(BF16)
+
+
 def gate_kernel(count, place, *refs):
-    pieces, (gate_w, up_w, act_out, gate_out, up_out, cut_out, buf) = refs[:count], refs[count:]
-    stack(pieces, buf)
-    cut_out[...] = buf[:, pair_lanes(place, cut_out)]
-    for lanes in spans(act_out.shape[1], 256):
-        gate, up = dot(buf[...], gate_w[:, lanes]), dot(buf[...], up_w[:, lanes])
-        sig = jax.nn.sigmoid(gate)
-        swish = gate * sig
-        act_out[:, lanes] = (swish * up).astype(BF16)
-        gate_out[:, lanes] = (up * sig * (1.0 + gate * (1.0 - sig))).astype(gate_out.dtype)
-        up_out[:, lanes] = swish.astype(up_out.dtype)
-
-
-def gate_up(pair, pieces, gate_weight, up_weight, kind):
+    buf, rest = stacked(refs[:count], refs[count:])
+    for cut_out in rest[5:]:
+        cut_out[...] = buf[:, pair_lanes(place, cut_out)]
+    gate_parts(buf, *rest[:5])
+
+
+def gate_up(pieces, gate_weight, up_weight, pair=0):
     length = sum(p.shape[0] for p in pieces)
     width = gate_weight.shape[1]
     return (
         functools.partial(gate_kernel, len(pieces)),
         [*pieces, gate_weight, up_weight],
-        [
-            ((length, width), BF16),
-            ((length, width), kind),
-            ((length, width), kind),
-            ((length, pair), BF16),
-        ],
-        [((length, D), BF16)],
+        [((length, width), BF16)] * 3 + [((length, pair), BF16)] * (pair > 0),
+        [((length, D), BF16)] * (len(pieces) > 1),
     )
 
 
 def gate_back_kernel_rows(count, place, *refs):
-    pieces, (down_w, gate_in, up_in, d_gate_out, d_up_out, cut_out, buf) = refs[:count], refs[count:]
-    stack(pieces, buf)
-    cut_out[...] = buf[:, pair_lanes(place, cut_out)]
-    for lanes in spans(d_gate_out.shape[1], 256):
-        d_act = dot(buf[...], down_w[:, lanes])
-        d_gate_out[:, lanes] = (d_act * gate_in[:, lanes].astype(F32)).astype(BF16)
-        d_up_out[:, lanes] = (d_act * up_in[:, lanes].astype(F32)).astype(BF16)
-
-
-def gate_back_rows(pair, pieces, down_weight, gate_in, up_in):
+    buf, rest = stacked(refs[:count], refs[count:])
+    for cut_out in rest[5:]:
+        cut_out[...] = buf[:, pair_lanes(place, cut_out)]
+    gate_back_parts(buf, *rest[:5])
+
+
+def gate_back_rows(pieces, down_weight, gate_in, up_in, pair=0):
     length, width = gate_in.shape
     return (
         functools.partial(gate_back_kernel_rows, len(pieces)),
         [*pieces, down_weight, gate_in, up_in],
-        [((length, width), BF16), ((length, width), BF16), ((length, pair), BF16)],
-        [((length, D), BF16)],
-    )
-
-
-def weight_kernel(kind, blocks, place, *refs):
-    sent, kept, left_buf, res = refs[-4:]
-    rights, lefts = refs[-4 - blocks : -4], refs[: -4 - blocks]
-    m, side = place[0], place[2]
+        [((length, width), BF16)] * 2 + [((length, pair), BF16)] * (pair > 0),
+        [((length, D), BF16)] * (len(pieces) > 1),
+    )
+
+
+def zone_rows(turns, place, refs, buf):
+    owns, sides = refs[:turns], []
+    taken = turns
+    quarter = buf.shape[0] // (2 * turns)
+    while len(sides) < turns:
+        ref = refs[taken]
+        sides += [(ref, at) for at in range(0, ref.shape[0], quarter)]
+        taken += 1
+    zone = place[1]
+    for by in range(turns):
+        source = jnp.where(zone < by, zone - by + turns, zone - by)
+        at = pl.multiple_of(2 * source * quarter, quarter)
+        buf[pl.ds(at, quarter), :] = owns[by][:, 0:D]
+        ref, row = sides[by]
+        buf[pl.ds(at + quarter, quarter), :] = ref[row : row + quarter, :]
+    return refs[taken:]
+
+
+def far_gate_kernel(turns, place, *refs):
+    buf = refs[-1]
+    gate_w, up_w, *outs = zone_rows(turns, place, refs[:-1], buf)
+    outs[3][...] = buf[:, pair_lanes(place, outs[3])]
+    gate_parts(buf, gate_w, up_w, *outs[:3])
+
+
+def far_gate_up(owns, sides, gate_weight, up_weight, pair):
+    length, width = 2 * len(owns) * owns[0].shape[0], gate_weight.shape[1]
+    return (
+        functools.partial(far_gate_kernel, len(owns)),
+        [*owns, *sides, gate_weight, up_weight],
+        [((length, width), BF16)] * 3 + [((length, pair), BF16), ((length, D), BF16)],
+    )
+
+
+def far_back_kernel(turns, place, *refs):
+    buf = refs[-1]
+    down_w, gate_in, up_in, d_gate_out, d_up_out, cut_out = zone_rows(turns, place, refs[:-1], buf)
+    cut_out[...] = buf[:, pair_lanes(place, cut_out)]
+    gate_back_parts(buf, down_w, gate_in, up_in, d_gate_out, d_up_out)
+
+
+def far_back_rows(owns, sides, down_weight, gate_in, up_in, pair):
+    length, width = gate_in.shape
+    return (
+        functools.partial(far_back_kernel, len(owns)),
+        [*owns, *sides, down_weight, gate_in, up_in],
+        [((length, width), BF16)] * 2 + [((length, pair), BF16), ((length, D), BF16)],
+    )
+
+
+def pair_sums(blocks, side, sent, kept, res, at=0):
     share = kept.shape[0]
-    length = rights[0].shape[0]
-    quarter = length // 4
-    if kind == "cuts":
-        stack(lefts, left_buf)
-    else:
-        if kind == "natural":
-            lanes = pair_lanes(place, left_buf)
-            for p in range(4):
-                rows = pl.ds(pl.multiple_of((m ^ p) * quarter, quarter), quarter)
-                left_buf[p * quarter : (p + 1) * quarter, :] = lefts[0][rows, lanes]
-        else:
-            left_buf[0:length, :] = lefts[0][...]
-        for block in range(1, blocks):
-            for p in range(4):
-                at = block * length + p * quarter
-                piece = lefts[1 + p][(block - 1) * quarter : block * quarter, :]
-                left_buf[at : at + quarter, :] = piece
-    for cols in spans(kept.shape[1], 256):
+    width_all = kept.shape[1] // (2 if at or len(blocks[0]) == 4 else 1)
+    for cols in spans(width_all, 256):
         acc = None
-        for block, right in enumerate(rights):
-            term = contract_rows(
-                left_buf[block * length : (block + 1) * length, :], right[:, cols]
-            )
+        for left, right, first, *_ in blocks:
+            term = contract_rows(left[...], right[:, first + cols.start : first + cols.stop])
             acc = term if acc is None else acc + term
         width = cols.stop - cols.start
+        out = slice(at + cols.start, at + cols.stop)
         res[:, 0:width] = acc
-        sent[:, cols] = res[
+        sent[:, out] = res[
             pl.ds(pl.multiple_of((1 - side) * share, share), share), 0:width
         ].astype(BF16)
-        kept[:, cols] = res[pl.ds(pl.multiple_of(side * share, share), share), 0:width]
-
-
-def weight_args(kind, share, lefts, rights):
-    tokens, width = rights[0].shape[0] * len(rights), rights[0].shape[1]
+        kept[:, out] = res[pl.ds(pl.multiple_of(side * share, share), share), 0:width]
+
+
+def far_weight_kernel(place, *refs):
+    sent, kept, res = refs[-3:]
+    count = (len(refs) - 3) // 2
+    blocks = [(left, right, 0) for left, right in zip(refs[:count], refs[count:-3])]
+    pair_sums(blocks, place[2], sent, kept, res)
+
+
+def far_weight(share, lefts, rights):
+    width = rights[0].shape[1]
     return (
-        functools.partial(weight_kernel, kind, len(rights)),
+        far_weight_kernel,
         [*lefts, *rights],
         [((share, width), BF16), ((share, width), F32)],
-        [((tokens, 2 * share), BF16), ((2 * share, 256), F32)],
-    )
-
-
-def natural_kernel(place, piece_0, piece_1, piece_2, piece_3, out):
-    quarter = piece_0.shape[0]
-    for p, piece in enumerate((piece_0, piece_1, piece_2, piece_3)):
-        at = pl.multiple_of((place[0] ^ p) * quarter, quarter)
-        out[pl.ds(at, quarter), :] = piece[...].astype(F32)
+        [((2 * share, 256), F32)],
+    )
+
+
+def fill_lefts(place, turns, own, cuts, first, buf):
+    m = place[0]
+    quarter = buf.shape[0] // (4 * turns)
+    pair = buf.shape[1]
+    lanes = pair_lanes(place, buf)
+    for p in range(4):
+        rows = slice(p * quarter, (p + 1) * quarter)
+        if len(own) == 1:
+            from_rows = pl.ds(pl.multiple_of((m ^ p) * quarter, quarter), quarter)
+            buf[rows, :] = own[0][from_rows, lanes]
+        else:
+            buf[rows, :] = own[p][:, lanes]
+        for block in range(1, turns):
+            at = (4 * block + p) * quarter
+            piece = cuts[p][(block - 1) * quarter : block * quarter, first : first + pair]
+            buf[at : at + quarter, :] = piece
+
+
+def both_kernel(turns, place, *refs):
+    branch, normed, cuts = refs[0:4], refs[4:5], refs[5:9]
+    d_outgate, gated = refs[9], refs[10]
+    outgates, gateds = refs[11 : 10 + turns], refs[10 + turns : 9 + 2 * turns]
+    sent, kept, buf, res = refs[9 + 2 * turns :]
+    length = gated.shape[0]
+    pair, half = buf.shape[1], gated.shape[1]
+    for own, first, rights, at in (
+        (branch, pair, (gated, *gateds), 0),
+        (normed, 0, (d_outgate, *outgates), half),
+    ):
+        fill_lefts(place, turns, own, cuts, first, buf)
+        blocks = [
+            (buf.at[block * length : (block + 1) * length, :], right, 0, None)
+            for block, right in enumerate(rights)
+        ]
+        pair_sums(blocks, place[2], sent, kept, res, at)
+
+
+def pre_kernel(turns, place, *refs):
+    normed, cuts, rights = refs[0:1], refs[1:5], refs[5 : 5 + turns]
+    sent, kept, buf, res = refs[5 + turns :]
+    length = rights[0].shape[0]
+    fill_lefts(place, turns, normed, cuts, 0, buf)
+    blocks = [
+        (buf.at[block * length : (block + 1) * length, :], right, 0)
+        for block, right in enumerate(rights)
+    ]
+    pair_sums(blocks, place[2], sent, kept, res)
+
+
+def zone_weight(body, turns, share, length, width, args):
+    return (
+        functools.partial(body, turns),
+        args,
+        [((share, width), BF16), ((share, width), F32)],
+        [((turns * length, 2 * share), BF16), ((2 * share, 256), F32)],
+    )
+
+
+def edge_kernel(place, d_pre, last_rows, from_next, keep, out):
+    quarter = d_pre.shape[0] // 4
+    out[...] = d_pre[...]
+    at = pl.multiple_of((place[0] ^ 3) * quarter + quarter - 8, 8)
+    out[pl.ds(at, 8), :] = (last_rows[...] + from_next[...] * keep[...]).astype(BF16)
+
+
+def stack_kernel(place, *refs):
+    stack(refs[:-1], refs[-1])
+
+
+def natural_kernel(row, place, own, side, other_own, other_side, out):
+    quarter = out.shape[0] // 4
+    for p, ref in enumerate((own, side, other_own, other_side)):
+        to = pl.multiple_of((place[0] ^ p) * quarter, quarter)
+        out[pl.ds(to, quarter), :] = ref[row : row + quarter, :].astype(F32)
 
 
 def settle_kernel(place, kept, got, out_0, out_1, out_2):
@@ -625,9 +767,13 @@
         at += width
 
 
-def low_kernel(place, d_low, normed, pack, out):
+def low_kernel(place, d_low, normed, pack, first, second, outnorm, squared, out):
     out[0:RANK, :] = dot(d_low[...], normed[...])
     out[RANK:, :] = pack[...]
+    out[RANK + 5 : RANK + 6, :] = first[...]
+    out[RANK + 6 : RANK + 7, :] = second[...]
+    out[RANK + 7 : RANK + 8, 0:DV] = outnorm[...]
+    out[RANK + 7 : RANK + 8, DV : 2 * DV] = jnp.broadcast_to(squared[...], (1, DV))
 
 
 def unpack_kernel(share, place, summed, query_out, key_out, value_out, up_out, bias_out, down_out):
@@ -653,9 +799,12 @@
     "gate_back_kernel": 2.0,
     "mixer_back_kernel": 4.5,
     "rows_kernel": 2.8,
-    "gate_kernel": 4.0,
-    "gate_back_kernel_rows": 2.4,
-    "weight_kernel": 2.4,
+    "gate_kernel": 5.0,
+    "gate_back_kernel_rows": 3.0,
+    "far_back_kernel": 4.0,
+    "far_weight_kernel": 2.5,
+    "both_kernel": 3.0,
+    "pre_kernel": 2.0,
     "natural_kernel": 2.0,
 }
 
@@ -699,6 +848,7 @@
     loss_weight = float(length * places * D // 8)
     row_shape = (quarter, D)
     window_shape = (DK + 16, 2 * DK)
+    roomy = 6 if turns <= 4 else 20
 
 
     waiting = []
@@ -717,16 +867,9 @@
     def ready(x):
         return after(x, *waiting)
 
-    def own(x):
-        return lax.dynamic_slice_in_dim(x, mine * quarter, quarter, 0)
-
     def fold(sent, kept):
         got = flip(sent, "head", 1)
         return run(fold_kernel, [kept, got], [(row_shape, F32), (row_shape, BF16)])
-
-    def cut(own_rows, by):
-        target = lax.rem(zone + by, turns)
-        return lax.dynamic_slice_in_dim(own_rows, target * pair, pair, 1)
 
     def quarters(own_rows, side_rows):
         return [own_rows, side_rows, flip(own_rows, "head", 1), flip(side_rows, "head", 1)]
@@ -780,31 +923,25 @@
         return blocks
 
     valid_float = valid_mask.astype(F32)
-    normed_own = own(normed)
-    counts, normed_got, outgates = [jnp.full((8, 128), jnp.sum(valid_float), F32)], [], []
+    counts, outgates = [jnp.full((8, 128), jnp.sum(valid_float), F32)], []
 
     def with_forward(at, step, got, window):
         count = after(counts[-1], window)
         beside = [count + flip(count, "seq", step)]
-        if at + 1 < turns:
-            beside.append(turn(after(cut(normed_own, at + 1), window), at + 1))
         if at == 0:
             beside.append(dot(after(normed, window), outgate_weight))
         got, *beside = join(got, *beside)
         counts.append(beside[0])
-        normed_got.extend(beside[1:2])
-        outgates.extend(beside[2:])
+        outgates.extend(beside[1:])
         return (got,)
 
     state_in = carry(window, 1, with_forward)
-    outgate, valid_count = outgates[0], counts[-1][0:1, 0:1]
-    for by in range(len(normed_got) + 1, turns):
-        normed_got.append(turn(cut(normed_own, by), by))
+    outgate, valid_count = outgates[0], counts[-1]
     gain_row = outnorm_gain.reshape(1, DV)
     second_row = second_gain.reshape(1, D)
-    input_own = own(block_input)
-    valid_own = own(valid_float)[:, None]
-    teacher_own, cotangent_own = own(teacher), own(cotangent)
+    first_row = first_gain.reshape(1, D)
+    valid_row = valid_float.reshape(1, length)
+    steps = [("seq", bit) for bit in (1 << p for p in range(16)) if bit < places]
     gated, mixed, scores, sent, kept = run(
         output_kernel,
         [u, v, x, start_row, state_in, outgate, gain_row, output_weight],
@@ -821,18 +958,18 @@
     far, turned = join(far, gated)
     far, gated_1 = join(flip(far, "head", 2), turn(turned, 1))
     hidden, ffn_own = run(
-        hidden_kernel, [near, far, input_own, second_row], [(row_shape, F32), (row_shape, BF16)]
+        hidden_kernel, [near, far, block_input, second_row], [(row_shape, F32), (row_shape, BF16)]
     )
     ffn_side, ffn_1 = join(flip(ffn_own, "head", 2), turn(ffn_own, 1))
     ffn_in = quarters(ffn_own, ffn_side)
-    activated, gate_in, up_in, ffn_cut = run(*gate_up(pair, ffn_in, gate_weight, up_weight, BF16))
+    activated, gate_in, up_in = run(*gate_up(ffn_in, gate_weight, up_weight))
     sent, kept = run(*rows_times([activated], [(0, 0, hidden_units, down_weight)]))
     near, far = fold(sent, kept)
     far, turned = join(far, ffn_1)
     far, ffn_2 = join(flip(far, "head", 2), turn(turned, 1))
     output_own, d_out, d_ffn_own, squared = run(
         functools.partial(loss_kernel, loss_weight),
-        [near, far, hidden, teacher_own, cotangent_own, valid_own, valid_count],
+        [near, far, hidden, teacher, cotangent, valid_row, valid_count],
         [(row_shape, BF16), (row_shape, F32), (row_shape, BF16), ((1, 1), F32)],
     )
     d_ffn_own, turned, turned_too = join(d_ffn_own, ffn_2, gated_1)
@@ -840,7 +977,9 @@
         flip(d_ffn_own, "head", 2), turn(turned, 1), turn(turned_too, 1)
     )
     d_ffn = quarters(d_ffn_own, d_ffn_side)
-    d_gate, d_up, d_ffn_cut = run(*gate_back_rows(pair, d_ffn, down_weight, gate_in, up_in))
+    d_gate, d_up = run(*gate_back_rows(d_ffn, down_weight, gate_in, up_in))
+    ffn_turns = [ffn_own, *finish([ffn_1, ffn_2, ffn_3])]
+    (ffn_far,) = run(stack_kernel, ffn_turns[1:], [(((turns - 1) * quarter, D), BF16)])
     sent, kept = run(
         *rows_times(
             [d_gate, d_up],
@@ -850,68 +989,63 @@
     near, far = fold(sent, kept)
     far, turned = join(far, d_ffn_own)
     far, d_1 = join(flip(far, "head", 2), turn(turned, 1))
-    d_hidden, d_branch_own, second_part = run(
-        hidden_back_kernel,
-        [near, far, hidden, d_out, second_row],
-        [(row_shape, F32), (row_shape, BF16), ((1, D), F32)],
+    d_hidden, d_branch_own, second_part, *cuts = run(
+        functools.partial(hidden_back_kernel, turns),
+        [near, far, hidden, d_out, second_row, normed],
+        [(row_shape, F32), (row_shape, BF16), ((1, D), F32)]
+        + [((quarter, 2 * pair), BF16)] * (turns - 1),
     )
     d_branch_own, turned, turned_too = join(d_branch_own, d_1, gated_2)
     d_branch_side, d_2, gated_3 = join(
         flip(d_branch_own, "head", 2), turn(turned, 1), turn(turned_too, 1)
     )
+    gated_turns = finish([gated_1, gated_2, gated_3])
     d_branch = quarters(d_branch_own, d_branch_side)
 
-    d_outgate, d_mixed, outnorm_part, direct, branch_cut = run(
+    d_outgate, d_mixed, outnorm_part, direct = run(
         gate_back_kernel,
         [*d_branch, output_weight, mixed, outgate, gain_row, u, x, start_row],
-        [
-            ((length, DV), BF16),
-            ((length, DV), BF16),
-            ((1, DV), F32),
-            (window_shape, BF16),
-            ((length, pair), BF16),
-        ],
+        [((length, DV), BF16), ((length, DV), BF16), ((1, DV), F32), (window_shape, BF16)],
         [((length, D), BF16)],
     )
-
-    made, grads = [], []
-
-    def far_forward(own_rows, side_rows):
-        made.append(run(*gate_up(pair, quarters(own_rows, side_rows), gate_weight, up_weight, BF16)))
-
-    def far_back(own_rows, side_rows):
-        part = made[len(grads)]
-        pieces = quarters(own_rows, side_rows)
-        grads.append(run(*gate_back_rows(pair, pieces, down_weight, part[1], part[2])))
-
-    ffn_turns, d_turns = finish([ffn_1, ffn_2, ffn_3]), [d_1, d_2]
-    gated_turns = finish([gated_1, gated_2, gated_3])
-    ffn_sides, d_sides, outgate_turns, branch_got, sums = [], [], [], [], {}
+    (d_far,) = run(stack_kernel, [d_1, d_2], [((half, D), BF16)])
+
+    d_turns, d_sides, cuts_got, outgate_turns = [d_ffn_own, d_1, d_2], [d_ffn_side], [], []
+    made, grads, sums, held = [], [], {}, {}
 
     def weigh(name, lefts, rights):
-        sums[name] = run(*weight_args("cuts", share, lefts, rights), vmem=8)
+        sums[name] = run(*far_weight(share, lefts, rights))
 
     def with_back(at, step, got, window):
         if at == 0:
-            ffn_sides.extend(flip(after(r, window), "head", 2) for r in (ffn_1, ffn_2))
-            d_turns.append(turn(after(d_2, window), 1))
-            hold(*ffn_sides, d_turns[2])
+            got, third, sides = join(
+                got, turn(after(d_2, window), 1), flip(after(ffn_far, d_branch_side), "head", 2)
+            )
+            d_turns.append(third)
+            held["ffn"] = sides
         elif at == 1:
-            ffn_sides.append(flip(after(ffn_3, window), "head", 2))
-            d_sides.append(flip(after(d_1, window), "head", 2))
-            outgate_turns.append(turn(after(d_outgate, window), 1))
-            far_forward(ffn_1, ffn_sides[0])
-            far_forward(ffn_2, ffn_sides[1])
-            hold(ffn_sides[2], *d_sides, *outgate_turns)
+            sides = flip(after(d_far, window), "head", 2)
+            right = turn(after(d_outgate, window), 1)
+            made.append(
+                run(
+                    *far_gate_up(ffn_turns, [ffn_side, held["ffn"]], gate_weight, up_weight, pair),
+                    vmem=roomy,
+                )
+            )
+            got, sides, right = join(got, sides, right)
+            d_sides.append(sides)
+            outgate_turns.append(right)
         elif at == 2:
-            d_sides.extend(flip(after(r, window), "head", 2) for r in (d_2, d_turns[2]))
-            outgate_turns.append(turn(after(outgate_turns[-1], window), 1))
-            branch_got.extend(
-                turn(after(cut(d_branch_own, by), window), by) for by in range(1, turns)
-            )
-            far_forward(ffn_3, ffn_sides[2])
-            far_back(d_1, d_sides[0])
-            hold(*d_sides[1:], outgate_turns[-1], *branch_got)
+            side = flip(after(d_turns[3], window), "head", 2)
+            other = flip(after(made[0][4], window), "head", 1)
+            made.append(run(*gate_up([other], gate_weight, up_weight, pair), vmem=roomy))
+            right = turn(after(outgate_turns[-1], made[1][3]), 1)
+            got, side, right = join(got, side, right)
+            d_sides.append(side)
+            outgate_turns.append(right)
+            for extra in range(4, turns):
+                d_turns.append(turn(d_turns[-1], 1))
+                d_sides.append(flip(d_turns[-1], "head", 2))
         return (got,)
 
     later = carry(direct, -1, with_back)
@@ -937,23 +1071,38 @@
         vmem=7,
     )
 
-    from_next = shift(back_rows, "seq", -1)
-    outgate_turns.append(turn(after(outgate_turns[-1], back_rows), 1))
-    far_back(d_2, d_sides[1])
-    far_back(d_turns[2], d_sides[2])
-    finish(d_turns)
-    for extra in range(3, turns - 1):
-        far_forward(ffn_turns[extra], flip(ffn_turns[extra], "head", 2))
-        far_back(d_turns[extra], flip(d_turns[extra], "head", 2))
-    hold(outgate_turns[-1])
-    fixed = (last_rows + from_next * tail_keep[:, None]).astype(BF16)
-    d_pre = lax.dynamic_update_slice(d_pre, fixed, ((mine ^ 3) * quarter + quarter - 8, 0))
+    grads.append(
+        run(
+            *far_back_rows(d_turns, d_sides, down_weight, made[0][1], made[0][2], pair), vmem=roomy
+        )
+    )
+    from_next, d_low_got, right, rows_other = join(
+        shift(back_rows, "seq", -1),
+        flip(d_low, "head", 1),
+        turn(after(outgate_turns[-1], back_rows), 1),
+        flip(grads[0][3], "head", 1),
+    )
+    outgate_turns = finish([*outgate_turns, right])
+    hold(from_next)
+    (d_pre,) = run(
+        edge_kernel, [d_pre, last_rows, from_next, tail_keep[:, None]], [((length, channels), BF16)]
+    )
 
     pre_1 = turn(d_pre, 1)
-
-    def across(sums, *gates):
-        return sums[0], flip(after(sums[0], *gates), "seq", 1), sums[1]
-
+    cuts_got = [turn(after(cuts[by - 1], d_pre), by) for by in range(1, turns)]
+    d_low = d_low + d_low_got
+    grads.append(
+        run(*gate_back_rows([rows_other], down_weight, made[1][1], made[1][2], pair), vmem=roomy)
+    )
+    cuts_in = [part[3] for part in made]
+    weigh("gate", cuts_in, [grad[0] for grad in grads])
+    pre_1, gate_sent, d_low_got, *cuts_got = join(
+        pre_1, sums["gate"][0], flip(d_low, "head", 2), *cuts_got
+    )
+
+    pre_2 = turn(pre_1, 1)
+    gate_got = flip(gate_sent, "seq", 1)
+    hold(pre_1)
     sent, kept = run(
         *rows_times(
             [d_outgate, d_pre],
@@ -965,66 +1114,79 @@
             ],
         )
     )
-    d_low = after(d_low, *waiting)
     near, far = fold(sent, kept)
     far = flip(far, "head", 2)
-    d_lowrank = total(d_low, [("head", 1), ("head", 2)]).astype(BF16)
-    low_own = lax.dynamic_slice_in_dim(d_lowrank, mine * quarter, quarter, 1)
-    cuts = [ffn_cut, *(f[3] for f in made)]
-    weigh("gate", cuts, [d_gate, *(g[0] for g in grads)])
-    moved_gate = across(sums["gate"])
-    weigh("up", cuts, [d_up, *(g[1] for g in grads)])
-    moved_up = across(sums["up"])
-    hold(pre_1)
-    grad_own, first_part = run(
+    weigh("up", cuts_in, [grad[1] for grad in grads])
+    weigh("down", [grad[2] for grad in grads], [part[0] for part in made])
+    (cuts_near,) = run(stack_kernel, cuts_got, [(((turns - 1) * quarter, 2 * pair), BF16)])
+    cuts_side = flip(cuts_near, "head", 2)
+    grad_own, first_part, d_lowrank = run(
         input_back_kernel,
-        [near, far, input_own, d_hidden, first_gain.reshape(1, D), low_own, lowrank_down.T],
-        [(row_shape, BF16), ((1, D), F32)],
-    )
-    pre_2 = turn(ready(pre_1), 1)
-    weigh("down", [d_ffn_cut, *(g[2] for g in grads)], [activated, *(f[0] for f in made)])
-    moved_down = across(sums["down"])
-    branch_near = after(jnp.concatenate(branch_got, axis=0), grad_own)
-    branch_far = quarters(branch_near, flip(branch_near, "head", 2))
-    normed_near = after(jnp.concatenate(normed_got, axis=0), grad_own)
-    normed_far = quarters(normed_near, flip(normed_near, "head", 2))
-    grad_side = flip(after(grad_own, branch_near), "head", 2)
-    sum_output = run(*weight_args("stacked", share, [branch_cut, *branch_far], [gated, *gated_turns]))
-    sum_outgate = run(
-        *weight_args("natural", share, [normed, *normed_far], [d_outgate, *finish(outgate_turns)])
-    )
-    (apart,) = run(low_kernel, [d_lowrank, normed, pack], [((RANK + 8, D), F32)])
-    odd = jnp.concatenate(
-        [outnorm_part, jnp.broadcast_to(squared, (1, DV)), jnp.zeros((1, D - 2 * DV), F32)], axis=1
-    )
-    shared = jnp.concatenate([first_part, second_part, odd], axis=0)
-    upper = [("seq", bit) for bit in (1 << p for p in range(1, 16)) if bit < places]
-    hold(pre_2, grad_side, moved_gate[1])
-    (grad_input,) = run(natural_kernel, quarters(grad_own, grad_side), [((length, D), F32)])
-    pre_3 = turn(ready(pre_2), 1)
-    moved_output, moved_outgate = across(sum_output, pre_2), across(sum_outgate, pre_2)
-    output_later = after(output_own, pre_2)
-    output_side = flip(output_later, "head", 2)
-    shared = total(after(shared, pre_2), [("head", 1), ("head", 2)])
-    apart = total(after(apart, pre_2), upper, BF16)
-    hold(moved_up[1])
-    (block_output,) = run(natural_kernel, quarters(output_later, output_side), [((length, D), F32)])
+        [near, far, block_input, d_hidden, first_row, d_low, d_low_got, lowrank_down.T],
+        [(row_shape, BF16), ((1, D), F32), ((RANK, length), BF16)],
+    )
+    (small,) = run(
+        low_kernel,
+        [d_lowrank, normed, pack, first_part, second_part, outnorm_part, squared],
+        [((RANK + 8, D), F32)],
+    )
+    (rows_both,) = run(stack_kernel, [grad_own, output_own], [((half, D), BF16)])
+    pre_2, gate_got, small, rows_both, up_sent, down_sent, cuts_near, cuts_side = join(
+        pre_2, gate_got, small, rows_both, sums["up"][0], sums["down"][0], cuts_near, cuts_side
+    )
+
+    pre_3 = turn(pre_2, 1)
+    cuts_far = quarters(cuts_near, cuts_side)
+    shared = total(small[RANK + 5 :], [("head", 1), ("head", 2)])
+    up_got = flip(up_sent, "seq", 1)
+    rows_side = flip(rows_both, "head", 2)
+    sum_both = run(
+        *zone_weight(
+            both_kernel, turns, share, length, 2 * DV,
+            [*d_branch, normed, *cuts_far, d_outgate, gated, *outgate_turns, *gated_turns],
+        )
+    )
+    pre_3, up_got, rows_side, shared, both_sent, rows_both, down_sent = join(
+        pre_3, up_got, rows_side, shared, sum_both[0], rows_both, down_sent
+    )
+    small = jnp.concatenate([small[: RANK + 5], shared], axis=0)
+    small = total(after(small, pre_3), steps[:1])
+    down_got, both_got = flip(down_sent, "seq", 1), flip(both_sent, "seq", 1)
     sum_pre = run(
-        *weight_args(
-            "natural", share, [normed, *normed_far], [d_pre, *finish([pre_1, pre_2, pre_3])]
+        *zone_weight(
+            pre_kernel, turns, share, length, channels,
+            [normed, *cuts_far, d_pre, *finish([pre_1, pre_2, pre_3])],
         )
     )
-    moved_pre = flip(sum_pre[0], "seq", 1)
-    shared = total(after(shared, sum_pre[0]), [*upper, ("seq", 1)])
-    apart = total(after(apart, sum_pre[0]), [("seq", 1)], BF16)
-    grad_gate, grad_up, grad_down, grad_output, grad_outgate = (
-        kept + after(got, sum_pre[0]).astype(F32)
-        for _, got, kept in (moved_gate, moved_up, moved_down, moved_output, moved_outgate)
-    )
+    pre_got = flip(sum_pre[0], "seq", 1)
+    small = total(after(small, sum_pre[0]), steps[1:])
+    shared = small[RANK + 5 :]
     grad_query, grad_key, grad_value = run(
-        settle_kernel, [sum_pre[1], moved_pre],
+        settle_kernel, [sum_pre[1], pre_got],
         [((share, DK), F32), ((share, DK), F32), ((share, DV), F32)],
     )
+    both_other, side_other = flip(rows_both, "head", 1), flip(rows_side, "head", 1)
+    (grad_input,) = run(
+        functools.partial(natural_kernel, 0),
+        [rows_both, rows_side, both_other, side_other],
+        [((length, D), F32)],
+    )
+    (block_output,) = run(
+        functools.partial(natural_kernel, quarter),
+        [rows_both, rows_side, both_other, side_other],
+        [((length, D), F32)],
+    )
+    grad_gate, grad_up, grad_down, grad_both = (
+        after(kept, sum_pre[0]) + got.astype(F32)
+        for got, kept in (
+            (gate_got, sums["gate"][1]),
+            (up_got, sums["up"][1]),
+            (down_got, sums["down"][1]),
+            (both_got, sum_both[1]),
+        )
+    )
+    grad_output, grad_outgate = grad_both[:, :DV], grad_both[:, DV:]
+    apart = small
     taps_query, taps_key, taps_value, grad_lowrank_up, bias_row, down_row = run(
         functools.partial(unpack_kernel, share),
         [apart],

time: 398 us -> 370 us (0.930)
  local copies, waits for them, and re-layouts: 37.5 us -> 17.1 us
  starting transfers between devices: 88.6 us -> 72.7 us
  waiting for transfers between devices: 159 us -> 171 us
  other arithmetic: 13.8 us -> 8.57 us
  Pallas kernels: 81.1 us -> 85.1 us
    ppermute x66 -> x43, waiting for transfers between devices: 74.3 us -> 90.5 us  [flip(): return lax.ppermute(x, axis, [(i, i ^ bit) for i in range(n)])]
    unnamed x320 -> x184, local copies, waits for them, and re-layouts: 28.4 us -> 12.5 us
    ppermute x21 -> x18, waiting for transfers between devices: 80.1 us -> 66 us  [turn(): return lax.ppermute(x, 'seq', [(i, (i + 2 * by) % n) for i in range(n)])]
    ppermute x21 -> x18, starting transfers between devices: 29.9 us -> 16.3 us  [turn(): return lax.ppermute(x, 'seq', [(i, (i + 2 * by) % n) for i in range(n)])]
    ppermute x8, waiting for transfers between devices: 5.06 us -> 14.9 us  [shift(): lax.ppermute(x, axis, [(i, i + by) for i in range(n) if 0 <= i + by < n])]
    ppermute x66 -> x43, starting transfers between devices: 36.2 us -> 30.3 us  [flip(): return lax.ppermute(x, axis, [(i, i ^ bit) for i in range(n)])]
    pallas_call x40 -> x42, Pallas kernels: 81.1 us -> 85.1 us  [call(): pl.pallas_call(body, out_shape=[jax.ShapeDtypeStruct(shape, kind) for sha...]
  transfers between devices with their start and end apart: 95 -> 69, of which waited for: 45 -> 47; matrix products, arithmetic and copies ran while one was open for 5% -> 2% of each run, Pallas kernels for 12% -> 13%
where the time goes in v3:
time: 370 us; the launch traced here: 364 us
  waiting for transfers between devices  171 us (46%)
  Pallas kernels  85.1 us (23%)
  starting transfers between devices  72.7 us (20%)
  local copies, waits for them, and re-layouts  17.1 us (5%)
  other arithmetic  8.57 us (2%)
  between operations  6.42 us (2%)
    ppermute x43, waiting for transfers between devices, flip(): return lax.ppermute(x, axis, [(i, i ^ bit) for i in range(n)])  90.5 us
    pallas_call x42, Pallas kernels, call(): pl.pallas_call(body, out_shape=[jax.ShapeDtypeStruct(shape, kind) for sha...  85.1 us
    ppermute x18, waiting for transfers between devices, turn(): return lax.ppermute(x, 'seq', [(i, (i + 2 * by) % n) for i in range(n)])  66 us
    ppermute x43, starting transfers between devices, flip(): return lax.ppermute(x, axis, [(i, i ^ bit) for i in range(n)])  30.3 us
    ppermute x8, starting transfers between devices, shift(): lax.ppermute(x, axis, [(i, i + by) for i in range(n) if 0 <= i + by < n])  26.1 us
    ppermute x18, starting transfers between devices, turn(): return lax.ppermute(x, 'seq', [(i, (i + 2 * by) % n) for i in range(n)])  16.3 us
    ppermute x8, waiting for transfers between devices, shift(): lax.ppermute(x, axis, [(i, i + by) for i in range(n) if 0 <= i + by < n])  14.9 us
    unnamed x184, local copies, waits for them, and re-layouts  12.5 us
  transfers between devices with their start and end apart: 69, of which 47 were waited for; matrix products, arithmetic and copies ran while one was open for 2% of the time, Pallas kernels for 13%

profile of v3, /device:TPU:0, one launch (start us, length us, event | category | flops | bytes accessed | tf_op | source)
XLA Modules:
  0.0 364.0 jit_solution(7337940989940315321)
XLA Ops:
  9.6 4.8 %collective-permute-start = (bf16[8,1024]{1,0:T(8,128)(2,1)S(1)}, bf16[8,1024]{1,0:T(8,128)(2,1)S(1)}, u32[]{:S(2)}, u32[]{:S(2)}) collective-permute-start(bf16[8,1024]{1,0:T(8,128)(2,1)S(1)} %maximum_multiply_fusion), channel_id=1, source_target_pairs={{0,4},{4,8},{8,12},{12,16},{16,20},{20,24},{24,28},{1,5},{5,9},{9,... | collective-permute-start | bytes 49160 | tf_op jit(solution)/shard_map/ppermute | solution.py:57
  19.2 4.2 %collective-permute-start.1 = (bf16[272,512]{1,0:T(8,128)(2,1)S(1)}, bf16[272,512]{1,0:T(8,128)(2,1)S(1)}, u32[]{:S(2)}, u32[]{:S(2)}) collective-permute-start(bf16[272,512]{1,0:T(8,128)(2,1)S(1)} %get-tuple-element.245.refs_0_), channel_id=1, source_target_pairs={{0,4},{4,8},{8,12},{12,16},{16,20},{20,24},{24,28},{1,5},{5,9},{9,... | collective-permute-start | bytes 835592 | tf_op jit(solution)/shard_map/ppermute | solution.py:57
  29.0 6.3 %collective-permute-start.3 = (bf16[272,512]{1,0:T(8,128)(2,1)S(1)}, bf16[272,512]{1,0:T(8,128)(2,1)S(1)}, u32[]{:S(2)}, u32[]{:S(2)}) collective-permute-start(bf16[272,512]{1,0:T(8,128)(2,1)S(1)} %get-tuple-element.252.refs_0_), channel_id=1, source_target_pairs={{0,8},{4,12},{8,16},{12,20},{16,24},{20,28},{1,9},{5,13},{9,17},{1... | collective-permute-start | bytes 835592 | tf_op jit(solution)/shard_map/ppermute | solution.py:57
  40.1 5.5 %collective-permute-start.5 = (bf16[272,512]{1,0:T(8,128)(2,1)S(1)}, bf16[272,512]{1,0:T(8,128)(2,1)S(1)}, u32[]{:S(2)}, u32[]{:S(2)}) collective-permute-start(bf16[272,512]{1,0:T(8,128)(2,1)S(1)} %get-tuple-element.258), channel_id=1, source_target_pairs={{0,16},{4,20},{8,24},{12,28},{1,17},{5,21},{9,25},{13,29},{2,18},{... | collective-permute-start | bytes 835592 | tf_op jit(solution)/shard_map/ppermute | solution.py:57
  45.7 4.5 %collective-permute-done.6 = f32[8,128]{1,0:T(8,128)S(1)} collective-permute-done((f32[8,128]{1,0:T(8,128)S(1)}, f32[8,128]{1,0:T(8,128)S(1)}, u32[]{:S(2)}, u32[]{:S(2)}) %collective-permute-start.6) | collective-permute-done | bytes 4128 | tf_op jit(solution)/shard_map/ppermute | solution.py:52
  57.2 5.6 %collective-permute-start.9 = (bf16[256,512]{1,0:T(8,128)(2,1)S(1)}, bf16[256,512]{1,0:T(8,128)(2,1)S(1)}, u32[]{:S(2)}, u32[]{:S(2)}) collective-permute-start(bf16[256,512]{1,0:T(8,128)(2,1)S(1)} %get-tuple-element.275.refs_10_), channel_id=1, source_target_pairs={{0,8},{4,12},{8,16},{12,20},{16,24},{20,28},{24,0},{28,4},{1,9},{5... | collective-permute-start | bytes 786440 | tf_op jit(solution)/shard_map/ppermute | solution.py:62
  64.0 7.9 %collective-permute-done.9.refs_14_ = bf16[256,512]{1,0:T(8,128)(2,1)S(1)} collective-permute-done((bf16[256,512]{1,0:T(8,128)(2,1)S(1)}, bf16[256,512]{1,0:T(8,128)(2,1)S(1)}, u32[]{:S(2)}, u32[]{:S(2)}) %collective-permute-start.9) | collective-permute-done | bytes 262176 | tf_op jit(solution)/shard_map/ppermute | solution.py:62
  73.8 6.5 %collective-permute-done.10.refs_1_.refs_4_ = bf16[64,2048]{1,0:T(8,128)(2,1)S(1)} collective-permute-done((bf16[64,2048]{1,0:T(8,128)(2,1)S(1)}, bf16[64,2048]{1,0:T(8,128)(2,1)S(1)}, u32[]{:S(2)}, u32[]{:S(2)}) %collective-permute-start.10) | collective-permute-done | bytes 262176 | tf_op jit(solution)/shard_map/ppermute | solution.py:52
  84.4 4.0 %shard_map.372 = (bf16[256,1408]{1,0:T(8,128)(2,1)S(1)}, bf16[256,1408]{1,0:T(8,128)(2,1)S(1)}, bf16[256,1408]{1,0:T(8,128)(2,1)S(1)}) custom-call(s32[3]{0:T(128)S(1)} %pad_add_fusion.place, bf16[64,2048]{1,0:T(8,128)(2,1)S(1)} %get-tuple-element.277.refs_0_, bf16[64,2048]{1,0:T(8,128)(2,1)S(1)} %collective-permute-done.10.refs_1_.refs_4_, ...), custom_call_target="tpu_custom_call" | custom-call | flops 5000000000 | bytes 15000000 | tf_op jit(solution)/shard_map/pallas_call | solution.py:375
  95.1 6.8 %collective-permute-done.15.got = bf16[64,2048]{1,0:T(8,128)(2,1)S(1)} collective-permute-done((bf16[64,2048]{1,0:T(8,128)(2,1)S(1)}, bf16[64,2048]{1,0:T(8,128)(2,1)S(1)}, u32[]{:S(2)}, u32[]{:S(2)}) %collective-permute-start.15) | collective-permute-done | bytes 262176 | tf_op jit(solution)/shard_map/ppermute | solution.py:52
  107.0 6.6 %collective-permute-done.17.refs_1_.refs_4_ = bf16[64,2048]{1,0:T(8,128)(2,1)S(1)} collective-permute-done((bf16[64,2048]{1,0:T(8,128)(2,1)S(1)}, bf16[64,2048]{1,0:T(8,128)(2,1)S(1)}, u32[]{:S(2)}, u32[]{:S(2)}) %collective-permute-start.17) | collective-permute-done | bytes 262176 | tf_op jit(solution)/shard_map/ppermute | solution.py:52
  113.6 4.3 %collective-permute-done.18.refs_2_.refs_3_ = bf16[64,2048]{1,0:T(8,128)(2,1)S(1)} collective-permute-done((bf16[64,2048]{1,0:T(8,128)(2,1)S(1)}, bf16[64,2048]{1,0:T(8,128)(2,1)S(1)}, u32[]{:S(2)}, u32[]{:S(2)}) %collective-permute-start.18) | collective-permute-done | bytes 262176 | tf_op jit(solution)/shard_map/ppermute | solution.py:62
  125.8 4.0 %shard_map.378 = (bf16[128,2048]{1,0:T(8,128)(2,1)S(1)}, f32[128,2048]{1,0:T(8,128)S(1)}) custom-call(s32[3]{0:T(128)S(1)} %pad_add_fusion.place, bf16[256,1408]{1,0:T(8,128)(2,1)S(1)} %get-tuple-element.309.refs_0_, bf16[256,1408]{1,0:T(8,128)(2,1)S(1)} %get-tuple-element.305.refs_1_, bf16[2048,1408]{1,0:T(8,128)(2,1)S(1)} %bitcast.31, ...), custom_call_target="tpu_custom_call" | custom-call | flops 2800000000 | bytes 8400000 | tf_op jit(solution)/shard_map/pallas_call | solution.py:375
  134.0 6.8 %collective-permute-done.23.got = bf16[64,2048]{1,0:T(8,128)(2,1)S(1)} collective-permute-done((bf16[64,2048]{1,0:T(8,128)(2,1)S(1)}, bf16[64,2048]{1,0:T(8,128)(2,1)S(1)}, u32[]{:S(2)}, u32[]{:S(2)}) %collective-permute-start.23) | collective-permute-done | bytes 262176 | tf_op jit(solution)/shard_map/ppermute | solution.py:52
  147.6 6.5 %collective-permute-done.25.branch_1.refs_1_ = bf16[64,2048]{1,0:T(8,128)(2,1)S(1)} collective-permute-done((bf16[64,2048]{1,0:T(8,128)(2,1)S(1)}, bf16[64,2048]{1,0:T(8,128)(2,1)S(1)}, u32[]{:S(2)}, u32[]{:S(2)}) %collective-permute-start.25) | collective-permute-done | bytes 262176 | tf_op jit(solution)/shard_map/ppermute | solution.py:52
  154.1 4.3 %collective-permute-done.26.refs_1_.refs_2_ = bf16[64,2048]{1,0:T(8,128)(2,1)S(1)} collective-permute-done((bf16[64,2048]{1,0:T(8,128)(2,1)S(1)}, bf16[64,2048]{1,0:T(8,128)(2,1)S(1)}, u32[]{:S(2)}, u32[]{:S(2)}) %collective-permute-start.26) | collective-permute-done | bytes 262176 | tf_op jit(solution)/shard_map/ppermute | solution.py:62
  171.0 10.3 %collective-permute-done.31.refs_3_ = bf16[64,2048]{1,0:T(8,128)(2,1)S(1)} collective-permute-done((bf16[64,2048]{1,0:T(8,128)(2,1)S(1)}, bf16[64,2048]{1,0:T(8,128)(2,1)S(1)}, u32[]{:S(2)}, u32[]{:S(2)}) %collective-permute-start.31) | collective-permute-done | bytes 262176 | tf_op jit(solution)/shard_map/ppermute | solution.py:62
  186.6 7.5 %shard_map.384 = (bf16[512,1408]{1,0:T(8,128)(2,1)S(1)}, bf16[512,1408]{1,0:T(8,128)(2,1)S(1)}, bf16[512,1408]{1,0:T(8,128)(2,1)S(1)}, bf16[512,512]{1,0:T(8,128)(2,1)S(1)}, bf16[512,2048]{1,0:T(8,128)(2,1)S(1)}) custom-call(s32[3]{0:T(128)S(1)} %pad_add_fusion.place, bf16[64,2048]{1,0:T(8,128)(2,1)S(1)} %get-tuple-element.277.refs_0_, ...), custom_call_target="tpu_custom_call" | custom-call | flops 1000000000 | bytes 3000000 | tf_op jit(solution)/shard_map/pallas_call | solution.py:375
  202.9 7.5 %shard_map.386 = (bf16[512,1408]{1,0:T(8,128)(2,1)S(1)}, bf16[512,1408]{1,0:T(8,128)(2,1)S(1)}, bf16[512,1408]{1,0:T(8,128)(2,1)S(1)}, bf16[512,512]{1,0:T(8,128)(2,1)S(1)}) custom-call(s32[3]{0:T(128)S(1)} %pad_add_fusion.place, bf16[512,2048]{1,0:T(8,128)(2,1)S(1)} %collective-permute-done.36.refs_0_, bf16[2048,1408]{1,0:T(8,128)(2,1)S(1)} %bitcast.31, ...), custom_call_target="tpu_custom_call" | custom-call | flops 5000000000 | bytes 15000000 | tf_op jit(solution)/shard_map/pallas_call | solution.py:375
  212.3 9.8 %collective-permute-done.37.got = bf16[272,512]{1,0:T(8,128)(2,1)S(1)} collective-permute-done((bf16[272,512]{1,0:T(8,128)(2,1)S(1)}, bf16[272,512]{1,0:T(8,128)(2,1)S(1)}, u32[]{:S(2)}, u32[]{:S(2)}) %collective-permute-start.37) | collective-permute-done | bytes 278560 | tf_op jit(solution)/shard_map/ppermute | solution.py:57
  222.9 4.2 %shard_map.388 = (bf16[256,1024]{1,0:T(8,128)(2,1)S(1)}, f32[8,1024]{1,0:T(8,128)S(1)}, f32[8,2048]{1,0:T(8,128)S(1)}, f32[16,256]{1,0:T(8,128)S(1)}, f32[8,1024]{1,0:T(8,128)S(1)}) custom-call(s32[3]{0:T(128)S(1)} %pad_add_fusion.place, bf16[256,512]{1,0:T(8,128)(2,1)S(1)} %get-tuple-element.359.d_mixed, bf16[256,512]{1,0:T(8,128)(2,1)S(1)} %shard_map.368.state_in, ...), custom_call_target="tpu_custom_call" | custom-call | flops 4499999744 | bytes 13500000 | tf_op jit(solution)/shard_map/pallas_call | solution.py:375
  227.2 4.3 %shard_map.389 = (bf16[512,1408]{1,0:T(8,128)(2,1)S(1)}, bf16[512,1408]{1,0:T(8,128)(2,1)S(1)}, bf16[512,512]{1,0:T(8,128)(2,1)S(1)}, bf16[512,2048]{1,0:T(8,128)(2,1)}) custom-call(s32[3]{0:T(128)S(1)} %pad_add_fusion.place, bf16[64,2048]{1,0:T(8,128)(2,1)S(1)} %get-tuple-element.317.refs_0_, bf16[64,2048]{1,0:T(8,128)(2,1)S(1)} %collective-permute-done.24.refs_0_.refs_1_, ...), custom_call_target="tpu_custom_call" | custom-call | flops 4000000000 | bytes 12000000 | tf_op jit(solution)/shard_map/pallas_call | solution.py:375
  241.0 4.8 %collective-permute-done.42.refs_13_ = bf16[256,512]{1,0:T(8,128)(2,1)} collective-permute-done((bf16[256,512]{1,0:T(8,128)(2,1)}, bf16[256,512]{1,0:T(8,128)(2,1)}, u32[]{:S(2)}, u32[]{:S(2)}) %collective-permute-start.42) | collective-permute-done | bytes 262176 | tf_op jit(solution)/shard_map/ppermute | solution.py:62
  248.3 3.8 %collective-permute-start.48 = (bf16[64,1024]{1,0:T(8,128)(2,1)}, bf16[64,1024]{1,0:T(8,128)(2,1)S(1)}, u32[]{:S(2)}, u32[]{:S(2)}) collective-permute-start(bf16[64,1024]{1,0:T(8,128)(2,1)} %copy-done.43), channel_id=1, source_target_pairs={{0,24},{4,28},{8,0},{12,4},{16,8},{20,12},{24,16},{28,20},{1,25},{... | collective-permute-start | bytes 393224 | tf_op jit(solution)/shard_map/ppermute | solution.py:62
  256.9 5.3 %shard_map.391 = (bf16[512,1408]{1,0:T(8,128)(2,1)S(1)}, bf16[512,1408]{1,0:T(8,128)(2,1)S(1)}, bf16[512,512]{1,0:T(8,128)(2,1)S(1)}) custom-call(s32[3]{0:T(128)S(1)} %pad_add_fusion.place, bf16[512,2048]{1,0:T(8,128)(2,1)} %collective-permute-done.43.refs_0_, bf16[2048,1408]{1,0:T(8,128)(2,1)S(1)} %copy-done.8, bf16[512,1408]{1,0:T(8,128)(2,1)S(1)} %copy-done.53, ...), custom_call_target="tpu_custom_call" | custom-call | flops 3000000000 | bytes 9000000 | tf_op jit(solution)/shard_map/pallas_call | solution.py:375
  265.5 7.4 %collective-permute-done.47.refs_1_ = bf16[64,1024]{1,0:T(8,128)(2,1)S(1)} collective-permute-done((bf16[64,1024]{1,0:T(8,128)(2,1)}, bf16[64,1024]{1,0:T(8,128)(2,1)S(1)}, u32[]{:S(2)}, u32[]{:S(2)}) %collective-permute-start.47) | collective-permute-done | bytes 131104 | tf_op jit(solution)/shard_map/ppermute | solution.py:62
  300.0 3.5 collective-permute-done.60
  306.6 8.9 %collective-permute-done.56.refs_8_ = bf16[256,1024]{1,0:T(8,128)(2,1)S(1)} collective-permute-done((bf16[256,1024]{1,0:T(8,128)(2,1)S(1)}, bf16[256,1024]{1,0:T(8,128)(2,1)S(1)}, u32[]{:S(2)}, u32[]{:S(2)}) %collective-permute-start.56) | collective-permute-done | bytes 524320 | tf_op jit(solution)/shard_map/ppermute | solution.py:62
  326.0 4.8 %collective-permute-done.65 = f32[24,2048]{1,0:T(8,128)S(1)} collective-permute-done((f32[24,2048]{1,0:T(8,128)S(1)}, f32[24,2048]{1,0:T(8,128)S(1)}, u32[]{:S(2)}, u32[]{:S(2)}) %collective-permute-start.65) | collective-permute-done | bytes 196640 | tf_op jit(solution)/shard_map/ppermute | solution.py:52
  331.5 4.7 %collective-permute-done.61.got = bf16[256,1024]{1,0:T(8,128)(2,1)S(1)} collective-permute-done((bf16[256,1024]{1,0:T(8,128)(2,1)S(1)}, bf16[256,1024]{1,0:T(8,128)(2,1)S(1)}, u32[]{:S(2)}, u32[]{:S(2)}) %collective-permute-start.61) | collective-permute-done | bytes 524320 | tf_op jit(solution)/shard_map/ppermute | solution.py:52
  341.9 5.6 %collective-permute-done.67 = bf16[256,1024]{1,0:T(8,128)(2,1)S(1)} collective-permute-done((bf16[256,1024]{1,0:T(8,128)(2,1)S(1)}, bf16[256,1024]{1,0:T(8,128)(2,1)S(1)}, u32[]{:S(2)}, u32[]{:S(2)}) %collective-permute-start.67) | collective-permute-done | bytes 524320 | tf_op jit(solution)/shard_map/ppermute | solution.py:52
  352.3 9.0 %collective-permute-done.68 = bf16[256,1408]{1,0:T(8,128)(2,1)S(1)} collective-permute-done((bf16[256,1408]{1,0:T(8,128)(2,1)S(1)}, bf16[256,1408]{1,0:T(8,128)(2,1)S(1)}, u32[]{:S(2)}, u32[]{:S(2)}) %collective-permute-start.68) | collective-permute-done | bytes 720928 | tf_op jit(solution)/shard_map/ppermute | solution.py:52
  (376 shorter events, 167.4 us)
Async XLA Ops:
  57.2 14.8 %collective-permute-start.9 = (bf16[256,512]{1,0:T(8,128)(2,1)S(1)}, bf16[256,512]{1,0:T(8,128)(2,1)S(1)}, u32[]{:S(2)}, u32[]{:S(2)}) collective-permute-start(bf16[256,512]{1,0:T(8,128)(2,1)S(1)} %get-tuple-element.275.refs_10_), channel_id=1, source_target_pairs={{0,8},{4,12},{8,16},{12,20},{16,24},{20,28},{24,0},{28,4},{1,9},{5... | collective-permute-start | bytes 786440 | tf_op jit(solution)/shard_map/ppermute | solution.py:62
  106.9 11.0 %collective-permute-start.18 = (bf16[64,2048]{1,0:T(8,128)(2,1)S(1)}, bf16[64,2048]{1,0:T(8,128)(2,1)S(1)}, u32[]{:S(2)}, u32[]{:S(2)}) collective-permute-start(bf16[64,2048]{1,0:T(8,128)(2,1)S(1)} %collective-permute-done.16.refs_1_.refs_2_), channel_id=1, source_target_pairs={{0,8},{4,12},{8,16},{12,20},{16,24},{20,28},{24,0},{28,4},{1,9},{5... | collective-permute-start | bytes 786440 | tf_op jit(solution)/shard_map/ppermute | solution.py:62
  106.9 14.3 %collective-permute-start.19 = (bf16[256,512]{1,0:T(8,128)(2,1)S(1)}, bf16[256,512]{1,0:T(8,128)(2,1)S(1)}, u32[]{:S(2)}, u32[]{:S(2)}) collective-permute-start(bf16[256,512]{1,0:T(8,128)(2,1)S(1)} %collective-permute-done.9.refs_14_), channel_id=1, source_target_pairs={{0,8},{4,12},{8,16},{12,20},{16,24},{20,28},{24,0},{28,4},{1,9},{5... | collective-permute-start | bytes 786440 | tf_op jit(solution)/shard_map/ppermute | solution.py:62
  106.9 14.3 %collective-permute-start.20 = (bf16[64,2048]{1,0:T(8,128)(2,1)S(1)}, bf16[64,2048]{1,0:T(8,128)(2,1)S(1)}, u32[]{:S(2)}, u32[]{:S(2)}) collective-permute-start(bf16[64,2048]{1,0:T(8,128)(2,1)S(1)} %get-tuple-element.317.refs_0_), channel_id=1, source_target_pairs={{0,1},{1,0},{2,3},{3,2},{4,5},{5,4},{6,7},{7,6},{8,9},{9,8},{10,11... | collective-permute-start | bytes 786440 | tf_op jit(solution)/shard_map/ppermute | solution.py:52
  147.4 11.0 %collective-permute-start.26 = (bf16[64,2048]{1,0:T(8,128)(2,1)S(1)}, bf16[64,2048]{1,0:T(8,128)(2,1)S(1)}, u32[]{:S(2)}, u32[]{:S(2)}) collective-permute-start(bf16[64,2048]{1,0:T(8,128)(2,1)S(1)} %collective-permute-done.24.refs_0_.refs_1_), channel_id=1, source_target_pairs={{0,8},{4,12},{8,16},{12,20},{16,24},{20,28},{24,0},{28,4},{1,9},{5... | collective-permute-start | bytes 786440 | tf_op jit(solution)/shard_map/ppermute | solution.py:62
  147.4 14.3 %collective-permute-start.27 = (bf16[256,512]{1,0:T(8,128)(2,1)S(1)}, bf16[256,512]{1,0:T(8,128)(2,1)S(1)}, u32[]{:S(2)}, u32[]{:S(2)}) collective-permute-start(bf16[256,512]{1,0:T(8,128)(2,1)S(1)} %collective-permute-done.19.refs_15_), channel_id=1, source_target_pairs={{0,8},{4,12},{8,16},{12,20},{16,24},{20,28},{24,0},{28,4},{1,9},{5... | collective-permute-start | bytes 786440 | tf_op jit(solution)/shard_map/ppermute | solution.py:62
  161.7 19.6 %collective-permute-start.32 = (bf16[192,2048]{1,0:T(8,128)(2,1)S(1)}, bf16[192,2048]{1,0:T(8,128)(2,1)S(1)}, u32[]{:S(2)}, u32[]{:S(2)}) collective-permute-start(bf16[192,2048]{1,0:T(8,128)(2,1)S(1)} %shard_map.377), channel_id=1, source_target_pairs={{0,2},{1,3},{2,0},{3,1},{4,6},{5,7},{6,4},{7,5},{8,10},{9,11},{10,... | collective-permute-start | bytes 2359304 | tf_op jit(solution)/shard_map/ppermute | solution.py:52
  167.2 14.1 %collective-permute-start.30 = (bf16[272,512]{1,0:T(8,128)(2,1)S(1)}, bf16[272,512]{1,0:T(8,128)(2,1)S(1)}, u32[]{:S(2)}, u32[]{:S(2)}) collective-permute-start(bf16[272,512]{1,0:T(8,128)(2,1)S(1)} %get-tuple-element.330.refs_0_), channel_id=1, source_target_pairs={{4,0},{8,4},{12,8},{16,12},{20,16},{24,20},{28,24},{5,1},{9,5},{13... | collective-permute-start | bytes 835592 | tf_op jit(solution)/shard_map/ppermute | solution.py:57
  168.5 12.8 %collective-permute-start.31 = (bf16[64,2048]{1,0:T(8,128)(2,1)S(1)}, bf16[64,2048]{1,0:T(8,128)(2,1)S(1)}, u32[]{:S(2)}, u32[]{:S(2)}) collective-permute-start(bf16[64,2048]{1,0:T(8,128)(2,1)S(1)} %collective-permute-done.26.refs_1_.refs_2_), channel_id=1, source_target_pairs={{0,8},{4,12},{8,16},{12,20},{16,24},{20,28},{24,0},{28,4},{1,9},{5... | collective-permute-start | bytes 786440 | tf_op jit(solution)/shard_map/ppermute | solution.py:62
  182.0 15.9 %collective-permute-start.34 = (bf16[128,2048]{1,0:T(8,128)(2,1)S(1)}, bf16[128,2048]{1,0:T(8,128)(2,1)S(1)}, u32[]{:S(2)}, u32[]{:S(2)}) collective-permute-start(bf16[128,2048]{1,0:T(8,128)(2,1)S(1)} %shard_map.382), channel_id=1, source_target_pairs={{0,2},{1,3},{2,0},{3,1},{4,6},{5,7},{6,4},{7,5},{8,10},{9,11},{10,... | collective-permute-start | bytes 1572872 | tf_op jit(solution)/shard_map/ppermute | solution.py:52
  182.6 15.3 %collective-permute-start.33 = (bf16[272,512]{1,0:T(8,128)(2,1)S(1)}, bf16[272,512]{1,0:T(8,128)(2,1)S(1)}, u32[]{:S(2)}, u32[]{:S(2)}) collective-permute-start(bf16[272,512]{1,0:T(8,128)(2,1)S(1)} %get-tuple-element.342.refs_0_), channel_id=1, source_target_pairs={{8,0},{12,4},{16,8},{20,12},{24,16},{28,20},{9,1},{13,5},{17,9},{2... | collective-permute-start | bytes 835592 | tf_op jit(solution)/shard_map/ppermute | solution.py:57
  183.9 11.3 %collective-permute-start.35 = (bf16[256,512]{1,0:T(8,128)(2,1)S(1)}, bf16[256,512]{1,0:T(8,128)(2,1)S(1)}, u32[]{:S(2)}, u32[]{:S(2)}) collective-permute-start(bf16[256,512]{1,0:T(8,128)(2,1)S(1)} %get-tuple-element.345.refs_0_.refs_9_), channel_id=1, source_target_pairs={{0,8},{4,12},{8,16},{12,20},{16,24},{20,28},{24,0},{28,4},{1,9},{5... | collective-permute-start | bytes 786440 | tf_op jit(solution)/shard_map/ppermute | solution.py:62
  198.7 23.4 %collective-permute-start.37 = (bf16[272,512]{1,0:T(8,128)(2,1)S(1)}, bf16[272,512]{1,0:T(8,128)(2,1)S(1)}, u32[]{:S(2)}, u32[]{:S(2)}) collective-permute-start(bf16[272,512]{1,0:T(8,128)(2,1)S(1)} %get-tuple-element.349), channel_id=1, source_target_pairs={{16,0},{20,4},{24,8},{28,12},{17,1},{21,5},{25,9},{29,13},{18,2},{... | collective-permute-start | bytes 835592 | tf_op jit(solution)/shard_map/ppermute | solution.py:57
  200.0 12.3 %collective-permute-start.38 = (bf16[64,2048]{1,0:T(8,128)(2,1)S(1)}, bf16[64,2048]{1,0:T(8,128)(2,1)S(1)}, u32[]{:S(2)}, u32[]{:S(2)}) collective-permute-start(bf16[64,2048]{1,0:T(8,128)(2,1)S(1)} %collective-permute-done.31.refs_3_), channel_id=1, source_target_pairs={{0,2},{1,3},{2,0},{3,1},{4,6},{5,7},{6,4},{7,5},{8,10},{9,11},{10,... | collective-permute-start | bytes 786440 | tf_op jit(solution)/shard_map/ppermute | solution.py:52
  234.6 11.2 %collective-permute-start.43 = (bf16[512,2048]{1,0:T(8,128)(2,1)}, bf16[512,2048]{1,0:T(8,128)(2,1)}, u32[]{:S(2)}, u32[]{:S(2)}) collective-permute-start(bf16[512,2048]{1,0:T(8,128)(2,1)} %get-tuple-element.368), channel_id=1, source_target_pairs={{0,1},{1,0},{2,3},{3,2},{4,5},{5,4},{6,7},{7,6},{8,9},{9,8},{10,11... | collective-permute-start | bytes 6291464 | tf_op jit(solution)/shard_map/ppermute | solution.py:52
  234.6 11.2 %collective-permute-start.42 = (bf16[256,512]{1,0:T(8,128)(2,1)}, bf16[256,512]{1,0:T(8,128)(2,1)}, u32[]{:S(2)}, u32[]{:S(2)}) collective-permute-start(bf16[256,512]{1,0:T(8,128)(2,1)} %collective-permute-done.39.refs_12_), channel_id=1, source_target_pairs={{0,8},{4,12},{8,16},{12,20},{16,24},{20,28},{24,0},{28,4},{1,9},{5... | collective-permute-start | bytes 786440 | tf_op jit(solution)/shard_map/ppermute | solution.py:62
  248.2 24.7 %collective-permute-start.44 = (bf16[256,1024]{1,0:T(8,128)(2,1)S(1)}, bf16[256,1024]{1,0:T(8,128)(2,1)S(1)}, u32[]{:S(2)}, u32[]{:S(2)}) collective-permute-start(bf16[256,1024]{1,0:T(8,128)(2,1)S(1)} %shard_map.390.refs_1_.refs_5_), channel_id=1, source_target_pairs={{0,8},{4,12},{8,16},{12,20},{16,24},{20,28},{24,0},{28,4},{1,9},{5... | collective-permute-start | bytes 1572872 | tf_op jit(solution)/shard_map/ppermute | solution.py:62
  248.3 17.2 %collective-permute-start.48 = (bf16[64,1024]{1,0:T(8,128)(2,1)}, bf16[64,1024]{1,0:T(8,128)(2,1)S(1)}, u32[]{:S(2)}, u32[]{:S(2)}) collective-permute-start(bf16[64,1024]{1,0:T(8,128)(2,1)} %copy-done.43), channel_id=1, source_target_pairs={{0,24},{4,28},{8,0},{12,4},{16,8},{20,12},{24,16},{28,20},{1,25},{... | collective-permute-start | bytes 393224 | tf_op jit(solution)/shard_map/ppermute | solution.py:62
  252.1 20.8 %collective-permute-start.47 = (bf16[64,1024]{1,0:T(8,128)(2,1)}, bf16[64,1024]{1,0:T(8,128)(2,1)S(1)}, u32[]{:S(2)}, u32[]{:S(2)}) collective-permute-start(bf16[64,1024]{1,0:T(8,128)(2,1)} %copy-done.42), channel_id=1, source_target_pairs={{0,16},{4,20},{8,24},{12,28},{16,0},{20,4},{24,8},{28,12},{1,17},{... | collective-permute-start | bytes 393224 | tf_op jit(solution)/shard_map/ppermute | solution.py:62
  252.1 20.8 %collective-permute-start.46 = (bf16[64,1024]{1,0:T(8,128)(2,1)S(1)}, bf16[64,1024]{1,0:T(8,128)(2,1)S(1)}, u32[]{:S(2)}, u32[]{:S(2)}) collective-permute-start(bf16[64,1024]{1,0:T(8,128)(2,1)S(1)} %copy-done.41), channel_id=1, source_target_pairs={{0,8},{4,12},{8,16},{12,20},{16,24},{20,28},{24,0},{28,4},{1,9},{5... | collective-permute-start | bytes 393224 | tf_op jit(solution)/shard_map/ppermute | solution.py:62
  252.6 12.2 %collective-permute-start.45 = (f32[16,256]{1,0:T(8,128)S(1)}, f32[16,256]{1,0:T(8,128)S(1)}, u32[]{:S(2)}, u32[]{:S(2)}) collective-permute-start(f32[16,256]{1,0:T(8,128)S(1)} %add.70.d_low), channel_id=1, source_target_pairs={{0,2},{1,3},{2,0},{3,1},{4,6},{5,7},{6,4},{7,5},{8,10},{9,11},{10,... | collective-permute-start | bytes 49160 | tf_op jit(solution)/shard_map/ppermute | solution.py:52
  275.4 16.4 %collective-permute-start.51 = (bf16[256,1024]{1,0:T(8,128)(2,1)S(1)}, bf16[256,1024]{1,0:T(8,128)(2,1)S(1)}, u32[]{:S(2)}, u32[]{:S(2)}) collective-permute-start(bf16[256,1024]{1,0:T(8,128)(2,1)S(1)} %collective-permute-done.44.refs_6_), channel_id=1, source_target_pairs={{0,8},{4,12},{8,16},{12,20},{16,24},{20,28},{24,0},{28,4},{1,9},{5... | collective-permute-start | bytes 1572872 | tf_op jit(solution)/shard_map/ppermute | solution.py:62
  275.7 19.3 %collective-permute-start.52 = (bf16[256,1408]{1,0:T(8,128)(2,1)S(1)}, bf16[256,1408]{1,0:T(8,128)(2,1)S(1)}, u32[]{:S(2)}, u32[]{:S(2)}) collective-permute-start(bf16[256,1408]{1,0:T(8,128)(2,1)S(1)} %get-tuple-element.426), channel_id=1, source_target_pairs={{0,4},{4,0},{8,12},{12,8},{16,20},{20,16},{24,28},{28,24},{1,5},{5... | collective-permute-start | bytes 2162696 | tf_op jit(solution)/shard_map/ppermute | solution.py:52
  298.0 18.6 %collective-permute-start.57 = (bf16[256,1408]{1,0:T(8,128)(2,1)S(1)}, bf16[256,1408]{1,0:T(8,128)(2,1)S(1)}, u32[]{:S(2)}, u32[]{:S(2)}) collective-permute-start(bf16[256,1408]{1,0:T(8,128)(2,1)S(1)} %get-tuple-element.436), channel_id=1, source_target_pairs={{0,4},{4,0},{8,12},{12,8},{16,20},{20,16},{24,28},{28,24},{1,5},{5... | collective-permute-start | bytes 2162696 | tf_op jit(solution)/shard_map/ppermute | solution.py:52
  300.0 15.5 %collective-permute-start.56 = (bf16[256,1024]{1,0:T(8,128)(2,1)S(1)}, bf16[256,1024]{1,0:T(8,128)(2,1)S(1)}, u32[]{:S(2)}, u32[]{:S(2)}) collective-permute-start(bf16[256,1024]{1,0:T(8,128)(2,1)S(1)} %collective-permute-done.51.refs_7_), channel_id=1, source_target_pairs={{0,8},{4,12},{8,16},{12,20},{16,24},{20,28},{24,0},{28,4},{1,9},{5... | collective-permute-start | bytes 1572872 | tf_op jit(solution)/shard_map/ppermute | solution.py:62
  303.5 13.1 %collective-permute-start.58 = (bf16[128,2048]{1,0:T(8,128)(2,1)S(1)}, bf16[128,2048]{1,0:T(8,128)(2,1)S(1)}, u32[]{:S(2)}, u32[]{:S(2)}) collective-permute-start(bf16[128,2048]{1,0:T(8,128)(2,1)S(1)} %shard_map.400.own), channel_id=1, source_target_pairs={{0,2},{1,3},{2,0},{3,1},{4,6},{5,7},{6,4},{7,5},{8,10},{9,11},{10,... | collective-permute-start | bytes 1572872 | tf_op jit(solution)/shard_map/ppermute | solution.py:52
  321.3 14.9 %collective-permute-start.61 = (bf16[256,1024]{1,0:T(8,128)(2,1)S(1)}, bf16[256,1024]{1,0:T(8,128)(2,1)S(1)}, u32[]{:S(2)}, u32[]{:S(2)}) collective-permute-start(bf16[256,1024]{1,0:T(8,128)(2,1)S(1)} %get-tuple-element.444), channel_id=1, source_target_pairs={{0,4},{4,0},{8,12},{12,8},{16,20},{20,16},{24,28},{28,24},{1,5},{5... | collective-permute-start | bytes 1572872 | tf_op jit(solution)/shard_map/ppermute | solution.py:52
  322.0 25.4 %collective-permute-start.67 = (bf16[256,1024]{1,0:T(8,128)(2,1)S(1)}, bf16[256,1024]{1,0:T(8,128)(2,1)S(1)}, u32[]{:S(2)}, u32[]{:S(2)}) collective-permute-start(bf16[256,1024]{1,0:T(8,128)(2,1)S(1)} %get-tuple-element.463), channel_id=1, source_target_pairs={{0,4},{4,0},{8,12},{12,8},{16,20},{20,16},{24,28},{28,24},{1,5},{5... | collective-permute-start | bytes 1572872 | tf_op jit(solution)/shard_map/ppermute | solution.py:52
  323.4 14.5 %collective-permute-start.62 = (bf16[128,2048]{1,0:T(8,128)(2,1)S(1)}, bf16[128,2048]{1,0:T(8,128)(2,1)S(1)}, u32[]{:S(2)}, u32[]{:S(2)}) collective-permute-start(bf16[128,2048]{1,0:T(8,128)(2,1)S(1)} %shard_map.400.own), channel_id=1, source_target_pairs={{0,1},{1,0},{2,3},{3,2},{4,5},{5,4},{6,7},{7,6},{8,9},{9,8},{10,11... | collective-permute-start | bytes 1572872 | tf_op jit(solution)/shard_map/ppermute | solution.py:52
  323.4 14.5 %collective-permute-start.63 = (bf16[128,2048]{1,0:T(8,128)(2,1)S(1)}, bf16[128,2048]{1,0:T(8,128)(2,1)S(1)}, u32[]{:S(2)}, u32[]{:S(2)}) collective-permute-start(bf16[128,2048]{1,0:T(8,128)(2,1)S(1)} %collective-permute-done.58.side), channel_id=1, source_target_pairs={{0,1},{1,0},{2,3},{3,2},{4,5},{5,4},{6,7},{7,6},{8,9},{9,8},{10,11... | collective-permute-start | bytes 1572872 | tf_op jit(solution)/shard_map/ppermute | solution.py:52
  330.8 30.4 %collective-permute-start.68 = (bf16[256,1408]{1,0:T(8,128)(2,1)S(1)}, bf16[256,1408]{1,0:T(8,128)(2,1)S(1)}, u32[]{:S(2)}, u32[]{:S(2)}) collective-permute-start(bf16[256,1408]{1,0:T(8,128)(2,1)S(1)} %get-tuple-element.469), channel_id=1, source_target_pairs={{0,4},{4,0},{8,12},{12,8},{16,20},{20,16},{24,28},{28,24},{1,5},{5... | collective-permute-start | bytes 2162696 | tf_op jit(solution)/shard_map/ppermute | solution.py:52
  336.2 12.5 %collective-permute-start.66 = (f32[24,2048]{1,0:T(8,128)S(1)}, f32[24,2048]{1,0:T(8,128)S(1)}, u32[]{:S(2)}, u32[]{:S(2)}) collective-permute-start(f32[24,2048]{1,0:T(8,128)S(1)} %add.74), channel_id=1, source_target_pairs={{0,16},{4,20},{8,24},{12,28},{16,0},{20,4},{24,8},{28,12},{1,17},{... | collective-permute-start | bytes 589832 | tf_op jit(solution)/shard_map/ppermute | solution.py:52
  (128 other events, 1188.4 us)

commit v4 on v3

--- a/solution.py
+++ b/solution.py
@@ -741,11 +741,16 @@
     )
 
 
-def edge_kernel(place, d_pre, last_rows, from_next, keep, out):
-    quarter = d_pre.shape[0] // 4
+def edge_kernel(place, d_pre, last_rows, from_next, start_row, out):
+    length = d_pre.shape[0]
+    quarter = length // 4
     out[...] = d_pre[...]
+    row = lax.broadcasted_iota(jnp.int32, (8, 1), 0)
+    one = 1.0 - start_row[:, length - 1 : length]
+    two = one * (1.0 - start_row[:, length - 2 : length - 1])
+    keep = jnp.where(row == 7, 1.0, jnp.where(row == 6, one, jnp.where(row == 5, two, 0.0)))
     at = pl.multiple_of((place[0] ^ 3) * quarter + quarter - 8, 8)
-    out[pl.ds(at, 8), :] = (last_rows[...] + from_next[...] * keep[...]).astype(BF16)
+    out[pl.ds(at, 8), :] = (last_rows[...] + from_next[...] * keep).astype(BF16)
 
 
 def stack_kernel(place, *refs):
@@ -1085,23 +1090,21 @@
     outgate_turns = finish([*outgate_turns, right])
     hold(from_next)
     (d_pre,) = run(
-        edge_kernel, [d_pre, last_rows, from_next, tail_keep[:, None]], [((length, channels), BF16)]
+        edge_kernel, [d_pre, last_rows, from_next, start_row], [((length, channels), BF16)]
     )
 
     pre_1 = turn(d_pre, 1)
-    cuts_got = [turn(after(cuts[by - 1], d_pre), by) for by in range(1, turns)]
     d_low = d_low + d_low_got
     grads.append(
         run(*gate_back_rows([rows_other], down_weight, made[1][1], made[1][2], pair), vmem=roomy)
     )
     cuts_in = [part[3] for part in made]
     weigh("gate", cuts_in, [grad[0] for grad in grads])
-    pre_1, gate_sent, d_low_got, *cuts_got = join(
-        pre_1, sums["gate"][0], flip(d_low, "head", 2), *cuts_got
-    )
+    pre_1, gate_sent, d_low_got = join(pre_1, sums["gate"][0], flip(d_low, "head", 2))
 
     pre_2 = turn(pre_1, 1)
     gate_got = flip(gate_sent, "seq", 1)
+    cuts_got = [turn(after(cuts[by - 1], pre_1), by) for by in range(1, turns)]
     hold(pre_1)
     sent, kept = run(
         *rows_times(
@@ -1118,8 +1121,6 @@
     far = flip(far, "head", 2)
     weigh("up", cuts_in, [grad[1] for grad in grads])
     weigh("down", [grad[2] for grad in grads], [part[0] for part in made])
-    (cuts_near,) = run(stack_kernel, cuts_got, [(((turns - 1) * quarter, 2 * pair), BF16)])
-    cuts_side = flip(cuts_near, "head", 2)
     grad_own, first_part, d_lowrank = run(
         input_back_kernel,
         [near, far, block_input, d_hidden, first_row, d_low, d_low_got, lowrank_down.T],
@@ -1131,36 +1132,35 @@
         [((RANK + 8, D), F32)],
     )
     (rows_both,) = run(stack_kernel, [grad_own, output_own], [((half, D), BF16)])
-    pre_2, gate_got, small, rows_both, up_sent, down_sent, cuts_near, cuts_side = join(
-        pre_2, gate_got, small, rows_both, sums["up"][0], sums["down"][0], cuts_near, cuts_side
-    )
+    pre_2, gate_got, small, rows_both, up_sent, down_sent, *cuts_got = join(
+        pre_2, gate_got, small, rows_both, sums["up"][0], sums["down"][0], *cuts_got
+    )
+    (cuts_near,) = run(stack_kernel, cuts_got, [(((turns - 1) * quarter, 2 * pair), BF16)])
 
     pre_3 = turn(pre_2, 1)
+    cuts_side = flip(cuts_near, "head", 2)
     cuts_far = quarters(cuts_near, cuts_side)
-    shared = total(small[RANK + 5 :], [("head", 1), ("head", 2)])
     up_got = flip(up_sent, "seq", 1)
     rows_side = flip(rows_both, "head", 2)
+    pre_3, up_got, down_sent, *cuts_far = join(pre_3, up_got, down_sent, *cuts_far)
+    small = total(after(small, pre_3), steps[:1])
+    down_got = flip(down_sent, "seq", 1)
+    sum_pre = run(
+        *zone_weight(
+            pre_kernel, turns, share, length, channels,
+            [normed, *cuts_far, d_pre, *finish([pre_1, pre_2, pre_3])],
+        )
+    )
+    pre_got = flip(sum_pre[0], "seq", 1)
     sum_both = run(
         *zone_weight(
             both_kernel, turns, share, length, 2 * DV,
             [*d_branch, normed, *cuts_far, d_outgate, gated, *outgate_turns, *gated_turns],
         )
     )
-    pre_3, up_got, rows_side, shared, both_sent, rows_both, down_sent = join(
-        pre_3, up_got, rows_side, shared, sum_both[0], rows_both, down_sent
-    )
-    small = jnp.concatenate([small[: RANK + 5], shared], axis=0)
-    small = total(after(small, pre_3), steps[:1])
-    down_got, both_got = flip(down_sent, "seq", 1), flip(both_sent, "seq", 1)
-    sum_pre = run(
-        *zone_weight(
-            pre_kernel, turns, share, length, channels,
-            [normed, *cuts_far, d_pre, *finish([pre_1, pre_2, pre_3])],
-        )
-    )
-    pre_got = flip(sum_pre[0], "seq", 1)
+    both_got = flip(sum_both[0], "seq", 1)
     small = total(after(small, sum_pre[0]), steps[1:])
-    shared = small[RANK + 5 :]
+    shared = total(small[RANK + 5 :], [("head", 1), ("head", 2)])
     grad_query, grad_key, grad_value = run(
         settle_kernel, [sum_pre[1], pre_got],
         [((share, DK), F32), ((share, DK), F32), ((share, DV), F32)],

time: 370 us -> 364 us (0.984)
  local copies, waits for them, and re-layouts: 17.1 us -> 7.19 us
  starting transfers between devices: 72.7 us -> 78.5 us
    unnamed x184 -> x62, local copies, waits for them, and re-layouts: 12.5 us -> 2.66 us
    ppermute x43, waiting for transfers between devices: 90.5 us -> 97.6 us  [flip(): return lax.ppermute(x, axis, [(i, i ^ bit) for i in range(n)])]
    ppermute x18, waiting for transfers between devices: 66 us -> 59.5 us  [turn(): return lax.ppermute(x, 'seq', [(i, (i + 2 * by) % n) for i in range(n)])]
    ppermute x43, starting transfers between devices: 30.3 us -> 34.9 us  [flip(): return lax.ppermute(x, axis, [(i, i ^ bit) for i in range(n)])]
  transfers between devices with their start and end apart: 69 -> 69, of which waited for: 47 -> 42; matrix products, arithmetic and copies ran while one was open for 2% -> 3% of each run, Pallas kernels for 13% -> 12%
where the time goes in v4:
time: 364 us; the launch traced here: 358 us
  waiting for transfers between devices  171 us (47%)
  Pallas kernels  83.5 us (23%)
  starting transfers between devices  78.5 us (22%)
  other arithmetic  8.77 us (2%)
  local copies, waits for them, and re-layouts  7.19 us (2%)
  between operations  5.85 us (2%)
    ppermute x43, waiting for transfers between devices, flip(): return lax.ppermute(x, axis, [(i, i ^ bit) for i in range(n)])  97.6 us
    pallas_call x42, Pallas kernels, call(): pl.pallas_call(body, out_shape=[jax.ShapeDtypeStruct(shape, kind) for sha...  83.5 us
    ppermute x18, waiting for transfers between devices, turn(): return lax.ppermute(x, 'seq', [(i, (i + 2 * by) % n) for i in range(n)])  59.5 us
    ppermute x43, starting transfers between devices, flip(): return lax.ppermute(x, axis, [(i, i ^ bit) for i in range(n)])  34.9 us
    ppermute x8, starting transfers between devices, shift(): lax.ppermute(x, axis, [(i, i + by) for i in range(n) if 0 <= i + by < n])  24.4 us
    ppermute x18, starting transfers between devices, turn(): return lax.ppermute(x, 'seq', [(i, (i + 2 * by) % n) for i in range(n)])  19.1 us
    ppermute x8, waiting for transfers between devices, shift(): lax.ppermute(x, axis, [(i, i + by) for i in range(n) if 0 <= i + by < n])  14 us
  transfers between devices with their start and end apart: 69, of which 42 were waited for; matrix products, arithmetic and copies ran while one was open for 3% of the time, Pallas kernels for 12%

profile of v4, /device:TPU:0, one launch (start us, length us, event | category | flops | bytes accessed | tf_op | source)
XLA Modules:
  0.0 358.2 jit_solution(17323940966833826588)
XLA Ops:
  9.1 4.8 %collective-permute-start = (bf16[8,1024]{1,0:T(8,128)(2,1)S(1)}, bf16[8,1024]{1,0:T(8,128)(2,1)S(1)}, u32[]{:S(2)}, u32[]{:S(2)}) collective-permute-start(bf16[8,1024]{1,0:T(8,128)(2,1)S(1)} %maximum_multiply_fusion), channel_id=1, source_target_pairs={{0,4},{4,8},{8,12},{12,16},{16,20},{20,24},{24,28},{1,5},{5,9},{9,... | collective-permute-start | bytes 49160 | tf_op jit(solution)/shard_map/ppermute | solution.py:57
  20.6 3.5 collective-permute-start.1
  30.5 5.3 %collective-permute-start.3 = (bf16[272,512]{1,0:T(8,128)(2,1)S(1)}, bf16[272,512]{1,0:T(8,128)(2,1)S(1)}, u32[]{:S(2)}, u32[]{:S(2)}) collective-permute-start(bf16[272,512]{1,0:T(8,128)(2,1)S(1)} %get-tuple-element.250.refs_0_), channel_id=1, source_target_pairs={{0,8},{4,12},{8,16},{12,20},{16,24},{20,28},{1,9},{5,13},{9,17},{1... | collective-permute-start | bytes 835592 | tf_op jit(solution)/shard_map/ppermute | solution.py:57
  40.7 5.5 %collective-permute-start.5 = (bf16[272,512]{1,0:T(8,128)(2,1)S(1)}, bf16[272,512]{1,0:T(8,128)(2,1)S(1)}, u32[]{:S(2)}, u32[]{:S(2)}) collective-permute-start(bf16[272,512]{1,0:T(8,128)(2,1)S(1)} %get-tuple-element.256), channel_id=1, source_target_pairs={{0,16},{4,20},{8,24},{12,28},{1,17},{5,21},{9,25},{13,29},{2,18},{... | collective-permute-start | bytes 835592 | tf_op jit(solution)/shard_map/ppermute | solution.py:57
  46.2 4.5 %collective-permute-done.6 = f32[8,128]{1,0:T(8,128)S(1)} collective-permute-done((f32[8,128]{1,0:T(8,128)S(1)}, f32[8,128]{1,0:T(8,128)S(1)}, u32[]{:S(2)}, u32[]{:S(2)}) %collective-permute-start.6) | collective-permute-done | bytes 4128 | tf_op jit(solution)/shard_map/ppermute | solution.py:52
  57.7 5.8 %collective-permute-start.9 = (bf16[256,512]{1,0:T(8,128)(2,1)S(1)}, bf16[256,512]{1,0:T(8,128)(2,1)S(1)}, u32[]{:S(2)}, u32[]{:S(2)}) collective-permute-start(bf16[256,512]{1,0:T(8,128)(2,1)S(1)} %get-tuple-element.273.refs_10_), channel_id=1, source_target_pairs={{0,8},{4,12},{8,16},{12,20},{16,24},{20,28},{24,0},{28,4},{1,9},{5... | collective-permute-start | bytes 786440 | tf_op jit(solution)/shard_map/ppermute | solution.py:62
  64.5 8.2 %collective-permute-done.9.refs_14_ = bf16[256,512]{1,0:T(8,128)(2,1)S(1)} collective-permute-done((bf16[256,512]{1,0:T(8,128)(2,1)S(1)}, bf16[256,512]{1,0:T(8,128)(2,1)S(1)}, u32[]{:S(2)}, u32[]{:S(2)}) %collective-permute-start.9) | collective-permute-done | bytes 262176 | tf_op jit(solution)/shard_map/ppermute | solution.py:62
  74.6 6.5 %collective-permute-done.10.refs_1_.refs_4_ = bf16[64,2048]{1,0:T(8,128)(2,1)S(1)} collective-permute-done((bf16[64,2048]{1,0:T(8,128)(2,1)S(1)}, bf16[64,2048]{1,0:T(8,128)(2,1)S(1)}, u32[]{:S(2)}, u32[]{:S(2)}) %collective-permute-start.10) | collective-permute-done | bytes 262176 | tf_op jit(solution)/shard_map/ppermute | solution.py:52
  85.1 4.1 %shard_map.372 = (bf16[256,1408]{1,0:T(8,128)(2,1)S(1)}, bf16[256,1408]{1,0:T(8,128)(2,1)S(1)}, bf16[256,1408]{1,0:T(8,128)(2,1)S(1)}) custom-call(s32[3]{0:T(128)S(1)} %pad_add_fusion.place, bf16[64,2048]{1,0:T(8,128)(2,1)S(1)} %get-tuple-element.275.refs_0_, bf16[64,2048]{1,0:T(8,128)(2,1)S(1)} %collective-permute-done.10.refs_1_.refs_4_, ...), custom_call_target="tpu_custom_call" | custom-call | flops 5000000000 | bytes 15000000 | tf_op jit(solution)/shard_map/pallas_call | solution.py:375
  95.8 6.8 %collective-permute-done.15.got = bf16[64,2048]{1,0:T(8,128)(2,1)S(1)} collective-permute-done((bf16[64,2048]{1,0:T(8,128)(2,1)S(1)}, bf16[64,2048]{1,0:T(8,128)(2,1)S(1)}, u32[]{:S(2)}, u32[]{:S(2)}) %collective-permute-start.15) | collective-permute-done | bytes 262176 | tf_op jit(solution)/shard_map/ppermute | solution.py:52
  107.7 6.7 %collective-permute-done.17.refs_1_.refs_4_ = bf16[64,2048]{1,0:T(8,128)(2,1)S(1)} collective-permute-done((bf16[64,2048]{1,0:T(8,128)(2,1)S(1)}, bf16[64,2048]{1,0:T(8,128)(2,1)S(1)}, u32[]{:S(2)}, u32[]{:S(2)}) %collective-permute-start.17) | collective-permute-done | bytes 262176 | tf_op jit(solution)/shard_map/ppermute | solution.py:52
  114.4 4.3 %collective-permute-done.18.refs_2_.refs_3_ = bf16[64,2048]{1,0:T(8,128)(2,1)S(1)} collective-permute-done((bf16[64,2048]{1,0:T(8,128)(2,1)S(1)}, bf16[64,2048]{1,0:T(8,128)(2,1)S(1)}, u32[]{:S(2)}, u32[]{:S(2)}) %collective-permute-start.18) | collective-permute-done | bytes 262176 | tf_op jit(solution)/shard_map/ppermute | solution.py:62
  126.6 4.0 %shard_map.378 = (bf16[128,2048]{1,0:T(8,128)(2,1)S(1)}, f32[128,2048]{1,0:T(8,128)S(1)}) custom-call(s32[3]{0:T(128)S(1)} %pad_add_fusion.place, bf16[256,1408]{1,0:T(8,128)(2,1)S(1)} %get-tuple-element.307.refs_0_, bf16[256,1408]{1,0:T(8,128)(2,1)S(1)} %get-tuple-element.303.refs_1_, bf16[2048,1408]{1,0:T(8,128)(2,1)S(1)} %bitcast.29, ...), custom_call_target="tpu_custom_call" | custom-call | flops 2800000000 | bytes 8400000 | tf_op jit(solution)/shard_map/pallas_call | solution.py:375
  134.8 6.8 %collective-permute-done.23.got = bf16[64,2048]{1,0:T(8,128)(2,1)S(1)} collective-permute-done((bf16[64,2048]{1,0:T(8,128)(2,1)S(1)}, bf16[64,2048]{1,0:T(8,128)(2,1)S(1)}, u32[]{:S(2)}, u32[]{:S(2)}) %collective-permute-start.23) | collective-permute-done | bytes 262176 | tf_op jit(solution)/shard_map/ppermute | solution.py:52
  146.3 6.7 %collective-permute-done.25.branch_1.refs_1_ = bf16[64,2048]{1,0:T(8,128)(2,1)S(1)} collective-permute-done((bf16[64,2048]{1,0:T(8,128)(2,1)S(1)}, bf16[64,2048]{1,0:T(8,128)(2,1)S(1)}, u32[]{:S(2)}, u32[]{:S(2)}) %collective-permute-start.25) | collective-permute-done | bytes 262176 | tf_op jit(solution)/shard_map/ppermute | solution.py:52
  153.0 4.3 %collective-permute-done.26.refs_1_.refs_2_ = bf16[64,2048]{1,0:T(8,128)(2,1)S(1)} collective-permute-done((bf16[64,2048]{1,0:T(8,128)(2,1)S(1)}, bf16[64,2048]{1,0:T(8,128)(2,1)S(1)}, u32[]{:S(2)}, u32[]{:S(2)}) %collective-permute-start.26) | collective-permute-done | bytes 262176 | tf_op jit(solution)/shard_map/ppermute | solution.py:62
  171.3 9.0 %collective-permute-done.31.refs_3_ = bf16[64,2048]{1,0:T(8,128)(2,1)S(1)} collective-permute-done((bf16[64,2048]{1,0:T(8,128)(2,1)S(1)}, bf16[64,2048]{1,0:T(8,128)(2,1)S(1)}, u32[]{:S(2)}, u32[]{:S(2)}) %collective-permute-start.31) | collective-permute-done | bytes 262176 | tf_op jit(solution)/shard_map/ppermute | solution.py:62
  185.7 7.5 %shard_map.384 = (bf16[512,1408]{1,0:T(8,128)(2,1)S(1)}, bf16[512,1408]{1,0:T(8,128)(2,1)S(1)}, bf16[512,1408]{1,0:T(8,128)(2,1)S(1)}, bf16[512,512]{1,0:T(8,128)(2,1)S(1)}, bf16[512,2048]{1,0:T(8,128)(2,1)S(1)}) custom-call(s32[3]{0:T(128)S(1)} %pad_add_fusion.place, bf16[64,2048]{1,0:T(8,128)(2,1)S(1)} %get-tuple-element.275.refs_0_, ...), custom_call_target="tpu_custom_call" | custom-call | flops 1000000000 | bytes 3000000 | tf_op jit(solution)/shard_map/pallas_call | solution.py:375
  202.1 7.5 %shard_map.386 = (bf16[512,1408]{1,0:T(8,128)(2,1)S(1)}, bf16[512,1408]{1,0:T(8,128)(2,1)S(1)}, bf16[512,1408]{1,0:T(8,128)(2,1)S(1)}, bf16[512,512]{1,0:T(8,128)(2,1)S(1)}) custom-call(s32[3]{0:T(128)S(1)} %pad_add_fusion.place, bf16[512,2048]{1,0:T(8,128)(2,1)S(1)} %collective-permute-done.36.refs_0_, bf16[2048,1408]{1,0:T(8,128)(2,1)S(1)} %bitcast.29, ...), custom_call_target="tpu_custom_call" | custom-call | flops 5000000000 | bytes 15000000 | tf_op jit(solution)/shard_map/pallas_call | solution.py:375
  211.6 9.8 %collective-permute-done.37.got = bf16[272,512]{1,0:T(8,128)(2,1)S(1)} collective-permute-done((bf16[272,512]{1,0:T(8,128)(2,1)S(1)}, bf16[272,512]{1,0:T(8,128)(2,1)S(1)}, u32[]{:S(2)}, u32[]{:S(2)}) %collective-permute-start.37) | collective-permute-done | bytes 278560 | tf_op jit(solution)/shard_map/ppermute | solution.py:57
  222.1 4.2 %shard_map.388 = (bf16[256,1024]{1,0:T(8,128)(2,1)S(1)}, f32[8,1024]{1,0:T(8,128)S(1)}, f32[8,2048]{1,0:T(8,128)S(1)}, f32[16,256]{1,0:T(8,128)S(1)}, f32[8,1024]{1,0:T(8,128)S(1)}) custom-call(s32[3]{0:T(128)S(1)} %pad_add_fusion.place, bf16[256,512]{1,0:T(8,128)(2,1)S(1)} %get-tuple-element.357.d_mixed, bf16[256,512]{1,0:T(8,128)(2,1)S(1)} %shard_map.368.state_in, ...), custom_call_target="tpu_custom_call" | custom-call | flops 4499999744 | bytes 13500000 | tf_op jit(solution)/shard_map/pallas_call | solution.py:375
  226.3 4.3 %shard_map.389 = (bf16[512,1408]{1,0:T(8,128)(2,1)S(1)}, bf16[512,1408]{1,0:T(8,128)(2,1)S(1)}, bf16[512,512]{1,0:T(8,128)(2,1)S(1)}, bf16[512,2048]{1,0:T(8,128)(2,1)S(1)}) custom-call(s32[3]{0:T(128)S(1)} %pad_add_fusion.place, bf16[64,2048]{1,0:T(8,128)(2,1)S(1)} %get-tuple-element.315.refs_0_, ...), custom_call_target="tpu_custom_call" | custom-call | flops 4000000000 | bytes 12000000 | tf_op jit(solution)/shard_map/pallas_call | solution.py:375
  237.3 4.3 %collective-permute-done.42.refs_13_ = bf16[256,512]{1,0:T(8,128)(2,1)S(1)} collective-permute-done((bf16[256,512]{1,0:T(8,128)(2,1)S(1)}, bf16[256,512]{1,0:T(8,128)(2,1)S(1)}, u32[]{:S(2)}, u32[]{:S(2)}) %collective-permute-start.42) | collective-permute-done | bytes 262176 | tf_op jit(solution)/shard_map/ppermute | solution.py:62
  243.9 4.2 %shard_map.391 = (bf16[512,1408]{1,0:T(8,128)(2,1)S(1)}, bf16[512,1408]{1,0:T(8,128)(2,1)S(1)}, bf16[512,512]{1,0:T(8,128)(2,1)S(1)}) custom-call(s32[3]{0:T(128)S(1)} %pad_add_fusion.place, bf16[512,2048]{1,0:T(8,128)(2,1)S(1)} %collective-permute-done.43.refs_0_, bf16[2048,1408]{1,0:T(8,128)(2,1)S(1)} %bitcast.41, ...), custom_call_target="tpu_custom_call" | custom-call | flops 3000000000 | bytes 9000000 | tf_op jit(solution)/shard_map/pallas_call | solution.py:375
  250.7 6.5 %collective-permute-done.44.refs_6_ = bf16[256,1024]{1,0:T(8,128)(2,1)S(1)} collective-permute-done((bf16[256,1024]{1,0:T(8,128)(2,1)S(1)}, bf16[256,1024]{1,0:T(8,128)(2,1)S(1)}, u32[]{:S(2)}, u32[]{:S(2)}) %collective-permute-start.44) | collective-permute-done | bytes 524320 | tf_op jit(solution)/shard_map/ppermute | solution.py:62
  259.7 4.0 %collective-permute-start.52 = (bf16[64,1024]{1,0:T(8,128)(2,1)S(1)}, bf16[64,1024]{1,0:T(8,128)(2,1)S(1)}, u32[]{:S(2)}, u32[]{:S(2)}) collective-permute-start(bf16[64,1024]{1,0:T(8,128)(2,1)S(1)} %get-tuple-element.422), channel_id=1, source_target_pairs={{0,24},{4,28},{8,0},{12,4},{16,8},{20,12},{24,16},{28,20},{1,25},{... | collective-permute-start | bytes 393224 | tf_op jit(solution)/shard_map/ppermute | solution.py:62
  279.8 4.5 %collective-permute-done.50.refs_0_ = bf16[64,1024]{1,0:T(8,128)(2,1)S(1)} collective-permute-done((bf16[64,1024]{1,0:T(8,128)(2,1)S(1)}, bf16[64,1024]{1,0:T(8,128)(2,1)S(1)}, u32[]{:S(2)}, u32[]{:S(2)}) %collective-permute-start.50) | collective-permute-done | bytes 131104 | tf_op jit(solution)/shard_map/ppermute | solution.py:62
  289.5 7.4 %collective-permute-done.55.refs_2_.refs_6_ = bf16[192,1024]{1,0:T(8,128)(2,1)S(1)} collective-permute-done((bf16[192,1024]{1,0:T(8,128)(2,1)S(1)}, bf16[192,1024]{1,0:T(8,128)(2,1)S(1)}, u32[]{:S(2)}, u32[]{:S(2)}) %collective-permute-start.55) | collective-permute-done | bytes 393248 | tf_op jit(solution)/shard_map/ppermute | solution.py:52
  298.7 8.1 %collective-permute-done.59.side = bf16[128,2048]{1,0:T(8,128)(2,1)S(1)} collective-permute-done((bf16[128,2048]{1,0:T(8,128)(2,1)S(1)}, bf16[128,2048]{1,0:T(8,128)(2,1)S(1)}, u32[]{:S(2)}, u32[]{:S(2)}) %collective-permute-start.59) | collective-permute-done | bytes 524320 | tf_op jit(solution)/shard_map/ppermute | solution.py:52
  315.7 12.9 %collective-permute-done.62 = f32[24,2048]{1,0:T(8,128)S(1)} collective-permute-done((f32[24,2048]{1,0:T(8,128)S(1)}, f32[24,2048]{1,0:T(8,128)S(1)}, u32[]{:S(2)}, u32[]{:S(2)}) %collective-permute-start.62) | collective-permute-done | bytes 196640 | tf_op jit(solution)/shard_map/ppermute | solution.py:52
  330.5 4.7 %collective-permute-done.63 = f32[24,2048]{1,0:T(8,128)S(1)} collective-permute-done((f32[24,2048]{1,0:T(8,128)S(1)}, f32[24,2048]{1,0:T(8,128)S(1)}, u32[]{:S(2)}, u32[]{:S(2)}) %collective-permute-start.63) | collective-permute-done | bytes 196640 | tf_op jit(solution)/shard_map/ppermute | solution.py:52
  341.7 5.2 %collective-permute-done.64 = f32[24,2048]{1,0:T(8,128)S(1)} collective-permute-done((f32[24,2048]{1,0:T(8,128)S(1)}, f32[24,2048]{1,0:T(8,128)S(1)}, u32[]{:S(2)}, u32[]{:S(2)}) %collective-permute-start.64) | collective-permute-done | bytes 196640 | tf_op jit(solution)/shard_map/ppermute | solution.py:52
  (252 shorter events, 160.4 us)
Async XLA Ops:
  57.7 15.0 %collective-permute-start.9 = (bf16[256,512]{1,0:T(8,128)(2,1)S(1)}, bf16[256,512]{1,0:T(8,128)(2,1)S(1)}, u32[]{:S(2)}, u32[]{:S(2)}) collective-permute-start(bf16[256,512]{1,0:T(8,128)(2,1)S(1)} %get-tuple-element.273.refs_10_), channel_id=1, source_target_pairs={{0,8},{4,12},{8,16},{12,20},{16,24},{20,28},{24,0},{28,4},{1,9},{5... | collective-permute-start | bytes 786440 | tf_op jit(solution)/shard_map/ppermute | solution.py:62
  107.7 11.0 %collective-permute-start.18 = (bf16[64,2048]{1,0:T(8,128)(2,1)S(1)}, bf16[64,2048]{1,0:T(8,128)(2,1)S(1)}, u32[]{:S(2)}, u32[]{:S(2)}) collective-permute-start(bf16[64,2048]{1,0:T(8,128)(2,1)S(1)} %collective-permute-done.16.refs_1_.refs_2_), channel_id=1, source_target_pairs={{0,8},{4,12},{8,16},{12,20},{16,24},{20,28},{24,0},{28,4},{1,9},{5... | collective-permute-start | bytes 786440 | tf_op jit(solution)/shard_map/ppermute | solution.py:62
  107.7 14.3 %collective-permute-start.19 = (bf16[256,512]{1,0:T(8,128)(2,1)S(1)}, bf16[256,512]{1,0:T(8,128)(2,1)S(1)}, u32[]{:S(2)}, u32[]{:S(2)}) collective-permute-start(bf16[256,512]{1,0:T(8,128)(2,1)S(1)} %collective-permute-done.9.refs_14_), channel_id=1, source_target_pairs={{0,8},{4,12},{8,16},{12,20},{16,24},{20,28},{24,0},{28,4},{1,9},{5... | collective-permute-start | bytes 786440 | tf_op jit(solution)/shard_map/ppermute | solution.py:62
  107.7 14.3 %collective-permute-start.20 = (bf16[64,2048]{1,0:T(8,128)(2,1)S(1)}, bf16[64,2048]{1,0:T(8,128)(2,1)S(1)}, u32[]{:S(2)}, u32[]{:S(2)}) collective-permute-start(bf16[64,2048]{1,0:T(8,128)(2,1)S(1)} %get-tuple-element.315.refs_0_), channel_id=1, source_target_pairs={{0,1},{1,0},{2,3},{3,2},{4,5},{5,4},{6,7},{7,6},{8,9},{9,8},{10,11... | collective-permute-start | bytes 786440 | tf_op jit(solution)/shard_map/ppermute | solution.py:52
  146.3 11.0 %collective-permute-start.26 = (bf16[64,2048]{1,0:T(8,128)(2,1)S(1)}, bf16[64,2048]{1,0:T(8,128)(2,1)S(1)}, u32[]{:S(2)}, u32[]{:S(2)}) collective-permute-start(bf16[64,2048]{1,0:T(8,128)(2,1)S(1)} %collective-permute-done.24.refs_0_.refs_1_), channel_id=1, source_target_pairs={{0,8},{4,12},{8,16},{12,20},{16,24},{20,28},{24,0},{28,4},{1,9},{5... | collective-permute-start | bytes 786440 | tf_op jit(solution)/shard_map/ppermute | solution.py:62
  146.3 14.3 %collective-permute-start.27 = (bf16[256,512]{1,0:T(8,128)(2,1)S(1)}, bf16[256,512]{1,0:T(8,128)(2,1)S(1)}, u32[]{:S(2)}, u32[]{:S(2)}) collective-permute-start(bf16[256,512]{1,0:T(8,128)(2,1)S(1)} %collective-permute-done.19.refs_15_), channel_id=1, source_target_pairs={{0,8},{4,12},{8,16},{12,20},{16,24},{20,28},{24,0},{28,4},{1,9},{5... | collective-permute-start | bytes 786440 | tf_op jit(solution)/shard_map/ppermute | solution.py:62
  160.6 19.7 %collective-permute-start.32 = (bf16[192,2048]{1,0:T(8,128)(2,1)S(1)}, bf16[192,2048]{1,0:T(8,128)(2,1)S(1)}, u32[]{:S(2)}, u32[]{:S(2)}) collective-permute-start(bf16[192,2048]{1,0:T(8,128)(2,1)S(1)} %shard_map.377), channel_id=1, source_target_pairs={{0,2},{1,3},{2,0},{3,1},{4,6},{5,7},{6,4},{7,5},{8,10},{9,11},{10,... | collective-permute-start | bytes 2359304 | tf_op jit(solution)/shard_map/ppermute | solution.py:52
  166.0 14.3 %collective-permute-start.30 = (bf16[272,512]{1,0:T(8,128)(2,1)S(1)}, bf16[272,512]{1,0:T(8,128)(2,1)S(1)}, u32[]{:S(2)}, u32[]{:S(2)}) collective-permute-start(bf16[272,512]{1,0:T(8,128)(2,1)S(1)} %get-tuple-element.328.refs_0_), channel_id=1, source_target_pairs={{4,0},{8,4},{12,8},{16,12},{20,16},{24,20},{28,24},{5,1},{9,5},{13... | collective-permute-start | bytes 835592 | tf_op jit(solution)/shard_map/ppermute | solution.py:57
  167.5 12.8 %collective-permute-start.31 = (bf16[64,2048]{1,0:T(8,128)(2,1)S(1)}, bf16[64,2048]{1,0:T(8,128)(2,1)S(1)}, u32[]{:S(2)}, u32[]{:S(2)}) collective-permute-start(bf16[64,2048]{1,0:T(8,128)(2,1)S(1)} %collective-permute-done.26.refs_1_.refs_2_), channel_id=1, source_target_pairs={{0,8},{4,12},{8,16},{12,20},{16,24},{20,28},{24,0},{28,4},{1,9},{5... | collective-permute-start | bytes 786440 | tf_op jit(solution)/shard_map/ppermute | solution.py:62
  181.0 16.1 %collective-permute-start.34 = (bf16[128,2048]{1,0:T(8,128)(2,1)S(1)}, bf16[128,2048]{1,0:T(8,128)(2,1)S(1)}, u32[]{:S(2)}, u32[]{:S(2)}) collective-permute-start(bf16[128,2048]{1,0:T(8,128)(2,1)S(1)} %shard_map.382), channel_id=1, source_target_pairs={{0,2},{1,3},{2,0},{3,1},{4,6},{5,7},{6,4},{7,5},{8,10},{9,11},{10,... | collective-permute-start | bytes 1572872 | tf_op jit(solution)/shard_map/ppermute | solution.py:52
  181.6 15.5 %collective-permute-start.33 = (bf16[272,512]{1,0:T(8,128)(2,1)S(1)}, bf16[272,512]{1,0:T(8,128)(2,1)S(1)}, u32[]{:S(2)}, u32[]{:S(2)}) collective-permute-start(bf16[272,512]{1,0:T(8,128)(2,1)S(1)} %get-tuple-element.340.refs_0_), channel_id=1, source_target_pairs={{8,0},{12,4},{16,8},{20,12},{24,16},{28,20},{9,1},{13,5},{17,9},{2... | collective-permute-start | bytes 835592 | tf_op jit(solution)/shard_map/ppermute | solution.py:57
  182.9 12.5 %collective-permute-start.35 = (bf16[256,512]{1,0:T(8,128)(2,1)S(1)}, bf16[256,512]{1,0:T(8,128)(2,1)S(1)}, u32[]{:S(2)}, u32[]{:S(2)}) collective-permute-start(bf16[256,512]{1,0:T(8,128)(2,1)S(1)} %get-tuple-element.343.refs_0_.refs_9_), channel_id=1, source_target_pairs={{0,8},{4,12},{8,16},{12,20},{16,24},{20,28},{24,0},{28,4},{1,9},{5... | collective-permute-start | bytes 786440 | tf_op jit(solution)/shard_map/ppermute | solution.py:62
  198.0 23.4 %collective-permute-start.37 = (bf16[272,512]{1,0:T(8,128)(2,1)S(1)}, bf16[272,512]{1,0:T(8,128)(2,1)S(1)}, u32[]{:S(2)}, u32[]{:S(2)}) collective-permute-start(bf16[272,512]{1,0:T(8,128)(2,1)S(1)} %get-tuple-element.347), channel_id=1, source_target_pairs={{16,0},{20,4},{24,8},{28,12},{17,1},{21,5},{25,9},{29,13},{18,2},{... | collective-permute-start | bytes 835592 | tf_op jit(solution)/shard_map/ppermute | solution.py:57
  199.3 12.3 %collective-permute-start.38 = (bf16[64,2048]{1,0:T(8,128)(2,1)S(1)}, bf16[64,2048]{1,0:T(8,128)(2,1)S(1)}, u32[]{:S(2)}, u32[]{:S(2)}) collective-permute-start(bf16[64,2048]{1,0:T(8,128)(2,1)S(1)} %collective-permute-done.31.refs_3_), channel_id=1, source_target_pairs={{0,2},{1,3},{2,0},{3,1},{4,6},{5,7},{6,4},{7,5},{8,10},{9,11},{10,... | collective-permute-start | bytes 786440 | tf_op jit(solution)/shard_map/ppermute | solution.py:52
  209.6 11.8 %collective-permute-start.39 = (bf16[256,512]{1,0:T(8,128)(2,1)S(1)}, bf16[256,512]{1,0:T(8,128)(2,1)S(1)}, u32[]{:S(2)}, u32[]{:S(2)}) collective-permute-start(bf16[256,512]{1,0:T(8,128)(2,1)S(1)} %collective-permute-done.35.refs_11_), channel_id=1, source_target_pairs={{0,8},{4,12},{8,16},{12,20},{16,24},{20,28},{24,0},{28,4},{1,9},{5... | collective-permute-start | bytes 786440 | tf_op jit(solution)/shard_map/ppermute | solution.py:62
  230.6 11.0 %collective-permute-start.43 = (bf16[512,2048]{1,0:T(8,128)(2,1)S(1)}, bf16[512,2048]{1,0:T(8,128)(2,1)S(1)}, u32[]{:S(2)}, u32[]{:S(2)}) collective-permute-start(bf16[512,2048]{1,0:T(8,128)(2,1)S(1)} %get-tuple-element.366), channel_id=1, source_target_pairs={{0,1},{1,0},{2,3},{3,2},{4,5},{5,4},{6,7},{7,6},{8,9},{9,8},{10,11... | collective-permute-start | bytes 6291464 | tf_op jit(solution)/shard_map/ppermute | solution.py:52
  230.7 10.9 %collective-permute-start.42 = (bf16[256,512]{1,0:T(8,128)(2,1)S(1)}, bf16[256,512]{1,0:T(8,128)(2,1)S(1)}, u32[]{:S(2)}, u32[]{:S(2)}) collective-permute-start(bf16[256,512]{1,0:T(8,128)(2,1)S(1)} %collective-permute-done.39.refs_12_), channel_id=1, source_target_pairs={{0,8},{4,12},{8,16},{12,20},{16,24},{20,28},{24,0},{28,4},{1,9},{5... | collective-permute-start | bytes 786440 | tf_op jit(solution)/shard_map/ppermute | solution.py:62
  242.3 14.9 %collective-permute-start.44 = (bf16[256,1024]{1,0:T(8,128)(2,1)S(1)}, bf16[256,1024]{1,0:T(8,128)(2,1)S(1)}, u32[]{:S(2)}, u32[]{:S(2)}) collective-permute-start(bf16[256,1024]{1,0:T(8,128)(2,1)S(1)} %shard_map.390.refs_1_.refs_5_), channel_id=1, source_target_pairs={{0,8},{4,12},{8,16},{12,20},{16,24},{20,28},{24,0},{28,4},{1,9},{5... | collective-permute-start | bytes 1572872 | tf_op jit(solution)/shard_map/ppermute | solution.py:62
  259.7 24.6 %collective-permute-start.48 = (bf16[256,1024]{1,0:T(8,128)(2,1)S(1)}, bf16[256,1024]{1,0:T(8,128)(2,1)S(1)}, u32[]{:S(2)}, u32[]{:S(2)}) collective-permute-start(bf16[256,1024]{1,0:T(8,128)(2,1)S(1)} %collective-permute-done.44.refs_6_), channel_id=1, source_target_pairs={{0,8},{4,12},{8,16},{12,20},{16,24},{20,28},{24,0},{28,4},{1,9},{5... | collective-permute-start | bytes 1572872 | tf_op jit(solution)/shard_map/ppermute | solution.py:62
  259.7 20.1 %collective-permute-start.52 = (bf16[64,1024]{1,0:T(8,128)(2,1)S(1)}, bf16[64,1024]{1,0:T(8,128)(2,1)S(1)}, u32[]{:S(2)}, u32[]{:S(2)}) collective-permute-start(bf16[64,1024]{1,0:T(8,128)(2,1)S(1)} %get-tuple-element.422), channel_id=1, source_target_pairs={{0,24},{4,28},{8,0},{12,4},{16,8},{20,12},{24,16},{28,20},{1,25},{... | collective-permute-start | bytes 393224 | tf_op jit(solution)/shard_map/ppermute | solution.py:62
  263.8 16.1 %collective-permute-start.51 = (bf16[64,1024]{1,0:T(8,128)(2,1)S(1)}, bf16[64,1024]{1,0:T(8,128)(2,1)S(1)}, u32[]{:S(2)}, u32[]{:S(2)}) collective-permute-start(bf16[64,1024]{1,0:T(8,128)(2,1)S(1)} %get-tuple-element.421), channel_id=1, source_target_pairs={{0,16},{4,20},{8,24},{12,28},{16,0},{20,4},{24,8},{28,12},{1,17},{... | collective-permute-start | bytes 393224 | tf_op jit(solution)/shard_map/ppermute | solution.py:62
  263.8 20.5 %collective-permute-start.49 = (bf16[256,1408]{1,0:T(8,128)(2,1)S(1)}, bf16[256,1408]{1,0:T(8,128)(2,1)S(1)}, u32[]{:S(2)}, u32[]{:S(2)}) collective-permute-start(bf16[256,1408]{1,0:T(8,128)(2,1)S(1)} %get-tuple-element.415), channel_id=1, source_target_pairs={{0,4},{4,0},{8,12},{12,8},{16,20},{20,16},{24,28},{28,24},{1,5},{5... | collective-permute-start | bytes 2162696 | tf_op jit(solution)/shard_map/ppermute | solution.py:52
  284.9 12.1 %collective-permute-start.55 = (bf16[192,1024]{1,0:T(8,128)(2,1)S(1)}, bf16[192,1024]{1,0:T(8,128)(2,1)S(1)}, u32[]{:S(2)}, u32[]{:S(2)}) collective-permute-start(bf16[192,1024]{1,0:T(8,128)(2,1)S(1)} %shard_map.400.refs_1_.refs_5_), channel_id=1, source_target_pairs={{0,2},{1,3},{2,0},{3,1},{4,6},{5,7},{6,4},{7,5},{8,10},{9,11},{10,... | collective-permute-start | bytes 1179656 | tf_op jit(solution)/shard_map/ppermute | solution.py:52
  286.5 20.4 %collective-permute-start.54 = (bf16[256,1408]{1,0:T(8,128)(2,1)S(1)}, bf16[256,1408]{1,0:T(8,128)(2,1)S(1)}, u32[]{:S(2)}, u32[]{:S(2)}) collective-permute-start(bf16[256,1408]{1,0:T(8,128)(2,1)S(1)} %get-tuple-element.428), channel_id=1, source_target_pairs={{0,4},{4,0},{8,12},{12,8},{16,20},{20,16},{24,28},{28,24},{1,5},{5... | collective-permute-start | bytes 2162696 | tf_op jit(solution)/shard_map/ppermute | solution.py:52
  289.1 17.8 %collective-permute-start.59 = (bf16[128,2048]{1,0:T(8,128)(2,1)S(1)}, bf16[128,2048]{1,0:T(8,128)(2,1)S(1)}, u32[]{:S(2)}, u32[]{:S(2)}) collective-permute-start(bf16[128,2048]{1,0:T(8,128)(2,1)S(1)} %shard_map.399.own), channel_id=1, source_target_pairs={{0,2},{1,3},{2,0},{3,1},{4,6},{5,7},{6,4},{7,5},{8,10},{9,11},{10,... | collective-permute-start | bytes 1572872 | tf_op jit(solution)/shard_map/ppermute | solution.py:52
  289.5 17.3 %collective-permute-start.53 = (bf16[256,1024]{1,0:T(8,128)(2,1)S(1)}, bf16[256,1024]{1,0:T(8,128)(2,1)S(1)}, u32[]{:S(2)}, u32[]{:S(2)}) collective-permute-start(bf16[256,1024]{1,0:T(8,128)(2,1)S(1)} %collective-permute-done.48.refs_7_), channel_id=1, source_target_pairs={{0,8},{4,12},{8,16},{12,20},{16,24},{20,28},{24,0},{28,4},{1,9},{5... | collective-permute-start | bytes 1572872 | tf_op jit(solution)/shard_map/ppermute | solution.py:62
  298.1 40.3 %collective-permute-start.60 = (bf16[128,2048]{1,0:T(8,128)(2,1)S(1)}, bf16[128,2048]{1,0:T(8,128)(2,1)S(1)}, u32[]{:S(2)}, u32[]{:S(2)}) collective-permute-start(bf16[128,2048]{1,0:T(8,128)(2,1)S(1)} %shard_map.399.own), channel_id=1, source_target_pairs={{0,1},{1,0},{2,3},{3,2},{4,5},{5,4},{6,7},{7,6},{8,9},{9,8},{10,11... | collective-permute-start | bytes 1572872 | tf_op jit(solution)/shard_map/ppermute | solution.py:52
  306.9 31.6 %collective-permute-start.61 = (bf16[128,2048]{1,0:T(8,128)(2,1)S(1)}, bf16[128,2048]{1,0:T(8,128)(2,1)S(1)}, u32[]{:S(2)}, u32[]{:S(2)}) collective-permute-start(bf16[128,2048]{1,0:T(8,128)(2,1)S(1)} %collective-permute-done.59.side), channel_id=1, source_target_pairs={{0,1},{1,0},{2,3},{3,2},{4,5},{5,4},{6,7},{7,6},{8,9},{9,8},{10,11... | collective-permute-start | bytes 1572872 | tf_op jit(solution)/shard_map/ppermute | solution.py:52
  308.9 27.8 %collective-permute-start.58 = (bf16[256,1024]{1,0:T(8,128)(2,1)S(1)}, bf16[256,1024]{1,0:T(8,128)(2,1)S(1)}, u32[]{:S(2)}, u32[]{:S(2)}) collective-permute-start(bf16[256,1024]{1,0:T(8,128)(2,1)S(1)} %get-tuple-element.441), channel_id=1, source_target_pairs={{0,4},{4,0},{8,12},{12,8},{16,20},{20,16},{24,28},{28,24},{1,5},{5... | collective-permute-start | bytes 1572872 | tf_op jit(solution)/shard_map/ppermute | solution.py:52
  311.6 17.0 %collective-permute-start.62 = (f32[24,2048]{1,0:T(8,128)S(1)}, f32[24,2048]{1,0:T(8,128)S(1)}, u32[]{:S(2)}, u32[]{:S(2)}) collective-permute-start(f32[24,2048]{1,0:T(8,128)S(1)} %shard_map.398), channel_id=1, source_target_pairs={{0,4},{4,0},{8,12},{12,8},{16,20},{20,16},{24,28},{28,24},{1,5},{5... | collective-permute-start | bytes 589832 | tf_op jit(solution)/shard_map/ppermute | solution.py:52
  313.7 26.8 %collective-permute-start.67 = (bf16[256,1024]{1,0:T(8,128)(2,1)S(1)}, bf16[256,1024]{1,0:T(8,128)(2,1)S(1)}, u32[]{:S(2)}, u32[]{:S(2)}) collective-permute-start(bf16[256,1024]{1,0:T(8,128)(2,1)S(1)} %get-tuple-element.459), channel_id=1, source_target_pairs={{0,4},{4,0},{8,12},{12,8},{16,20},{20,16},{24,28},{28,24},{1,5},{5... | collective-permute-start | bytes 1572872 | tf_op jit(solution)/shard_map/ppermute | solution.py:52
  335.2 20.2 %collective-permute-start.68 = (bf16[256,1408]{1,0:T(8,128)(2,1)S(1)}, bf16[256,1408]{1,0:T(8,128)(2,1)S(1)}, u32[]{:S(2)}, u32[]{:S(2)}) collective-permute-start(bf16[256,1408]{1,0:T(8,128)(2,1)S(1)} %get-tuple-element.465), channel_id=1, source_target_pairs={{0,4},{4,0},{8,12},{12,8},{16,20},{20,16},{24,28},{28,24},{1,5},{5... | collective-permute-start | bytes 2162696 | tf_op jit(solution)/shard_map/ppermute | solution.py:52
  (67 other events, 598.0 us)
